TPU v7x, 512 devices: a whole 4x8x8 slice. The times are simulated.
512 devices in a mesh: pipe: 32 (over z_lo, y, core), tensor: 16 (over z_hi, x).
Axes of the slice: x: 4, y: 8, z: 8 (z_hi: 4, z_lo: 2; z = z_hi * 2 + z_lo), core: 2. Of those that a mesh axis runs over, the one named last changes fastest.
Arguments:
- tokens: bfloat16 [256, 8192], P('pipe', 'tensor'), may hold values from -6 to 6
- gate_weight: bfloat16 [8192, 28672], P('tensor', 'pipe'), may hold values from -0.0625 to 0.0625
- upward_weight: bfloat16 [8192, 28672], P('tensor', 'pipe'), may hold values from -0.0625 to 0.0625
- down_weight: bfloat16 [28672, 8192], P('pipe', 'tensor'), may hold values from -0.03125 to 0.03125
- adapter_first_factors: bfloat16 [2, 8192, 64], P(None, 'tensor'), may hold values from -0.0625 to 0.0625
- adapter_second_factors: bfloat16 [2, 64, 28672], P(None, None, 'pipe'), may hold values from -0.75 to 0.75
- adapter_of_block: int32 [2], replicated, may hold values from 0 to 1, each once
- cotangent: bfloat16 [256, 8192], P('pipe', 'tensor'), may hold values from -6 to 6
Outputs:
- mixed: bfloat16 [256, 8192], P('pipe', 'tensor')
- grad_tokens: bfloat16 [256, 8192], P('pipe', 'tensor')
- grad_a: float32 [2, 8192, 64], P(None, 'tensor')
- grad_b: float32 [2, 64, 28672], P(None, None, 'pipe')
Inputs may be any that keep to these rules, and one draw needn't show every extreme that they name: `adapter_of_block`: each of the 2 adapters is named by exactly one block.
All inputs are finite; a program needn't handle non-finite values.
Results may differ from a plain program's by a relative error of at most 0.0052.
Values may be sent and summed in bfloat16 or wider, within the bound.
No kernel may reach another device: no remote copies, remote signals or barrier semaphores. Data moves between devices by JAX's collectives and lax.ppermute only.
A program may use at most 64 MiB of HBM per device.

v0:
```python
import jax
import jax.numpy as jnp
from jax import lax
from jax.sharding import PartitionSpec as P

BLOCK = 128


adapter_scale = 0.5


def adapter_mask(first_row, row_count, adapter_of_block, rank_columns):
    row_index = first_row + jnp.arange(row_count, dtype=jnp.int32)
    owner = row_index // BLOCK
    block_index = jnp.arange(adapter_of_block.shape[0], dtype=jnp.int32)
    chosen = jnp.sum(
        jnp.where(owner[:, None] == block_index[None, :], adapter_of_block[None, :], 0), axis=1
    )
    columns = jnp.arange(adapter_of_block.shape[0] * rank_columns, dtype=jnp.int32) // rank_columns
    return (columns[None, :] == chosen[:, None]).astype(jnp.float32)


def trailing_product(left, right):
    return lax.dot_general(
        left, right, (((1,), (1,)), ((), ())), preferred_element_type=jnp.float32
    )


def leading_product(left, right):
    return lax.dot_general(
        left, right, (((0,), (0,)), ((), ())), preferred_element_type=jnp.float32
    )


def on_device(
    tokens,
    gate_weight,
    upward_weight,
    down_weight,
    adapter_first_factors,
    adapter_second_factors,
    adapter_of_block,
    cotangent,
):
    adapter_total, width_shard, rank_columns = adapter_first_factors.shape
    hidden_shard = gate_weight.shape[1]
    first_factor_rows = jnp.transpose(adapter_first_factors, (1, 0, 2)).reshape(
        width_shard, adapter_total * rank_columns
    )
    second_factor_rows = adapter_second_factors.reshape(adapter_total * rank_columns, hidden_shard)
    pipe_rows = tokens.shape[0]
    all_rows = pipe_rows * lax.axis_size("pipe")
    tensor_rows = all_rows // lax.axis_size("tensor")
    token_rows = lax.all_gather(tokens, "pipe", axis=0, tiled=True)
    piece = token_rows
    parts = lax.psum_scatter(
        jnp.concatenate(
            [
                jnp.dot(piece, gate_weight, preferred_element_type=jnp.float32),
                jnp.dot(piece, upward_weight, preferred_element_type=jnp.float32),
                jnp.dot(piece, first_factor_rows, preferred_element_type=jnp.float32),
            ],
            axis=1,
        ),
        "tensor",
        scatter_dimension=0,
        tiled=True,
    )
    first_row = lax.axis_index("tensor") * tensor_rows
    adapter_select_mask = adapter_mask(first_row, parts.shape[0], adapter_of_block, rank_columns)
    gate = parts[:, :hidden_shard]
    upward_frozen_output = parts[:, hidden_shard : 2 * hidden_shard]
    reduced_activation = (parts[:, 2 * hidden_shard :] * adapter_select_mask).astype(jnp.bfloat16)
    upward_output = upward_frozen_output + adapter_scale * jnp.dot(
        reduced_activation, second_factor_rows, preferred_element_type=jnp.float32
    )
    sig = jax.nn.sigmoid(gate)
    act = gate * sig
    hidden = (act * upward_output).astype(jnp.bfloat16)
    hidden_all = lax.all_gather(hidden, "tensor", axis=0, tiled=True)
    piece = hidden_all
    mixed = lax.psum_scatter(
        jnp.dot(piece, down_weight, preferred_element_type=jnp.float32),
        "pipe",
        scatter_dimension=0,
        tiled=True,
    ).astype(jnp.bfloat16)
    adjoint_rows = lax.all_gather(cotangent, "pipe", axis=0, tiled=True)
    piece = adjoint_rows
    grad_hidden = lax.psum_scatter(
        trailing_product(piece, down_weight), "tensor", scatter_dimension=0, tiled=True
    )
    upward_gradient = (grad_hidden * act).astype(jnp.bfloat16)
    grad_gate = (grad_hidden * upward_output * sig * (1.0 + gate * (1.0 - sig))).astype(
        jnp.bfloat16
    )
    second_factor_term = adapter_scale * leading_product(reduced_activation, upward_gradient)
    second_factor_gradient = lax.psum(second_factor_term, "tensor")
    reduced_gradient = (
        adapter_scale * trailing_product(upward_gradient, second_factor_rows) * adapter_select_mask
    )
    low_summed = lax.psum(reduced_gradient, "pipe")
    low_all = lax.all_gather(low_summed, "tensor", axis=0, tiled=True)
    low_back = low_all.astype(jnp.bfloat16)
    stacked = jnp.concatenate([grad_gate, upward_gradient], axis=1)
    stacked_all = lax.all_gather(stacked, "tensor", axis=0, tiled=True)
    piece = stacked_all
    back_sum = lax.psum_scatter(
        trailing_product(piece[:, :hidden_shard], gate_weight)
        + trailing_product(piece[:, hidden_shard:], upward_weight),
        "pipe",
        scatter_dimension=0,
        tiled=True,
    )
    own_low = lax.dynamic_slice_in_dim(low_back, lax.axis_index("pipe") * pipe_rows, pipe_rows, 0)
    grad_tokens = (back_sum + trailing_product(own_low, first_factor_rows)).astype(jnp.bfloat16)
    grad_a_flat = leading_product(token_rows, low_back)
    grad_a = jnp.transpose(grad_a_flat.reshape(width_shard, adapter_total, rank_columns), (1, 0, 2))
    grad_b = second_factor_gradient.reshape(adapter_total, rank_columns, hidden_shard)
    return (mixed, grad_tokens, grad_a, grad_b)


def solution(mesh):
    in_specs = (
        P("pipe", "tensor"),
        P("tensor", "pipe"),
        P("tensor", "pipe"),
        P("pipe", "tensor"),
        P(None, "tensor", None),
        P(None, None, "pipe"),
        P(),
        P("pipe", "tensor"),
    )
    out_specs = (
        P("pipe", "tensor"),
        P("pipe", "tensor"),
        P(None, "tensor", None),
        P(None, None, "pipe"),
    )
    return jax.shard_map(
        on_device, mesh=mesh, in_specs=in_specs, out_specs=out_specs, check_vma=False
    )
```

profile of v0, /device:TPU:1, one launch (start us, length us, event | category | flops | bytes accessed | tf_op | source)
XLA Modules:
  0.0 677.9 jit_solution(7951810947184697650)
XLA Ops:
  7.2 0.0 copy-start
  7.2 0.0 copy-start.4
  7.2 0.0 copy-start.3
  7.2 0.0 reduce-scatter.9.cloned.1.call-start
  7.2 38.2 %all_gather.17 = bf16[256,512]{1,0:T(8,128)(2,1)S(1)} all-gather(bf16[8,512]{1,0:T(8,128)(2,1)} %param.15), channel_id=1, replica_groups=mesh['pipe'=32,'tensor'=16] {'pipe'}, dimensions={0}, use_global_device_ids=true | all-gather | bytes 270336 | tf_op jit(solution)/shard_map/all_gather | solution.py:88
  45.5 0.0 copy-done
  45.5 0.0 copy-start.1
  45.5 1.4 fusion.17
  46.9 0.0 copy-start.2
  46.9 0.0 reduce-scatter.9.cloned.1.call-update
  46.9 0.0 reduce-scatter.5.cloned.1.call-start
  47.0 0.0 copy-done.4
  47.0 33.1 %all_gather.15 = bf16[256,512]{1,0:T(8,128)(2,1)S(1)} all-gather(bf16[8,512]{1,0:T(8,128)(2,1)S(1)} %copy-done.4), channel_id=1, replica_groups=mesh['pipe'=32,'tensor'=16] {'pipe'}, dimensions={0}, use_global_device_ids=true | all-gather | bytes 270336 | tf_op jit(solution)/shard_map/all_gather | solution.py:54
  80.1 0.0 copy-done.3
  80.1 0.2 fusion.15
  80.4 0.0 copy-done.1
  80.4 0.4 fusion.13
  80.8 0.0 copy-done.2
  80.8 0.4 fusion.14
  81.3 1.4 pad_maximum_fusion
  82.7 0.0 copy-start.6
  82.7 0.0 copy-start.5
  82.7 0.0 reduce-scatter.5.cloned.1.call-update
  82.7 0.0 reduce-scatter.7.cloned.1.call-start
  82.8 0.5 copy-done.6
  83.4 0.1 fusion.9
  83.4 51.8 %reduce-scatter.9.cloned.1.call-done = f32[16,896]{1,0:T(8,128)} async-done(((f32[256,896]{1,0:T(8,128)}), f32[16,896]{1,0:T(8,128)}) %reduce-scatter.9.cloned.1.call-update) | async-done | bytes 57360 | tf_op jit(solution)/shard_map/reduce_scatter | solution.py:90
  135.3 97.4 %reduce-scatter.5.cloned.1.call-done = f32[16,1920]{1,0:T(8,128)} async-done(((f32[256,1920]{1,0:T(8,128)}), f32[16,1920]{1,0:T(8,128)}) %reduce-scatter.5.cloned.1.call-update) | async-done | bytes 122896 | tf_op jit(solution)/shard_map/reduce_scatter | solution.py:56
  232.7 0.0 copy-done.5
  232.7 1.1 multiply_convert_fusion.1
  233.8 37.6 %all_gather.16 = bf16[256,896]{1,0:T(8,128)(2,1)S(1)} all-gather(bf16[16,896]{1,0:T(8,128)(2,1)S(1)} %get-tuple-element.5), channel_id=1, replica_groups=mesh['pipe'=32,'tensor'=16] {'tensor'}, dimensions={0}, use_global_device_ids=true | all-gather | bytes 487424 | tf_op jit(solution)/shard_map/all_gather | solution.py:80
  271.4 1.2 fusion.16
  272.6 0.0 reduce-scatter.7.cloned.1.call-update
  272.7 0.0 reduce-scatter.11.cloned.1.call-start
  272.7 41.4 %all_gather.18 = bf16[256,1792]{1,0:T(8,128)(2,1)S(1)} all-gather(bf16[16,1792]{1,0:T(8,128)(2,1)S(1)} %pad_maximum_fusion.1), channel_id=1, replica_groups=mesh['pipe'=32,'tensor'=16] {'tensor'}, dimensions={0}, use_global_device_ids=true | all-gather | bytes 974848 | tf_op jit(solution)/shard_map/all_gather | solution.py:106
  314.2 0.5 fusion.4
  314.6 1.3 convolution_add_fusion
  315.9 0.0 reduce-scatter.11.cloned.1.call-update
  315.9 0.0 all-reduce.2.cloned.1.call-start
  316.0 0.2 fusion.2
  316.1 66.3 %psum.14 = bf16[16,128]{1,0:T(8,128)(2,1)S(1)} all-reduce(f32[16,128]{1,0:T(8,128)S(1)} %fusion.2), channel_id=1, replica_groups=mesh['pipe'=32,'tensor'=16] {'pipe'}, use_global_device_ids=true, to_apply=%region_5.6 | all-reduce | flops 2048 | bytes 12288 | tf_op jit(solution)/shard_map/psum | solution.py:102
  382.5 31.4 %all_gather.19 = bf16[256,128]{1,0:T(8,128)(2,1)S(1)} all-gather(bf16[16,128]{1,0:T(8,128)(2,1)S(1)} %psum.14), channel_id=1, replica_groups=mesh['pipe'=32,'tensor'=16] {'tensor'}, dimensions={0}, use_global_device_ids=true | all-gather | bytes 69632 | tf_op jit(solution)/shard_map/all_gather | solution.py:103
  413.8 1.8 convolution_multiply_fusion
  415.6 0.0 all-reduce.2.cloned.1.call-update
  415.6 0.9 fusion.18
  416.5 0.0 reduce-scatter.7.cloned.1.call-done
  416.5 1.3 convert_element_type.24
  417.9 92.9 %reduce-scatter.11.cloned.1.call-done = f32[8,512]{1,0:T(8,128)} async-done(((f32[256,512]{1,0:T(8,128)}), f32[8,512]{1,0:T(8,128)}) %reduce-scatter.11.cloned.1.call-update) | async-done | bytes 16400 | tf_op jit(solution)/shard_map/reduce_scatter | solution.py:108
  510.7 1.4 fusion.1
  512.2 157.3 %all-reduce.2.cloned.1.call-done = f32[2,64,896]{2,1,0:T(8,128)} async-done(((f32[2,64,896]{2,1,0:T(8,128)}), f32[2,64,896]{2,1,0:T(8,128)}) %all-reduce.2.cloned.1.call-update) | async-done | bytes 458768 | tf_op jit(solution)/shard_map/psum | solution.py:98
  669.5 1.8 copy.16
  (3 shorter events, 0.0 us)
Async XLA Ops:
  7.2 38.3 %copy-start = (bf16[896,512]{1,0:T(8,128)(2,1)S(1)}, bf16[896,512]{1,0:T(8,128)(2,1)}, u32[]{:S(2)}) copy-start(bf16[896,512]{1,0:T(8,128)(2,1)} %param.11) | copy-start | bytes 2752516
  7.2 39.8 %copy-start.4 = (bf16[8,512]{1,0:T(8,128)(2,1)S(1)}, bf16[8,512]{1,0:T(8,128)(2,1)}, u32[]{:S(2)}) copy-start(bf16[8,512]{1,0:T(8,128)(2,1)} %param.8) | copy-start | bytes 24580
  7.2 72.9 %copy-start.3 = (bf16[2,512,64]{1,2,0:T(8,128)(2,1)S(1)}, bf16[2,512,64]{1,2,0:T(8,128)(2,1)}, u32[]{:S(2)}) copy-start(bf16[2,512,64]{1,2,0:T(8,128)(2,1)} %param.12) | copy-start | bytes 393220
  7.2 128.1 %reduce-scatter.9.cloned.1.call-start = ((), (), s32[]{:S(2)}) async-start(), calls=%async_computation.6 | async-start | bytes 974848 | tf_op jit(solution)/shard_map/reduce_scatter | solution.py:90
  45.5 34.9 %copy-start.1 = (bf16[512,896]{1,0:T(8,128)(2,1)S(1)}, bf16[512,896]{1,0:T(8,128)(2,1)}, u32[]{:S(2)}) copy-start(bf16[512,896]{1,0:T(8,128)(2,1)} %param.9) | copy-start | bytes 2752516
  46.9 33.9 %copy-start.2 = (bf16[512,896]{1,0:T(8,128)(2,1)S(1)}, bf16[512,896]{1,0:T(8,128)(2,1)}, u32[]{:S(2)}) copy-start(bf16[512,896]{1,0:T(8,128)(2,1)} %param.10) | copy-start | bytes 2752516
  46.9 185.7 %reduce-scatter.5.cloned.1.call-start = ((), (), s32[]{:S(2)}) async-start(), calls=%async_computation.4 | async-start | bytes 2088960 | tf_op jit(solution)/shard_map/reduce_scatter | solution.py:56
  82.7 0.7 copy-start.6
  82.7 150.0 %copy-start.5 = (bf16[2,64,896]{2,1,0:T(8,128)(2,1)S(1)}, bf16[2,64,896]{2,1,0:T(8,128)(2,1)}, u32[]{:S(2)}) copy-start(bf16[2,64,896]{2,1,0:T(8,128)(2,1)} %param.13) | copy-start | bytes 688132
  82.7 333.8 %reduce-scatter.7.cloned.1.call-start = ((), (), s32[]{:S(2)}) async-start(), calls=%async_computation.5 | async-start | bytes 540672 | tf_op jit(solution)/shard_map/reduce_scatter | solution.py:82
  272.7 238.1 %reduce-scatter.11.cloned.1.call-start = ((), (), s32[]{:S(2)}) async-start(), calls=%async_computation.7 | async-start | bytes 540672 | tf_op jit(solution)/shard_map/reduce_scatter | solution.py:108
  315.9 353.6 %all-reduce.2.cloned.1.call-start = ((), (), s32[]{:S(2)}) async-start(), calls=%async_computation.8 | async-start | bytes 917504 | tf_op jit(solution)/shard_map/psum | solution.py:98
Sparse Core Ops, SparseCore 0:
  47.1 88.1 reduce-scatter.8
  140.0 92.6 reduce-scatter.4
  272.8 121.3 reduce-scatter.6
  397.0 113.6 reduce-scatter.10
  514.1 155.3 all-reduce.1
where the time goes:
time: 688 us; the launch traced here: 678 us
  waiting for transfers between devices  400 us (58%)
  blocking collectives  248 us (36%)
  between operations  13.9 us (2%)
  matrix products  10.9 us (2%)
    psum x1, waiting for transfers between devices, on_device(): second_factor_gradient = lax.psum(second_factor_term, 'tensor')  157 us
    reduce_scatter x1, waiting for transfers between devices, on_device(): lax.psum_scatter(jnp.concatenate([jnp.dot(piece, gate_weight, preferred_e...  97.4 us
    reduce_scatter x1, waiting for transfers between devices, on_device(): lax.psum_scatter(trailing_product(piece[:, :hidden_shard], gate_weight) +...  92.9 us
    psum x1, blocking collectives, on_device(): low_summed = lax.psum(reduced_gradient, 'pipe')  66.3 us
    reduce_scatter x1, waiting for transfers between devices, on_device(): lax.psum_scatter(trailing_product(piece, down_weight), 'tensor', scatter_...  51.8 us
    all_gather x1, blocking collectives, on_device(): stacked_all = lax.all_gather(stacked, 'tensor', axis=0, tiled=True)  41.4 us
    all_gather x1, blocking collectives, on_device(): adjoint_rows = lax.all_gather(cotangent, 'pipe', axis=0, tiled=True)  38.2 us
    all_gather x1, blocking collectives, on_device(): hidden_all = lax.all_gather(hidden, 'tensor', axis=0, tiled=True)  37.6 us
  transfers between devices with their start and end apart: 5, of which 4 were waited for; matrix products, arithmetic and copies ran while one was open for 1% of the time, Pallas kernels for 0%

commit v1 on v0

v1 whole, which is shorter than its diff:
```python
import jax
import jax.numpy as jnp
from jax import lax
from jax.sharding import Mesh, PartitionSpec as P

PIPE = ("zlo", "y", "core")
TENSOR = ("zhi", "x")
PIPE_LINKS = ("zlo", "y")
adapter_scale = 0.5
bf16 = jnp.bfloat16
f32 = jnp.float32


def product(left, right):
    return jnp.dot(left, right, preferred_element_type=f32)


def trailing_product(left, right):
    return lax.dot_general(left, right, (((1,), (1,)), ((), ())), preferred_element_type=f32)


def leading_product(left, right):
    return lax.dot_general(left, right, (((0,), (0,)), ((), ())), preferred_element_type=f32)


def gather_rows(value, axis):
    count = lax.axis_size(axis)
    blocks = jnp.broadcast_to(value[None], (count,) + value.shape)
    return lax.all_to_all(blocks, axis, 0, 0).reshape((count * value.shape[0],) + value.shape[1:])


def scatter_sum(value, axis, sent):
    count = lax.axis_size(axis)
    blocks = value.astype(sent).reshape(count, value.shape[0] // count, value.shape[1])
    return jnp.sum(lax.all_to_all(blocks, axis, 0, 0).astype(f32), axis=0)


def on_device(
    tokens,
    gate_weight,
    upward_weight,
    down_weight,
    adapter_first_factors,
    adapter_second_factors,
    adapter_of_block,
    cotangent,
):
    adapters, width, rank = adapter_first_factors.shape
    hidden_units = gate_weight.shape[1]
    columns = adapters * rank
    first = jnp.transpose(adapter_first_factors, (1, 0, 2)).reshape(width, columns)
    second = adapter_second_factors.reshape(columns, hidden_units)

    both = jnp.concatenate([tokens, cotangent], axis=1)
    both = lax.all_gather(gather_rows(both, PIPE_LINKS), "core", axis=0, tiled=True)
    token_rows, adjoint_rows = both[:, :width], both[:, width:]

    parts = jnp.concatenate(
        [
            product(token_rows, gate_weight).astype(bf16),
            product(token_rows, upward_weight).astype(bf16),
            trailing_product(adjoint_rows, down_weight).astype(bf16),
            product(token_rows, first).astype(bf16),
        ],
        axis=1,
    )
    parts = scatter_sum(scatter_sum(parts, "x", bf16), "zhi", f32)

    def mask_of(block):
        own = jnp.arange(columns, dtype=jnp.int32) // rank
        chosen = jnp.sum(
            jnp.where(
                block[:, None] == jnp.arange(adapter_of_block.shape[0], dtype=jnp.int32)[None, :],
                adapter_of_block[None, :],
                0,
            ),
            axis=1,
        )
        return (own[None, :] == chosen[:, None]).astype(f32)

    x_index = lax.axis_index("x")
    own_mask = mask_of(jnp.full((1,), x_index % 2, jnp.int32))
    gate = parts[:, :hidden_units]
    up_base = parts[:, hidden_units : 2 * hidden_units]
    grad_hidden = parts[:, 2 * hidden_units : 3 * hidden_units]
    low = (parts[:, 3 * hidden_units :] * own_mask).astype(bf16)
    up = up_base + adapter_scale * product(low, second)
    sig = jax.nn.sigmoid(gate)
    act = gate * sig
    hidden = (act * up).astype(bf16)
    grad_up = (grad_hidden * act).astype(bf16)
    grad_gate = (grad_hidden * up * sig * (1.0 + gate * (1.0 - sig))).astype(bf16)

    rows = jnp.concatenate([hidden, grad_gate, grad_up, low], axis=1)
    rows = gather_rows(gather_rows(rows, "zhi"), "x")
    hidden_all = rows[:, :hidden_units]
    grad_gate_all = rows[:, hidden_units : 2 * hidden_units]
    grad_up_all = rows[:, 2 * hidden_units : 3 * hidden_units]
    low_all = rows[:, 3 * hidden_units :]

    row_total = rows.shape[0]
    row_block = (jnp.arange(row_total, dtype=jnp.int32) // (row_total // 4)) % 2
    all_mask = mask_of(row_block)
    partial = jnp.concatenate(
        [
            product(hidden_all, down_weight),
            trailing_product(grad_gate_all, gate_weight)
            + trailing_product(grad_up_all, upward_weight),
            adapter_scale * trailing_product(grad_up_all, second) * all_mask,
        ],
        axis=1,
    )
    summed = scatter_sum(scatter_sum(partial, "core", f32), PIPE_LINKS, bf16)
    mixed = summed[:, :width].astype(bf16)
    low_own = summed[:, 2 * width :].astype(bf16)
    grad_tokens = (summed[:, width : 2 * width] + trailing_product(low_own, first)).astype(bf16)

    grad_b = (adapter_scale * leading_product(low_all, grad_up_all)).reshape(
        adapters, rank, hidden_units
    )
    low_back = lax.all_gather(gather_rows(low_own, PIPE_LINKS), "core", axis=0, tiled=True)
    grad_a = leading_product(token_rows, low_back).reshape(width, adapters, rank)
    return mixed, grad_tokens, jnp.transpose(grad_a, (1, 0, 2)), grad_b


def solution(mesh):
    parts = Mesh(mesh.devices.reshape(2, 8, 2, 4, 4), PIPE + TENSOR)
    in_specs = (
        P(PIPE, TENSOR),
        P(TENSOR, PIPE),
        P(TENSOR, PIPE),
        P(PIPE, TENSOR),
        P(None, TENSOR, None),
        P(None, None, PIPE),
        P(),
        P(PIPE, TENSOR),
    )
    out_specs = (
        P(PIPE, TENSOR),
        P(PIPE, TENSOR),
        P(None, TENSOR, None),
        P(None, None, PIPE),
    )
    return jax.shard_map(
        on_device, mesh=parts, in_specs=in_specs, out_specs=out_specs, check_vma=False
    )
```

time: 688 us -> 159 us (0.23); the launches traced: 678 us -> 158 us
  waiting for transfers between devices: 400 us -> 39.3 us
  blocking collectives: 248 us -> 76.4 us
  starting transfers between devices: 0.21 us -> 26.6 us
  between operations: 13.9 us -> 0.88 us
    reduce_scatter x4 -> x0, waiting for transfers between devices: 242 us -> none  [the longest x1 97.4 us: on_device(): lax.psum_scatter(jnp.concatenate([jnp.dot(piece, gate_weight, preferred_e...]
    all_gather x5 -> x2, blocking collectives: 182 us -> 8.07 us  [the longest x1 4.27 us: on_device(): lax.all_gather(gather_rows(both, PIPE_LINKS), 'core', axis=0, tiled=True)]
    psum x1 -> x0, waiting for transfers between devices: 157 us -> none  [on_device(): second_factor_gradient = lax.psum(second_factor_term, 'tensor')]
    all_to_all x0 -> x4, blocking collectives: none -> 68.3 us  [the longest x2 35.2 us: scatter_sum(): return jnp.sum(lax.all_to_all(blocks, axis, 0, 0).astype(f32), axis=0)]
    psum x1 -> x0, blocking collectives: 66.3 us -> none  [on_device(): low_summed = lax.psum(reduced_gradient, 'pipe')]
    all_to_all x0 -> x4, waiting for transfers between devices: none -> 39.3 us  [the longest x2 20.9 us: scatter_sum(): return jnp.sum(lax.all_to_all(blocks, axis, 0, 0).astype(f32), axis=0)]
    all_to_all x0 -> x4, starting transfers between devices: none -> 26.6 us  [the longest x2 17.6 us: scatter_sum(): return jnp.sum(lax.all_to_all(blocks, axis, 0, 0).astype(f32), axis=0)]
  transfers between devices with their start and end apart: 5 -> 4, of which waited for: 4 -> 4; matrix products, arithmetic and copies ran while one was open for 1% -> 2% of each run, Pallas kernels for 0% -> 0%
where the time goes in v1:
time: 159 us; the launch traced here: 158 us
  blocking collectives  76.4 us (48%)
  waiting for transfers between devices  39.3 us (25%)
  starting transfers between devices  26.6 us (17%)
  matrix products  6.08 us (4%)
  other arithmetic  5.72 us (4%)
  local copies, waits for them, and re-layouts  3.22 us (2%)
    all_to_all x2, blocking collectives, scatter_sum(): return jnp.sum(lax.all_to_all(blocks, axis, 0, 0).astype(f32), axis=0)  35.2 us
    all_to_all x2, blocking collectives, gather_rows(): lax.all_to_all(blocks, axis, 0, 0)  33.1 us
    all_to_all x2, waiting for transfers between devices, scatter_sum(): return jnp.sum(lax.all_to_all(blocks, axis, 0, 0).astype(f32), axis=0)  20.9 us
    all_to_all x2, waiting for transfers between devices, gather_rows(): lax.all_to_all(blocks, axis, 0, 0)  18.4 us
    all_to_all x2, starting transfers between devices, scatter_sum(): return jnp.sum(lax.all_to_all(blocks, axis, 0, 0).astype(f32), axis=0)  17.6 us
    all_to_all x2, starting transfers between devices, gather_rows(): lax.all_to_all(blocks, axis, 0, 0)  9.06 us
    all_gather x1, blocking collectives, on_device(): lax.all_gather(gather_rows(both, PIPE_LINKS), 'core', axis=0, tiled=True)  4.27 us
    all_gather x1, blocking collectives, on_device(): lax.all_gather(gather_rows(low_own, PIPE_LINKS), 'core', axis=0, tiled=True)  3.8 us
  transfers between devices with their start and end apart: 4, of which 4 were waited for; matrix products, arithmetic and copies ran while one was open for 2% of the time, Pallas kernels for 0%

profile of v1, /device:TPU:1, one launch (start us, length us, event | category | flops | bytes accessed | tf_op | source)
XLA Modules:
  0.0 158.2 jit_solution(11249426828117497746)
XLA Ops:
  0.6 0.0 copy-start
  0.6 0.0 copy-start.5
  0.7 0.0 copy-start.3
  0.7 0.9 pad_maximum_fusion.3
  1.5 18.1 %all_to_all.40 = bf16[16,8,1024]{2,1,0:T(8,128)(2,1)S(1)} all-to-all(bf16[16,8,1024]{2,1,0:T(8,128)(2,1)S(1)} %broadcast_in_dim.22), channel_id=1, replica_groups=mesh['zlo'=2,'y'=8,'core'=2,'zhi'=4,'x'=4] {'zlo','y'}, dimensions={0} | all-to-all | bytes 524288 | tf_op jit(solution)/shard_map/all_to_all | solution.py:29
  19.6 0.0 copy-start.1
  19.6 4.3 %all_gather.6 = bf16[256,1024]{1,0:T(8,128)(2,1)S(1)} all-gather(bf16[128,1024]{1,0:T(8,128)(2,1)S(1)} %bitcast.38), channel_id=1, replica_groups=mesh['zlo'=2,'y'=8,'core'=2,'zhi'=4,'x'=4] {'core'}, dimensions={0}, use_global_device_ids=true | all-gather | bytes 786432 | tf_op jit(solution)/shard_map/all_gather | solution.py:55
  23.9 0.0 copy-done.5
  23.9 0.2 convolution_convert_fusion.3
  24.1 0.0 copy-done.3
  24.2 0.4 convolution_convert_fusion.1
  24.6 0.0 copy-done.1
  24.6 0.5 convolution_convert_fusion
  25.1 0.0 copy-done
  25.1 0.4 convolution_convert_fusion.2
  25.5 0.1 pad_maximum_fusion
  25.7 22.3 %all_to_all.41 = bf16[4,64,2816]{2,1,0:T(8,128)(2,1)S(1)} all-to-all(bf16[4,64,2816]{2,1,0:T(8,128)(2,1)S(1)} %bitcast.35), channel_id=1, replica_groups=mesh['zlo'=2,'y'=8,'core'=2,'zhi'=4,'x'=4] {'x'}, dimensions={0} | all-to-all | bytes 2883584 | tf_op jit(solution)/shard_map/all_to_all | solution.py:35
  47.9 0.0 copy-start.6
  47.9 1.1 convert_reduce_fusion
  49.0 0.0 copy-start.7
  49.0 9.3 %all-to-all-start.2 = ((f32[4,16,2816]{2,1,0:T(8,128)}), f32[4,16,2816]{2,1,0:T(8,128)S(1)}, u32[]{:S(2)}, u32[]{:S(2)}) async-start(f32[4,16,2816]{2,1,0:T(8,128)} %bitcast.4), calls=%async_computation.2 | async-start | bytes 1441792 | tf_op jit(solution)/shard_map/all_to_all | solution.py:35
  58.2 0.0 copy-done.6
  58.2 0.6 fusion.21
  58.9 0.6 compare_convert_fusion
  59.5 12.4 %all-to-all-done.2 = f32[4,16,2816]{2,1,0:T(8,128)S(1)} async-done(((f32[4,16,2816]{2,1,0:T(8,128)}), f32[4,16,2816]{2,1,0:T(8,128)S(1)}, u32[]{:S(2)}, u32[]{:S(2)}) %all-to-all-start.2) | async-done | bytes 720928 | tf_op jit(solution)/shard_map/all_to_all | solution.py:35
  72.0 0.0 copy-done.7
  72.0 0.2 multiply_convert_fusion.2
  72.2 15.0 %all_to_all.42 = bf16[4,16,2816]{2,1,0:T(8,128)(2,1)S(1)} all-to-all(bf16[4,16,2816]{2,1,0:T(8,128)(2,1)S(1)} %broadcast_in_dim.28), channel_id=1, replica_groups=mesh['zlo'=2,'y'=8,'core'=2,'zhi'=4,'x'=4] {'zhi'}, dimensions={0} | all-to-all | bytes 720896 | tf_op jit(solution)/shard_map/all_to_all | solution.py:29
  87.2 1.2 broadcast_in_dim.30
  88.4 3.5 %all-to-all-start.4 = ((bf16[4,64,2816]{2,1,0:T(8,128)(2,1)}), bf16[4,64,2816]{2,1,0:T(8,128)(2,1)S(1)}, u32[]{:S(2)}, u32[]{:S(2)}) async-start(bf16[4,64,2816]{2,1,0:T(8,128)(2,1)} %broadcast_in_dim.30), calls=%async_computation.4 | async-start | bytes 2883584 | tf_op jit(solution)/shard_map/all_to_all | solution.py:29
  92.0 0.1 fusion.19
  92.1 12.3 %all-to-all-done.4 = bf16[4,64,2816]{2,1,0:T(8,128)(2,1)S(1)} async-done(((bf16[4,64,2816]{2,1,0:T(8,128)(2,1)}), bf16[4,64,2816]{2,1,0:T(8,128)(2,1)S(1)}, u32[]{:S(2)}, u32[]{:S(2)}) %all-to-all-start.4) | async-done | bytes 1441824 | tf_op jit(solution)/shard_map/all_to_all | solution.py:29
  104.4 0.0 copy-start.2
  104.4 0.0 copy-start.4
  104.4 0.5 fusion.3
  104.8 0.7 copy-done.2
  105.6 0.4 fusion.5
  106.0 0.0 copy-done.4
  106.0 0.5 convolution_add_fusion
  106.5 0.3 fusion
  106.8 0.1 pad_maximum_fusion.1
  106.9 12.9 %all_to_all.43 = f32[2,128,1152]{2,1,0:T(8,128)} all-to-all(f32[2,128,1152]{2,1,0:T(8,128)S(1)} %bitcast.36), channel_id=1, replica_groups=mesh['zlo'=2,'y'=8,'core'=2,'zhi'=4,'x'=4] {'core'}, dimensions={0} | all-to-all | bytes 2359296 | tf_op jit(solution)/shard_map/all_to_all | solution.py:35
  119.8 2.1 %reduce_sum.58 = bf16[128,1152]{1,0:T(8,128)(2,1)} reduce(f32[2,128,1152]{2,1,0:T(8,128)} %all_to_all.43, f32[]{:T(128)} %constant.56.clone.1), dimensions={0}, to_apply=%region_4.5 | reduce | flops 147456 | bytes 1474564 | tf_op jit(solution)/shard_map/reduce_sum | solution.py:35
  122.0 8.3 %all-to-all-start.6 = ((bf16[16,8,1152]{2,1,0:T(8,128)(2,1)}), bf16[16,8,1152]{2,1,0:T(8,128)(2,1)S(1)}, u32[]{:S(2)}, u32[]{:S(2)}) async-start(bf16[16,8,1152]{2,1,0:T(8,128)(2,1)} %bitcast.17), calls=%async_computation.6 | async-start | bytes 589824 | tf_op jit(solution)/shard_map/all_to_all | solution.py:35
  130.3 1.0 convolution_multiply_fusion
  131.3 8.5 %all-to-all-done.6 = bf16[16,8,1152]{2,1,0:T(8,128)(2,1)S(1)} async-done(((bf16[16,8,1152]{2,1,0:T(8,128)(2,1)}), bf16[16,8,1152]{2,1,0:T(8,128)(2,1)S(1)}, u32[]{:S(2)}, u32[]{:S(2)}) %all-to-all-start.6) | async-done | bytes 294944 | tf_op jit(solution)/shard_map/all_to_all | solution.py:35
  139.9 0.6 broadcast_in_dim.33
  140.5 5.5 %all-to-all-start.7 = ((bf16[16,8,128]{2,1,0:T(8,128)(2,1)}), bf16[16,8,128]{2,1,0:T(8,128)(2,1)S(1)}, u32[]{:S(2)}, u32[]{:S(2)}) async-start(bf16[16,8,128]{2,1,0:T(8,128)(2,1)} %broadcast_in_dim.33), calls=%async_computation.7 | async-start | bytes 65536 | tf_op jit(solution)/shard_map/all_to_all | solution.py:29
  146.1 0.7 fusion.2
  146.8 0.6 slice.63
  147.4 6.1 %all-to-all-done.7 = bf16[16,8,128]{2,1,0:T(8,128)(2,1)S(1)} async-done(((bf16[16,8,128]{2,1,0:T(8,128)(2,1)}), bf16[16,8,128]{2,1,0:T(8,128)(2,1)S(1)}, u32[]{:S(2)}, u32[]{:S(2)}) %all-to-all-start.7) | async-done | bytes 32800 | tf_op jit(solution)/shard_map/all_to_all | solution.py:29
  153.5 3.8 %all_gather.7 = bf16[256,128]{1,0:T(8,128)(2,1)S(1)} all-gather(bf16[128,128]{1,0:T(8,128)(2,1)S(1)} %bitcast.41), channel_id=1, replica_groups=mesh['zlo'=2,'y'=8,'core'=2,'zhi'=4,'x'=4] {'core'}, dimensions={0}, use_global_device_ids=true | all-gather | bytes 98304 | tf_op jit(solution)/shard_map/all_gather | solution.py:121
  157.3 0.9 fusion.11
  (10 shorter events, 0.2 us)
Async XLA Ops:
  0.6 24.5 %copy-start = (bf16[512,896]{1,0:T(8,128)(2,1)S(1)}, bf16[512,896]{1,0:T(8,128)(2,1)}, u32[]{:S(2)}) copy-start(bf16[512,896]{1,0:T(8,128)(2,1)} %param.9) | copy-start | bytes 2752516
  0.6 23.3 %copy-start.5 = (bf16[2,512,64]{1,2,0:T(8,128)(2,1)S(1)}, bf16[2,512,64]{1,2,0:T(8,128)(2,1)}, u32[]{:S(2)}) copy-start(bf16[2,512,64]{1,2,0:T(8,128)(2,1)} %param.12) | copy-start | bytes 393220
  0.7 23.5 %copy-start.3 = (bf16[512,896]{1,0:T(8,128)(2,1)S(1)}, bf16[512,896]{1,0:T(8,128)(2,1)}, u32[]{:S(2)}) copy-start(bf16[512,896]{1,0:T(8,128)(2,1)} %param.10) | copy-start | bytes 2752516
  19.6 5.0 %copy-start.1 = (bf16[896,512]{1,0:T(8,128)(2,1)S(1)}, bf16[896,512]{1,0:T(8,128)(2,1)}, u32[]{:S(2)}) copy-start(bf16[896,512]{1,0:T(8,128)(2,1)} %param.11) | copy-start | bytes 2752516
  47.9 10.3 %copy-start.6 = (s32[2]{0:T(128)S(1)}, s32[2]{0:T(128)}, u32[]{:S(2)}) copy-start(s32[2]{0:T(128)} %param.14) | copy-start | bytes 28
  49.0 23.0 %copy-start.7 = (bf16[2,64,896]{2,1,0:T(8,128)(2,1)S(1)}, bf16[2,64,896]{2,1,0:T(8,128)(2,1)}, u32[]{:S(2)}) copy-start(bf16[2,64,896]{2,1,0:T(8,128)(2,1)} %param.13) | copy-start | bytes 688132
  49.0 22.9 %all-to-all-start.2 = ((f32[4,16,2816]{2,1,0:T(8,128)}), f32[4,16,2816]{2,1,0:T(8,128)S(1)}, u32[]{:S(2)}, u32[]{:S(2)}) async-start(f32[4,16,2816]{2,1,0:T(8,128)} %bitcast.4), calls=%async_computation.2 | async-start | bytes 1441792 | tf_op jit(solution)/shard_map/all_to_all | solution.py:35
  88.4 15.9 %all-to-all-start.4 = ((bf16[4,64,2816]{2,1,0:T(8,128)(2,1)}), bf16[4,64,2816]{2,1,0:T(8,128)(2,1)S(1)}, u32[]{:S(2)}, u32[]{:S(2)}) async-start(bf16[4,64,2816]{2,1,0:T(8,128)(2,1)} %broadcast_in_dim.30), calls=%async_computation.4 | async-start | bytes 2883584 | tf_op jit(solution)/shard_map/all_to_all | solution.py:29
  104.4 1.2 copy-start.2
  104.4 1.6 %copy-start.4 = (bf16[512,896]{1,0:T(8,128)(2,1)S(1)}, bf16[512,896]{1,0:T(8,128)(2,1)}, u32[]{:S(2)}) copy-start(bf16[512,896]{1,0:T(8,128)(2,1)} %param.10) | copy-start | bytes 2752516
  122.0 17.9 %all-to-all-start.6 = ((bf16[16,8,1152]{2,1,0:T(8,128)(2,1)}), bf16[16,8,1152]{2,1,0:T(8,128)(2,1)S(1)}, u32[]{:S(2)}, u32[]{:S(2)}) async-start(bf16[16,8,1152]{2,1,0:T(8,128)(2,1)} %bitcast.17), calls=%async_computation.6 | async-start | bytes 589824 | tf_op jit(solution)/shard_map/all_to_all | solution.py:35
  140.5 12.9 %all-to-all-start.7 = ((bf16[16,8,128]{2,1,0:T(8,128)(2,1)}), bf16[16,8,128]{2,1,0:T(8,128)(2,1)S(1)}, u32[]{:S(2)}, u32[]{:S(2)}) async-start(bf16[16,8,128]{2,1,0:T(8,128)(2,1)} %broadcast_in_dim.33), calls=%async_computation.7 | async-start | bytes 65536 | tf_op jit(solution)/shard_map/all_to_all | solution.py:29

commit v2 on v1

--- a/solution.py
+++ b/solution.py
@@ -51,7 +51,16 @@
     first = jnp.transpose(adapter_first_factors, (1, 0, 2)).reshape(width, columns)
     second = adapter_second_factors.reshape(columns, hidden_units)
 
+    own = jnp.arange(columns, dtype=jnp.int32) // rank
+    masks = (own[None, :] == adapter_of_block[:, None]).astype(f32)
+    own_mask = lax.dynamic_slice_in_dim(masks, lax.axis_index("x") % 2, 1, 0)
+    block_mask = lax.dynamic_slice_in_dim(masks, lax.axis_index("zlo"), 1, 0)
     both = jnp.concatenate([tokens, cotangent], axis=1)
+    own_columns = lax.axis_index("y") * columns
+    masks16, block_mask = masks.astype(bf16), block_mask.astype(bf16)
+    both, masks, masks16, own_mask, block_mask, own_columns = lax.optimization_barrier(
+        (both, masks, masks16, own_mask, block_mask, own_columns)
+    )
     both = lax.all_gather(gather_rows(both, PIPE_LINKS), "core", axis=0, tiled=True)
     token_rows, adjoint_rows = both[:, :width], both[:, width:]
 
@@ -66,20 +75,6 @@
     )
     parts = scatter_sum(scatter_sum(parts, "x", bf16), "zhi", f32)
 
-    def mask_of(block):
-        own = jnp.arange(columns, dtype=jnp.int32) // rank
-        chosen = jnp.sum(
-            jnp.where(
-                block[:, None] == jnp.arange(adapter_of_block.shape[0], dtype=jnp.int32)[None, :],
-                adapter_of_block[None, :],
-                0,
-            ),
-            axis=1,
-        )
-        return (own[None, :] == chosen[:, None]).astype(f32)
-
-    x_index = lax.axis_index("x")
-    own_mask = mask_of(jnp.full((1,), x_index % 2, jnp.int32))
     gate = parts[:, :hidden_units]
     up_base = parts[:, hidden_units : 2 * hidden_units]
     grad_hidden = parts[:, 2 * hidden_units : 3 * hidden_units]
@@ -98,9 +93,10 @@
     grad_up_all = rows[:, 2 * hidden_units : 3 * hidden_units]
     low_all = rows[:, 3 * hidden_units :]
 
-    row_total = rows.shape[0]
-    row_block = (jnp.arange(row_total, dtype=jnp.int32) // (row_total // 4)) % 2
-    all_mask = mask_of(row_block)
+    quarter = rows.shape[0] // 4
+    all_mask = jnp.broadcast_to(masks[None, :, None, :], (2, 2, quarter, columns)).reshape(
+        rows.shape[0], columns
+    )
     partial = jnp.concatenate(
         [
             product(hidden_all, down_weight),
@@ -110,15 +106,34 @@
         ],
         axis=1,
     )
-    summed = scatter_sum(scatter_sum(partial, "core", f32), PIPE_LINKS, bf16)
-    mixed = summed[:, :width].astype(bf16)
-    low_own = summed[:, 2 * width :].astype(bf16)
-    grad_tokens = (summed[:, width : 2 * width] + trailing_product(low_own, first)).astype(bf16)
-
     grad_b = (adapter_scale * leading_product(low_all, grad_up_all)).reshape(
         adapters, rank, hidden_units
     )
-    low_back = lax.all_gather(gather_rows(low_own, PIPE_LINKS), "core", axis=0, tiled=True)
+    partial, grad_b = lax.optimization_barrier((partial, grad_b))
+
+    summed = scatter_sum(partial, "core", f32)
+    packed = (summed[:quarter, 2 * width :] + summed[quarter:, 2 * width :]).astype(bf16)
+    peers = lax.axis_size(PIPE_LINKS)
+    wide = jnp.transpose(packed.reshape(-1, 8, columns), (1, 0, 2)).reshape(8, -1)
+    sent = jnp.concatenate(
+        [
+            summed[:, : 2 * width].astype(bf16).reshape(peers, -1, 2 * width),
+            jnp.broadcast_to(wide[None], (peers,) + wide.shape),
+        ],
+        axis=2,
+    )
+    summed = jnp.sum(lax.all_to_all(sent, PIPE_LINKS, 0, 0).astype(f32), axis=0)
+    mixed = summed[:, :width].astype(bf16)
+    wide = summed[:, 2 * width :].astype(bf16)
+    packed = jnp.transpose(wide.reshape(8, -1, columns), (1, 0, 2)).reshape(quarter, columns)
+    low_own = lax.dynamic_slice(
+        wide, (0, own_columns), (8, columns), allow_negative_indices=False
+    )
+    low_own = low_own * block_mask
+    grad_tokens = (summed[:, width : 2 * width] + trailing_product(low_own, first)).astype(bf16)
+
+    packed = lax.all_gather(packed, "core", axis=0)
+    low_back = (packed[:, None] * masks16[None, :, None, :]).reshape(-1, columns)
     grad_a = leading_product(token_rows, low_back).reshape(width, adapters, rank)
     return mixed, grad_tokens, jnp.transpose(grad_a, (1, 0, 2)), grad_b
 

time: 159 us -> 150 us (0.943)
  blocking collectives: 76.4 us -> 136 us
  waiting for transfers between devices: 39.3 us -> 0 us
  starting transfers between devices: 26.6 us -> 0 us
  local copies, waits for them, and re-layouts: 3.22 us -> 0.96 us
    all_to_all x4 -> x0, waiting for transfers between devices: 39.3 us -> none  [the longest x2 20.9 us: scatter_sum(): return jnp.sum(lax.all_to_all(blocks, axis, 0, 0).astype(f32), axis=0)]
    all_to_all x4 -> x0, starting transfers between devices: 26.6 us -> none  [the longest x2 17.6 us: scatter_sum(): return jnp.sum(lax.all_to_all(blocks, axis, 0, 0).astype(f32), axis=0)]
    all_to_all x2 -> x3, blocking collectives: 35.2 us -> 58.8 us  [scatter_sum(): return jnp.sum(lax.all_to_all(blocks, axis, 0, 0).astype(f32), axis=0)]
    all_to_all x0 -> x1, blocking collectives: none -> 22.4 us  [on_device(): summed = jnp.sum(lax.all_to_all(sent, PIPE_LINKS, 0, 0).astype(f32), axis=0)]
    all_to_all x2 -> x3, blocking collectives: 33.1 us -> 46.5 us  [gather_rows(): lax.all_to_all(blocks, axis, 0, 0)]
    broadcast_in_dim x4 -> x3, local copies, waits for them, and re-layouts: 1.88 us -> 0.14 us  [gather_rows(): blocks = jnp.broadcast_to(value[None], (count,) + value.shape)]
    reduce_sum x4 -> x3, other arithmetic: 3.29 us -> 2.15 us  [scatter_sum(): return jnp.sum(lax.all_to_all(blocks, axis, 0, 0).astype(f32), axis=0)]
  transfers between devices with their start and end apart: 4 -> 0, of which waited for: 4 -> 0; matrix products, arithmetic and copies ran while one was open for 2% -> 0% of each run, Pallas kernels for 0% -> 0%
where the time goes in v2:
time: 150 us
  blocking collectives  136 us (91%)
  matrix products  6.96 us (5%)
  other arithmetic  4.78 us (3%)
    all_to_all x3, blocking collectives, scatter_sum(): return jnp.sum(lax.all_to_all(blocks, axis, 0, 0).astype(f32), axis=0)  58.8 us
    all_to_all x3, blocking collectives, gather_rows(): lax.all_to_all(blocks, axis, 0, 0)  46.5 us
    all_to_all x1, blocking collectives, on_device(): summed = jnp.sum(lax.all_to_all(sent, PIPE_LINKS, 0, 0).astype(f32), axis=0)  22.4 us
    all_gather x1, blocking collectives, on_device(): packed = lax.all_gather(packed, 'core', axis=0)  4.29 us
    all_gather x1, blocking collectives, on_device(): lax.all_gather(gather_rows(both, PIPE_LINKS), 'core', axis=0, tiled=True)  4.27 us

profile of v2, /device:TPU:1, one launch (start us, length us, event | category | flops | bytes accessed | tf_op | source)
XLA Modules:
  0.0 149.9 jit_solution(13653355122545656812)
XLA Ops:
  0.6 0.0 copy-start
  0.6 0.0 copy-start.4
  0.7 0.0 copy-start.2
  0.7 0.9 fusion.27
  1.6 0.7 pad_maximum_fusion.4
  2.3 18.1 %all_to_all.35 = bf16[16,8,1024]{2,1,0:T(8,128)(2,1)S(1)} all-to-all(bf16[16,8,1024]{2,1,0:T(8,128)(2,1)S(1)} %broadcast_in_dim.14), channel_id=1, replica_groups=mesh['zlo'=2,'y'=8,'core'=2,'zhi'=4,'x'=4] {'zlo','y'}, dimensions={0} | all-to-all | bytes 524288 | tf_op jit(solution)/shard_map/all_to_all | solution.py:29
  20.4 0.0 copy-start.1
  20.4 4.3 %all_gather.6 = bf16[256,1024]{1,0:T(8,128)(2,1)S(1)} all-gather(bf16[128,1024]{1,0:T(8,128)(2,1)S(1)} %bitcast.58), channel_id=1, replica_groups=mesh['zlo'=2,'y'=8,'core'=2,'zhi'=4,'x'=4] {'core'}, dimensions={0}, use_global_device_ids=true | all-gather | bytes 786432 | tf_op jit(solution)/shard_map/all_gather | solution.py:64
  24.7 0.0 copy-done.4
  24.7 0.2 convolution_convert_fusion.3
  24.9 0.0 copy-done.2
  24.9 0.4 convolution_convert_fusion.1
  25.4 0.0 copy-done.1
  25.4 0.5 convolution_convert_fusion
  25.9 0.0 copy-done
  25.9 0.4 convolution_convert_fusion.2
  26.3 0.1 pad_maximum_fusion
  26.4 22.2 %all_to_all.36 = bf16[4,64,2816]{2,1,0:T(8,128)(2,1)S(1)} all-to-all(bf16[4,64,2816]{2,1,0:T(8,128)(2,1)S(1)} %bitcast.54), channel_id=1, replica_groups=mesh['zlo'=2,'y'=8,'core'=2,'zhi'=4,'x'=4] {'x'}, dimensions={0} | all-to-all | bytes 2883584 | tf_op jit(solution)/shard_map/all_to_all | solution.py:35
  48.7 0.2 convert_reduce_fusion
  48.9 0.0 copy-start.3
  48.9 24.7 %all_to_all.37 = f32[4,16,2816]{2,1,0:T(8,128)} all-to-all(f32[4,16,2816]{2,1,0:T(8,128)S(1)} %bitcast.56), channel_id=1, replica_groups=mesh['zlo'=2,'y'=8,'core'=2,'zhi'=4,'x'=4] {'zhi'}, dimensions={0} | all-to-all | bytes 1441792 | tf_op jit(solution)/shard_map/all_to_all | solution.py:35
  73.6 1.8 %reduce_sum.37 = f32[16,2816]{1,0:T(8,128)} reduce(f32[4,16,2816]{2,1,0:T(8,128)} %all_to_all.37, f32[]{:T(128)} %constant.53.clone.1), dimensions={0}, to_apply=%region_1.2 | reduce | flops 135168 | bytes 901124 | tf_op jit(solution)/shard_map/reduce_sum | solution.py:35
  75.4 0.7 fusion.21
  76.1 0.0 copy-done.3
  76.1 1.0 multiply_convert_fusion.2
  77.2 13.3 %all_to_all.38 = bf16[4,16,2816]{2,1,0:T(8,128)(2,1)S(1)} all-to-all(bf16[4,16,2816]{2,1,0:T(8,128)(2,1)S(1)} %broadcast_in_dim.15), channel_id=1, replica_groups=mesh['zlo'=2,'y'=8,'core'=2,'zhi'=4,'x'=4] {'zhi'}, dimensions={0} | all-to-all | bytes 720896 | tf_op jit(solution)/shard_map/all_to_all | solution.py:29
  90.5 0.1 broadcast_in_dim.17
  90.6 15.1 %all_to_all.39 = bf16[4,64,2816]{2,1,0:T(8,128)(2,1)S(1)} all-to-all(bf16[4,64,2816]{2,1,0:T(8,128)(2,1)S(1)} %broadcast_in_dim.17), channel_id=1, replica_groups=mesh['zlo'=2,'y'=8,'core'=2,'zhi'=4,'x'=4] {'x'}, dimensions={0} | all-to-all | bytes 2883584 | tf_op jit(solution)/shard_map/all_to_all | solution.py:29
  105.7 1.0 convolution_multiply_fusion
  106.7 0.5 fusion.3
  107.2 0.4 fusion.5
  107.6 0.3 fusion
  107.9 0.5 convolution_add_fusion
  108.4 0.1 pad_maximum_fusion.1
  108.5 11.9 %all_to_all.40 = f32[2,128,1152]{2,1,0:T(8,128)S(1)} all-to-all(f32[2,128,1152]{2,1,0:T(8,128)S(1)} %bitcast.55), channel_id=1, replica_groups=mesh['zlo'=2,'y'=8,'core'=2,'zhi'=4,'x'=4] {'core'}, dimensions={0} | all-to-all | bytes 2359296 | tf_op jit(solution)/shard_map/all_to_all | solution.py:35
  120.4 0.1 reduce_sum.38
  120.7 0.0 copy-start.5
  120.7 22.4 %all_to_all.41 = bf16[16,8,2048]{2,1,0:T(8,128)(2,1)S(1)} all-to-all(bf16[16,8,2048]{2,1,0:T(8,128)(2,1)S(1)} %pad_maximum_fusion.2), channel_id=1, replica_groups=mesh['zlo'=2,'y'=8,'core'=2,'zhi'=4,'x'=4] {'zlo','y'}, dimensions={0} | all-to-all | bytes 1048576 | tf_op jit(solution)/shard_map/all_to_all | solution.py:125
  143.1 0.1 convert_reduce_fusion.1
  143.2 0.6 slice.80
  143.8 4.3 %all_gather.7 = bf16[2,64,128]{2,1,0:T(8,128)(2,1)S(1)} all-gather(bf16[1,64,128]{2,1,0:T(8,128)(2,1)S(1)} %get-tuple-element.23), channel_id=1, replica_groups=mesh['zlo'=2,'y'=8,'core'=2,'zhi'=4,'x'=4] {'core'}, dimensions={0}, use_global_device_ids=true | all-gather | bytes 49152 | tf_op jit(solution)/shard_map/all_gather | solution.py:135
  148.1 0.1 copy.27
  148.2 0.9 convolution_bitcast_fusion
  149.1 0.0 copy-done.5
  149.1 0.8 fusion.2
  (14 shorter events, 0.2 us)
Async XLA Ops:
  0.6 25.2 %copy-start = (bf16[512,896]{1,0:T(8,128)(2,1)S(1)}, bf16[512,896]{1,0:T(8,128)(2,1)}, u32[]{:S(2)}) copy-start(bf16[512,896]{1,0:T(8,128)(2,1)} %param.9) | copy-start | bytes 2752516
  0.6 24.1 %copy-start.4 = (bf16[2,512,64]{1,2,0:T(8,128)(2,1)S(1)}, bf16[2,512,64]{1,2,0:T(8,128)(2,1)}, u32[]{:S(2)}) copy-start(bf16[2,512,64]{1,2,0:T(8,128)(2,1)} %param.12) | copy-start | bytes 393220
  0.7 24.3 %copy-start.2 = (bf16[512,896]{1,0:T(8,128)(2,1)S(1)}, bf16[512,896]{1,0:T(8,128)(2,1)}, u32[]{:S(2)}) copy-start(bf16[512,896]{1,0:T(8,128)(2,1)} %param.10) | copy-start | bytes 2752516
  20.4 5.0 %copy-start.1 = (bf16[896,512]{1,0:T(8,128)(2,1)S(1)}, bf16[896,512]{1,0:T(8,128)(2,1)}, u32[]{:S(2)}) copy-start(bf16[896,512]{1,0:T(8,128)(2,1)} %param.11) | copy-start | bytes 2752516
  48.9 27.2 %copy-start.3 = (bf16[2,64,896]{2,1,0:T(8,128)(2,1)S(1)}, bf16[2,64,896]{2,1,0:T(8,128)(2,1)}, u32[]{:S(2)}) copy-start(bf16[2,64,896]{2,1,0:T(8,128)(2,1)} %param.13) | copy-start | bytes 688132
  120.7 28.5 %copy-start.5 = (bf16[2,512,64]{1,2,0:T(8,128)(2,1)S(1)}, bf16[2,512,64]{1,2,0:T(8,128)(2,1)}, u32[]{:S(2)}) copy-start(bf16[2,512,64]{1,2,0:T(8,128)(2,1)} %param.12) | copy-start | bytes 393220

commit v3 on v2

--- a/solution.py
+++ b/solution.py
@@ -33,6 +33,23 @@
     count = lax.axis_size(axis)
     blocks = value.astype(sent).reshape(count, value.shape[0] // count, value.shape[1])
     return jnp.sum(lax.all_to_all(blocks, axis, 0, 0).astype(f32), axis=0)
+
+
+def scatter_sum_own(pieces, axis, first_row, is_own):
+    count = lax.axis_size(axis)
+    rows = pieces[0].shape[0] // count
+    sent = jnp.concatenate([piece.astype(bf16) for piece in pieces], axis=1)
+    came = lax.all_to_all(sent.reshape(count, rows, sent.shape[1]), axis, 0, 0).astype(f32)
+    own = jnp.concatenate(
+        [
+            lax.dynamic_slice(
+                piece, (first_row, 0), (rows, piece.shape[1]), allow_negative_indices=False
+            )
+            for piece in pieces
+        ],
+        axis=1,
+    )
+    return jnp.sum(jnp.where(is_own[:, None, None], own[None], came), axis=0)
 
 
 def on_device(
@@ -58,22 +75,46 @@
     both = jnp.concatenate([tokens, cotangent], axis=1)
     own_columns = lax.axis_index("y") * columns
     masks16, block_mask = masks.astype(bf16), block_mask.astype(bf16)
-    both, masks, masks16, own_mask, block_mask, own_columns = lax.optimization_barrier(
-        (both, masks, masks16, own_mask, block_mask, own_columns)
+    own_rows_x = lax.axis_index("x") * 64
+    own_rows_z = lax.axis_index("zhi") * 16
+    is_own_x = jnp.arange(4, dtype=jnp.int32) == lax.axis_index("x")
+    is_own_z = jnp.arange(4, dtype=jnp.int32) == lax.axis_index("zhi")
+    (
+        both,
+        masks,
+        masks16,
+        own_mask,
+        block_mask,
+        own_columns,
+        own_rows_x,
+        own_rows_z,
+        is_own_x,
+        is_own_z,
+    ) = lax.optimization_barrier(
+        (
+            both,
+            masks,
+            masks16,
+            own_mask,
+            block_mask,
+            own_columns,
+            own_rows_x,
+            own_rows_z,
+            is_own_x,
+            is_own_z,
+        )
     )
     both = lax.all_gather(gather_rows(both, PIPE_LINKS), "core", axis=0, tiled=True)
     token_rows, adjoint_rows = both[:, :width], both[:, width:]
 
-    parts = jnp.concatenate(
-        [
-            product(token_rows, gate_weight).astype(bf16),
-            product(token_rows, upward_weight).astype(bf16),
-            trailing_product(adjoint_rows, down_weight).astype(bf16),
-            product(token_rows, first).astype(bf16),
-        ],
-        axis=1,
-    )
-    parts = scatter_sum(scatter_sum(parts, "x", bf16), "zhi", f32)
+    pieces = [
+        product(token_rows, gate_weight),
+        product(token_rows, upward_weight),
+        trailing_product(adjoint_rows, down_weight),
+        product(token_rows, first),
+    ]
+    parts = scatter_sum_own(pieces, "x", own_rows_x, is_own_x)
+    parts = scatter_sum_own([parts], "zhi", own_rows_z, is_own_z)
 
     gate = parts[:, :hidden_units]
     up_base = parts[:, hidden_units : 2 * hidden_units]

time: 150 us -> 147 us (0.980)
  blocking collectives: 136 us -> 87.6 us
  waiting for transfers between devices: 0 us -> 22.5 us
  starting transfers between devices: 0 us -> 13.1 us
  local copies, waits for them, and re-layouts: 0.96 us -> 6.44 us
  matrix products: 6.96 us -> 8.88 us
  other arithmetic: 4.78 us -> 6.55 us
    all_to_all x3 -> x1, blocking collectives: 58.8 us -> 10.4 us  [scatter_sum(): return jnp.sum(lax.all_to_all(blocks, axis, 0, 0).astype(f32), axis=0)]
    all_to_all x0 -> x2, waiting for transfers between devices: none -> 22.5 us  [scatter_sum_own(): lax.all_to_all(sent.reshape(count, rows, sent.shape[1]), axis, 0, 0)]
    all_to_all x0 -> x2, starting transfers between devices: none -> 13.1 us  [scatter_sum_own(): lax.all_to_all(sent.reshape(count, rows, sent.shape[1]), axis, 0, 0)]
    dynamic_slice x0 -> x5, local copies, waits for them, and re-layouts: none -> 3.92 us  [scatter_sum_own(): lax.dynamic_slice(piece, (first_row, 0), (rows, piece.shape[1]), allow_ne...]
    all_to_all x1, blocking collectives: 22.4 us -> 19.6 us  [on_device(): summed = jnp.sum(lax.all_to_all(sent, PIPE_LINKS, 0, 0).astype(f32), axis=0)]
    all_to_all x3, blocking collectives: 46.5 us -> 49.2 us  [gather_rows(): lax.all_to_all(blocks, axis, 0, 0)]
    reduce_sum x3 -> x1, other arithmetic: 2.15 us -> 0.12 us  [scatter_sum(): return jnp.sum(lax.all_to_all(blocks, axis, 0, 0).astype(f32), axis=0)]
    concatenate x1 -> x2, other arithmetic: 0.11 us -> 2.14 us  [the longest x1 1.22 us: scatter_sum_own(): sent = jnp.concatenate([piece.astype(bf16) for piece in pieces], axis=1)]
  transfers between devices with their start and end apart: 0 -> 2, of which waited for: 0 -> 2; matrix products, arithmetic and copies ran while one was open for 0% -> 3% of each run, Pallas kernels for 0% -> 0%
where the time goes in v3:
time: 147 us; the launch traced here: 146 us
  blocking collectives  87.6 us (60%)
  waiting for transfers between devices  22.5 us (15%)
  starting transfers between devices  13.1 us (9%)
  matrix products  8.88 us (6%)
  other arithmetic  6.55 us (4%)
  local copies, waits for them, and re-layouts  6.44 us (4%)
    all_to_all x3, blocking collectives, gather_rows(): lax.all_to_all(blocks, axis, 0, 0)  49.2 us
    all_to_all x2, waiting for transfers between devices, scatter_sum_own(): lax.all_to_all(sent.reshape(count, rows, sent.shape[1]), axis, 0, 0)  22.5 us
    all_to_all x1, blocking collectives, on_device(): summed = jnp.sum(lax.all_to_all(sent, PIPE_LINKS, 0, 0).astype(f32), axis=0)  19.6 us
    all_to_all x2, starting transfers between devices, scatter_sum_own(): lax.all_to_all(sent.reshape(count, rows, sent.shape[1]), axis, 0, 0)  13.1 us
    all_to_all x1, blocking collectives, scatter_sum(): return jnp.sum(lax.all_to_all(blocks, axis, 0, 0).astype(f32), axis=0)  10.4 us
    all_gather x1, blocking collectives, on_device(): packed = lax.all_gather(packed, 'core', axis=0)  4.29 us
    all_gather x1, blocking collectives, on_device(): lax.all_gather(gather_rows(both, PIPE_LINKS), 'core', axis=0, tiled=True)  4.14 us
    dynamic_slice x5, local copies, waits for them, and re-layouts, scatter_sum_own(): lax.dynamic_slice(piece, (first_row, 0), (rows, piece.shape[1]), allow_ne...  3.92 us
  transfers between devices with their start and end apart: 2, of which 2 were waited for; matrix products, arithmetic and copies ran while one was open for 3% of the time, Pallas kernels for 0%

profile of v3, /device:TPU:1, one launch (start us, length us, event | category | flops | bytes accessed | tf_op | source)
XLA Modules:
  0.0 146.1 jit_solution(9475315997325040085)
XLA Ops:
  0.6 0.0 copy-start
  0.6 0.0 copy-start.1
  0.7 0.9 fusion.31
  1.6 0.7 pad_maximum_fusion.5
  2.3 18.1 %all_to_all.35 = bf16[16,8,1024]{2,1,0:T(8,128)(2,1)S(1)} all-to-all(bf16[16,8,1024]{2,1,0:T(8,128)(2,1)S(1)} %broadcast_in_dim.48), channel_id=1, replica_groups=mesh['zlo'=2,'y'=8,'core'=2,'zhi'=4,'x'=4] {'zlo','y'}, dimensions={0} | all-to-all | bytes 524288 | tf_op jit(solution)/shard_map/all_to_all | solution.py:29
  20.4 4.1 %all_gather.6 = bf16[256,1024]{1,0:T(8,128)(2,1)S(1)} all-gather(bf16[128,1024]{1,0:T(8,128)(2,1)S(1)} %bitcast.57), channel_id=1, replica_groups=mesh['zlo'=2,'y'=8,'core'=2,'zhi'=4,'x'=4] {'core'}, dimensions={0}, use_global_device_ids=true | all-gather | bytes 786432 | tf_op jit(solution)/shard_map/all_gather | solution.py:107
  24.6 0.0 copy-done.1
  24.6 0.0 copy-start.3
  24.6 1.4 fusion.33
  26.0 0.0 copy-done.3
  26.0 1.4 fusion.34
  27.3 0.0 copy-done
  27.3 0.0 copy-start.6
  27.3 1.4 fusion.35
  28.7 0.0 copy-done.6
  28.7 0.2 fusion.32
  29.0 1.2 pad_maximum_fusion
  30.2 4.0 %all-to-all-start.1 = ((bf16[4,64,2816]{2,1,0:T(8,128)(2,1)}), bf16[4,64,2816]{2,1,0:T(8,128)(2,1)S(1)}, u32[]{:S(2)}, u32[]{:S(2)}) async-start(bf16[4,64,2816]{2,1,0:T(8,128)(2,1)} %bitcast.54), calls=%async_computation.1 | async-start | bytes 2883584 | tf_op jit(solution)/shard_map/all_to_all | solution.py:42
  34.2 1.0 constant_dynamic-slice_fusion.2
  35.2 1.0 constant_dynamic-slice_fusion.3
  36.2 1.0 constant_dynamic-slice_fusion.4
  37.2 0.9 pad_maximum_fusion.2
  38.1 14.9 %all-to-all-done.1 = bf16[4,64,2816]{2,1,0:T(8,128)(2,1)S(1)} async-done(((bf16[4,64,2816]{2,1,0:T(8,128)(2,1)}), bf16[4,64,2816]{2,1,0:T(8,128)(2,1)S(1)}, u32[]{:S(2)}, u32[]{:S(2)}) %all-to-all-start.1) | async-done | bytes 1441824 | tf_op jit(solution)/shard_map/all_to_all | solution.py:42
  52.9 1.6 %select_reduce_fusion = f32[64,2816]{1,0:T(8,128)S(1)} fusion(bf16[4,64,2816]{2,1,0:T(8,128)(2,1)S(1)} %all-to-all-done.1, f32[64,2816]{1,0:T(8,128)} %pad_maximum_fusion.2, pred[4]{0:T(512)(128)(4,1)S(1)} %get-tuple-element.17), kind=kLoop, calls=%fused_computation | loop fusion | flops 1982464 | bytes 2883588 | tf_op jit(solution)/shard_map/reduce_sum | solution.py:52
  54.5 0.0 copy-start.5
  54.5 0.9 copy-done.5
  55.4 0.0 copy-start.7
  55.4 0.8 convert_element_type.66
  56.1 9.1 %all-to-all-start.2 = ((bf16[4,16,2816]{2,1,0:T(8,128)(2,1)}), bf16[4,16,2816]{2,1,0:T(8,128)(2,1)S(1)}, u32[]{:S(2)}, u32[]{:S(2)}) async-start(bf16[4,16,2816]{2,1,0:T(8,128)(2,1)} %bitcast.4), calls=%async_computation.2 | async-start | bytes 720896 | tf_op jit(solution)/shard_map/all_to_all | solution.py:42
  65.3 1.0 constant_dynamic-slice_fusion
  66.2 7.7 %all-to-all-done.2 = bf16[4,16,2816]{2,1,0:T(8,128)(2,1)S(1)} async-done(((bf16[4,16,2816]{2,1,0:T(8,128)(2,1)}), bf16[4,16,2816]{2,1,0:T(8,128)(2,1)S(1)}, u32[]{:S(2)}, u32[]{:S(2)}) %all-to-all-start.2) | async-done | bytes 360480 | tf_op jit(solution)/shard_map/all_to_all | solution.py:42
  73.9 0.1 select_reduce_fusion.1
  74.1 0.0 copy-done.7
  74.1 0.2 multiply_convert_fusion.2
  74.3 14.5 %all_to_all.36 = bf16[4,16,2816]{2,1,0:T(8,128)(2,1)S(1)} all-to-all(bf16[4,16,2816]{2,1,0:T(8,128)(2,1)S(1)} %broadcast_in_dim.77), channel_id=1, replica_groups=mesh['zlo'=2,'y'=8,'core'=2,'zhi'=4,'x'=4] {'zhi'}, dimensions={0} | all-to-all | bytes 720896 | tf_op jit(solution)/shard_map/all_to_all | solution.py:29
  88.8 0.1 broadcast_in_dim.79
  88.9 16.6 %all_to_all.37 = bf16[4,64,2816]{2,1,0:T(8,128)(2,1)S(1)} all-to-all(bf16[4,64,2816]{2,1,0:T(8,128)(2,1)S(1)} %broadcast_in_dim.79), channel_id=1, replica_groups=mesh['zlo'=2,'y'=8,'core'=2,'zhi'=4,'x'=4] {'x'}, dimensions={0} | all-to-all | bytes 2883584 | tf_op jit(solution)/shard_map/all_to_all | solution.py:29
  105.5 0.0 copy-start.2
  105.5 0.5 fusion.3
  106.0 0.7 copy-done.2
  106.7 0.0 copy-start.4
  106.7 0.4 fusion.5
  107.2 1.0 convolution_multiply_fusion
  108.2 0.0 copy-done.4
  108.2 0.5 convolution_add_fusion
  108.7 0.3 fusion
  109.0 0.1 pad_maximum_fusion.1
  109.1 10.4 %all_to_all.38 = f32[2,128,1152]{2,1,0:T(8,128)S(1)} all-to-all(f32[2,128,1152]{2,1,0:T(8,128)S(1)} %bitcast.55), channel_id=1, replica_groups=mesh['zlo'=2,'y'=8,'core'=2,'zhi'=4,'x'=4] {'core'}, dimensions={0} | all-to-all | bytes 2359296 | tf_op jit(solution)/shard_map/all_to_all | solution.py:35
  119.4 0.1 reduce_sum.38
  119.7 19.6 %all_to_all.39 = bf16[16,8,2048]{2,1,0:T(8,128)(2,1)S(1)} all-to-all(bf16[16,8,2048]{2,1,0:T(8,128)(2,1)S(1)} %pad_maximum_fusion.3), channel_id=1, replica_groups=mesh['zlo'=2,'y'=8,'core'=2,'zhi'=4,'x'=4] {'zlo','y'}, dimensions={0} | all-to-all | bytes 1048576 | tf_op jit(solution)/shard_map/all_to_all | solution.py:166
  139.3 0.1 convert_reduce_fusion
  139.4 0.6 slice.80
  140.0 4.3 %all_gather.7 = bf16[2,64,128]{2,1,0:T(8,128)(2,1)S(1)} all-gather(bf16[1,64,128]{2,1,0:T(8,128)(2,1)S(1)} %get-tuple-element.31), channel_id=1, replica_groups=mesh['zlo'=2,'y'=8,'core'=2,'zhi'=4,'x'=4] {'core'}, dimensions={0}, use_global_device_ids=true | all-gather | bytes 49152 | tf_op jit(solution)/shard_map/all_gather | solution.py:176
  144.3 0.1 copy.22
  144.4 0.9 convolution_bitcast_fusion
  145.3 0.8 fusion.2
  (17 shorter events, 0.2 us)
Async XLA Ops:
  0.6 26.7 %copy-start = (bf16[512,896]{1,0:T(8,128)(2,1)S(1)}, bf16[512,896]{1,0:T(8,128)(2,1)}, u32[]{:S(2)}) copy-start(bf16[512,896]{1,0:T(8,128)(2,1)} %param.9) | copy-start | bytes 2752516
  0.6 23.9 %copy-start.1 = (bf16[896,512]{1,0:T(8,128)(2,1)S(1)}, bf16[896,512]{1,0:T(8,128)(2,1)}, u32[]{:S(2)}) copy-start(bf16[896,512]{1,0:T(8,128)(2,1)} %param.11) | copy-start | bytes 2752516
  24.6 1.4 copy-start.3
  27.3 1.4 copy-start.6
  30.2 22.8 %all-to-all-start.1 = ((bf16[4,64,2816]{2,1,0:T(8,128)(2,1)}), bf16[4,64,2816]{2,1,0:T(8,128)(2,1)S(1)}, u32[]{:S(2)}, u32[]{:S(2)}) async-start(bf16[4,64,2816]{2,1,0:T(8,128)(2,1)} %bitcast.54), calls=%async_computation.1 | async-start | bytes 2883584 | tf_op jit(solution)/shard_map/all_to_all | solution.py:42
  54.5 0.9 copy-start.5
  55.4 18.7 %copy-start.7 = (bf16[2,64,896]{2,1,0:T(8,128)(2,1)S(1)}, bf16[2,64,896]{2,1,0:T(8,128)(2,1)}, u32[]{:S(2)}) copy-start(bf16[2,64,896]{2,1,0:T(8,128)(2,1)} %param.13) | copy-start | bytes 688132
  56.1 17.8 %all-to-all-start.2 = ((bf16[4,16,2816]{2,1,0:T(8,128)(2,1)}), bf16[4,16,2816]{2,1,0:T(8,128)(2,1)S(1)}, u32[]{:S(2)}, u32[]{:S(2)}) async-start(bf16[4,16,2816]{2,1,0:T(8,128)(2,1)} %bitcast.4), calls=%async_computation.2 | async-start | bytes 720896 | tf_op jit(solution)/shard_map/all_to_all | solution.py:42
  105.5 1.2 copy-start.2
  106.7 1.5 %copy-start.4 = (bf16[512,896]{1,0:T(8,128)(2,1)S(1)}, bf16[512,896]{1,0:T(8,128)(2,1)}, u32[]{:S(2)}) copy-start(bf16[512,896]{1,0:T(8,128)(2,1)} %param.10) | copy-start | bytes 2752516

commit v4 on v2

--- a/solution.py
+++ b/solution.py
@@ -73,7 +73,9 @@
         ],
         axis=1,
     )
-    parts = scatter_sum(scatter_sum(parts, "x", bf16), "zhi", f32)
+    groups = jnp.transpose(parts.reshape(4, 4, -1, parts.shape[1]), (1, 0, 2, 3))
+    groups = groups.reshape(16, -1, parts.shape[1])
+    parts = jnp.sum(lax.all_to_all(groups, TENSOR, 0, 0).astype(f32), axis=0)
 
     gate = parts[:, :hidden_units]
     up_base = parts[:, hidden_units : 2 * hidden_units]

time: 150 us -> 146 us (0.973)
  other arithmetic: 4.78 us -> 2.24 us
    all_to_all x3 -> x1, blocking collectives: 58.8 us -> 12.6 us  [scatter_sum(): return jnp.sum(lax.all_to_all(blocks, axis, 0, 0).astype(f32), axis=0)]
    all_to_all x0 -> x1, blocking collectives: none -> 42.3 us  [on_device(): parts = jnp.sum(lax.all_to_all(groups, TENSOR, 0, 0).astype(f32), axis=0)]
    reduce_sum x3 -> x1, other arithmetic: 2.15 us -> 0.12 us  [scatter_sum(): return jnp.sum(lax.all_to_all(blocks, axis, 0, 0).astype(f32), axis=0)]
where the time goes in v4:
time: 146 us
  blocking collectives  135 us (92%)
  matrix products  6.09 us (4%)
  other arithmetic  2.24 us (2%)
  local copies, waits for them, and re-layouts  1.78 us (1%)
    all_to_all x3, blocking collectives, gather_rows(): lax.all_to_all(blocks, axis, 0, 0)  47.9 us
    all_to_all x1, blocking collectives, on_device(): parts = jnp.sum(lax.all_to_all(groups, TENSOR, 0, 0).astype(f32), axis=0)  42.3 us
    all_to_all x1, blocking collectives, on_device(): summed = jnp.sum(lax.all_to_all(sent, PIPE_LINKS, 0, 0).astype(f32), axis=0)  23.4 us
    all_to_all x1, blocking collectives, scatter_sum(): return jnp.sum(lax.all_to_all(blocks, axis, 0, 0).astype(f32), axis=0)  12.6 us
    all_gather x1, blocking collectives, on_device(): packed = lax.all_gather(packed, 'core', axis=0)  4.29 us
    all_gather x1, blocking collectives, on_device(): lax.all_gather(gather_rows(both, PIPE_LINKS), 'core', axis=0, tiled=True)  4.27 us

profile of v4, /device:TPU:1, one launch (start us, length us, event | category | flops | bytes accessed | tf_op | source)
XLA Modules:
  0.0 145.8 jit_solution(4314457273239267164)
XLA Ops:
  0.6 0.0 copy-start
  0.6 0.0 copy-start.4
  0.7 0.0 copy-start.2
  0.7 0.9 fusion.27
  1.6 0.7 pad_maximum_fusion.4
  2.3 18.1 %all_to_all.30 = bf16[16,8,1024]{2,1,0:T(8,128)(2,1)S(1)} all-to-all(bf16[16,8,1024]{2,1,0:T(8,128)(2,1)S(1)} %broadcast_in_dim.14), channel_id=1, replica_groups=mesh['zlo'=2,'y'=8,'core'=2,'zhi'=4,'x'=4] {'zlo','y'}, dimensions={0} | all-to-all | bytes 524288 | tf_op jit(solution)/shard_map/all_to_all | solution.py:29
  20.4 0.0 copy-start.1
  20.4 4.3 %all_gather.6 = bf16[256,1024]{1,0:T(8,128)(2,1)S(1)} all-gather(bf16[128,1024]{1,0:T(8,128)(2,1)S(1)} %bitcast.60), channel_id=1, replica_groups=mesh['zlo'=2,'y'=8,'core'=2,'zhi'=4,'x'=4] {'core'}, dimensions={0}, use_global_device_ids=true | all-gather | bytes 786432 | tf_op jit(solution)/shard_map/all_gather | solution.py:64
  24.7 0.0 copy-done.4
  24.7 0.2 convolution_convert_fusion.3
  24.9 0.0 copy-done.2
  24.9 0.4 convolution_convert_fusion.1
  25.4 0.0 copy-done.1
  25.4 0.5 convolution_convert_fusion
  25.9 0.0 copy-done
  25.9 0.4 convolution_convert_fusion.2
  26.3 0.1 pad_maximum_fusion
  26.4 0.1 copy.29
  26.5 42.3 %all_to_all.31 = bf16[16,16,2816]{2,1,0:T(8,128)(2,1)S(1)} all-to-all(bf16[16,16,2816]{2,1,0:T(8,128)(2,1)S(1)} %bitcast.57), channel_id=1, replica_groups=mesh['zlo'=2,'y'=8,'core'=2,'zhi'=4,'x'=4] {'zhi','x'}, dimensions={0} | all-to-all | bytes 2883584 | tf_op jit(solution)/shard_map/all_to_all | solution.py:78
  68.9 0.0 copy-start.3
  68.9 0.2 convert_reduce_fusion
  69.1 0.7 copy-done.3
  69.8 0.2 multiply_convert_fusion.2
  70.0 15.4 %all_to_all.32 = bf16[4,16,2816]{2,1,0:T(8,128)(2,1)S(1)} all-to-all(bf16[4,16,2816]{2,1,0:T(8,128)(2,1)S(1)} %broadcast_in_dim.15), channel_id=1, replica_groups=mesh['zlo'=2,'y'=8,'core'=2,'zhi'=4,'x'=4] {'zhi'}, dimensions={0} | all-to-all | bytes 720896 | tf_op jit(solution)/shard_map/all_to_all | solution.py:29
  85.4 0.1 broadcast_in_dim.17
  85.5 14.5 %all_to_all.33 = bf16[4,64,2816]{2,1,0:T(8,128)(2,1)S(1)} all-to-all(bf16[4,64,2816]{2,1,0:T(8,128)(2,1)S(1)} %broadcast_in_dim.17), channel_id=1, replica_groups=mesh['zlo'=2,'y'=8,'core'=2,'zhi'=4,'x'=4] {'x'}, dimensions={0} | all-to-all | bytes 2883584 | tf_op jit(solution)/shard_map/all_to_all | solution.py:29
  100.0 1.0 convolution_multiply_fusion
  101.0 0.5 fusion.3
  101.5 0.4 fusion.5
  101.9 0.3 fusion
  102.2 0.5 convolution_add_fusion
  102.7 0.1 pad_maximum_fusion.1
  102.8 12.6 %all_to_all.34 = f32[2,128,1152]{2,1,0:T(8,128)S(1)} all-to-all(f32[2,128,1152]{2,1,0:T(8,128)S(1)} %bitcast.58), channel_id=1, replica_groups=mesh['zlo'=2,'y'=8,'core'=2,'zhi'=4,'x'=4] {'core'}, dimensions={0} | all-to-all | bytes 2359296 | tf_op jit(solution)/shard_map/all_to_all | solution.py:35
  115.3 0.1 reduce_sum.28
  115.6 23.4 %all_to_all.35 = bf16[16,8,2048]{2,1,0:T(8,128)(2,1)S(1)} all-to-all(bf16[16,8,2048]{2,1,0:T(8,128)(2,1)S(1)} %pad_maximum_fusion.2), channel_id=1, replica_groups=mesh['zlo'=2,'y'=8,'core'=2,'zhi'=4,'x'=4] {'zlo','y'}, dimensions={0} | all-to-all | bytes 1048576 | tf_op jit(solution)/shard_map/all_to_all | solution.py:127
  139.0 0.1 convert_reduce_fusion.1
  139.1 0.6 slice.80
  139.7 4.3 %all_gather.7 = bf16[2,64,128]{2,1,0:T(8,128)(2,1)S(1)} all-gather(bf16[1,64,128]{2,1,0:T(8,128)(2,1)S(1)} %get-tuple-element.23), channel_id=1, replica_groups=mesh['zlo'=2,'y'=8,'core'=2,'zhi'=4,'x'=4] {'core'}, dimensions={0}, use_global_device_ids=true | all-gather | bytes 49152 | tf_op jit(solution)/shard_map/all_gather | solution.py:137
  144.0 0.1 copy.31
  144.1 0.9 convolution_bitcast_fusion
  145.0 0.8 fusion.2
  (15 shorter events, 0.2 us)
Async XLA Ops:
  0.6 25.2 %copy-start = (bf16[512,896]{1,0:T(8,128)(2,1)S(1)}, bf16[512,896]{1,0:T(8,128)(2,1)}, u32[]{:S(2)}) copy-start(bf16[512,896]{1,0:T(8,128)(2,1)} %param.9) | copy-start | bytes 2752516
  0.6 24.0 %copy-start.4 = (bf16[2,512,64]{1,2,0:T(8,128)(2,1)S(1)}, bf16[2,512,64]{1,2,0:T(8,128)(2,1)}, u32[]{:S(2)}) copy-start(bf16[2,512,64]{1,2,0:T(8,128)(2,1)} %param.12) | copy-start | bytes 393220
  0.7 24.3 %copy-start.2 = (bf16[512,896]{1,0:T(8,128)(2,1)S(1)}, bf16[512,896]{1,0:T(8,128)(2,1)}, u32[]{:S(2)}) copy-start(bf16[512,896]{1,0:T(8,128)(2,1)} %param.10) | copy-start | bytes 2752516
  20.4 5.0 %copy-start.1 = (bf16[896,512]{1,0:T(8,128)(2,1)S(1)}, bf16[896,512]{1,0:T(8,128)(2,1)}, u32[]{:S(2)}) copy-start(bf16[896,512]{1,0:T(8,128)(2,1)} %param.11) | copy-start | bytes 2752516
  68.9 0.9 copy-start.3

commit v5 on v2

--- a/solution.py
+++ b/solution.py
@@ -51,29 +51,69 @@
     first = jnp.transpose(adapter_first_factors, (1, 0, 2)).reshape(width, columns)
     second = adapter_second_factors.reshape(columns, hidden_units)
 
+    both = jnp.concatenate([tokens, cotangent], axis=1)
+    both = lax.all_gather(gather_rows(both, PIPE_LINKS), "core", axis=0, tiled=True)
+    both, adapter_of_block = lax.optimization_barrier((both, adapter_of_block))
+    token_rows, adjoint_rows = both[:, :width], both[:, width:]
+
+    def hidden_parts(row_pair):
+        token_part, adjoint_part = row_pair[:, :width], row_pair[:, width:]
+        return [
+            product(token_part, gate_weight),
+            product(token_part, upward_weight),
+            trailing_product(adjoint_part, down_weight),
+            product(token_part, first),
+        ]
+
     own = jnp.arange(columns, dtype=jnp.int32) // rank
     masks = (own[None, :] == adapter_of_block[:, None]).astype(f32)
     own_mask = lax.dynamic_slice_in_dim(masks, lax.axis_index("x") % 2, 1, 0)
-    block_mask = lax.dynamic_slice_in_dim(masks, lax.axis_index("zlo"), 1, 0)
-    both = jnp.concatenate([tokens, cotangent], axis=1)
+    masks16 = masks.astype(bf16)
+    block_mask = lax.dynamic_slice_in_dim(masks16, lax.axis_index("zlo"), 1, 0)
     own_columns = lax.axis_index("y") * columns
-    masks16, block_mask = masks.astype(bf16), block_mask.astype(bf16)
-    both, masks, masks16, own_mask, block_mask, own_columns = lax.optimization_barrier(
-        (both, masks, masks16, own_mask, block_mask, own_columns)
-    )
-    both = lax.all_gather(gather_rows(both, PIPE_LINKS), "core", axis=0, tiled=True)
-    token_rows, adjoint_rows = both[:, :width], both[:, width:]
-
-    parts = jnp.concatenate(
-        [
-            product(token_rows, gate_weight).astype(bf16),
-            product(token_rows, upward_weight).astype(bf16),
-            trailing_product(adjoint_rows, down_weight).astype(bf16),
-            product(token_rows, first).astype(bf16),
-        ],
-        axis=1,
-    )
-    parts = scatter_sum(scatter_sum(parts, "x", bf16), "zhi", f32)
+    own_rows_z = lax.axis_index("zhi") * 16
+    fours = jnp.arange(4, dtype=jnp.int32)
+    peers_x = (fours != lax.axis_index("x")).astype(f32).reshape(4, 1, 1)
+    peers_z = (fours != lax.axis_index("zhi")).astype(f32).reshape(4, 1, 1)
+
+    sent = jnp.concatenate([part.astype(bf16) for part in hidden_parts(both)], axis=1)
+    own_both = lax.dynamic_slice(
+        both, (lax.axis_index("x") * 64, 0), (64, both.shape[1]), allow_negative_indices=False
+    )
+    own_parts = jnp.concatenate(hidden_parts(own_both), axis=1)
+    came = lax.all_to_all(sent.reshape(4, 64, -1), "x", 0, 0)
+    (
+        came,
+        own_parts,
+        masks,
+        masks16,
+        own_mask,
+        block_mask,
+        own_columns,
+        own_rows_z,
+        peers_x,
+        peers_z,
+    ) = lax.optimization_barrier(
+        (
+            came,
+            own_parts,
+            masks,
+            masks16,
+            own_mask,
+            block_mask,
+            own_columns,
+            own_rows_z,
+            peers_x,
+            peers_z,
+        )
+    )
+    parts = own_parts + jnp.sum(came.astype(f32) * peers_x, axis=0)
+    came = lax.all_to_all(parts.astype(bf16).reshape(4, 16, -1), "zhi", 0, 0)
+    came, parts = lax.optimization_barrier((came, parts))
+    own_parts = lax.dynamic_slice(
+        parts, (own_rows_z, 0), (16, parts.shape[1]), allow_negative_indices=False
+    )
+    parts = own_parts + jnp.sum(came.astype(f32) * peers_z, axis=0)
 
     gate = parts[:, :hidden_units]
     up_base = parts[:, hidden_units : 2 * hidden_units]

time: 150 us -> 145 us (0.967)
  blocking collectives: 136 us -> 88.4 us
  waiting for transfers between devices: 0 us -> 25 us
  starting transfers between devices: 0 us -> 14 us
    all_to_all x3 -> x1, blocking collectives: 58.8 us -> 9.85 us  [scatter_sum(): return jnp.sum(lax.all_to_all(blocks, axis, 0, 0).astype(f32), axis=0)]
    all_to_all x0 -> x2, waiting for transfers between devices: none -> 25 us  [the longest x1 16.3 us: on_device(): came = lax.all_to_all(sent.reshape(4, 64, -1), 'x', 0, 0)]
    all_to_all x0 -> x1, blocking collectives: none -> 18.8 us  [on_device(): came = lax.all_to_all(parts.astype(bf16).reshape(4, 16, -1), 'zhi', 0, 0)]
    all_to_all x3 -> x2, blocking collectives: 46.5 us -> 31.3 us  [gather_rows(): lax.all_to_all(blocks, axis, 0, 0)]
    all_to_all x0 -> x2, starting transfers between devices: none -> 14 us  [the longest x1 9.56 us: gather_rows(): lax.all_to_all(blocks, axis, 0, 0)]
    all_to_all x1, blocking collectives: 22.4 us -> 20 us  [on_device(): summed = jnp.sum(lax.all_to_all(sent, PIPE_LINKS, 0, 0).astype(f32), axis=0)]
    reduce_sum x3 -> x1, other arithmetic: 2.15 us -> 0.12 us  [scatter_sum(): return jnp.sum(lax.all_to_all(blocks, axis, 0, 0).astype(f32), axis=0)]
    reduce_sum x0 -> x2, other arithmetic: none -> 2 us  [the longest x1 1.87 us: on_device(): parts = own_parts + jnp.sum(came.astype(f32) * peers_x, axis=0)]
  transfers between devices with their start and end apart: 0 -> 2, of which waited for: 0 -> 2; matrix products, arithmetic and copies ran while one was open for 0% -> 2% of each run, Pallas kernels for 0% -> 0%
where the time goes in v5:
time: 145 us; the launch traced here: 144 us
  blocking collectives  88.4 us (61%)
  waiting for transfers between devices  25 us (17%)
  starting transfers between devices  14 us (10%)
  matrix products  8.17 us (6%)
  other arithmetic  5.52 us (4%)
  local copies, waits for them, and re-layouts  2.11 us (1%)
    all_to_all x2, blocking collectives, gather_rows(): lax.all_to_all(blocks, axis, 0, 0)  31.3 us
    all_to_all x1, blocking collectives, on_device(): summed = jnp.sum(lax.all_to_all(sent, PIPE_LINKS, 0, 0).astype(f32), axis=0)  20 us
    all_to_all x1, blocking collectives, on_device(): came = lax.all_to_all(parts.astype(bf16).reshape(4, 16, -1), 'zhi', 0, 0)  18.8 us
    all_to_all x1, waiting for transfers between devices, on_device(): came = lax.all_to_all(sent.reshape(4, 64, -1), 'x', 0, 0)  16.3 us
    all_to_all x1, blocking collectives, scatter_sum(): return jnp.sum(lax.all_to_all(blocks, axis, 0, 0).astype(f32), axis=0)  9.85 us
    all_to_all x1, starting transfers between devices, gather_rows(): lax.all_to_all(blocks, axis, 0, 0)  9.56 us
    all_to_all x1, waiting for transfers between devices, gather_rows(): lax.all_to_all(blocks, axis, 0, 0)  8.68 us
    all_to_all x1, starting transfers between devices, on_device(): came = lax.all_to_all(sent.reshape(4, 64, -1), 'x', 0, 0)  4.46 us
  transfers between devices with their start and end apart: 2, of which 2 were waited for; matrix products, arithmetic and copies ran while one was open for 2% of the time, Pallas kernels for 0%

profile of v5, /device:TPU:1, one launch (start us, length us, event | category | flops | bytes accessed | tf_op | source)
XLA Modules:
  0.0 144.2 jit_solution(11126349903575454669)
XLA Ops:
  0.6 0.0 copy-start
  0.6 0.0 copy-start.4
  0.7 0.0 copy-start.2
  0.7 0.9 pad_maximum_fusion.5
  1.5 0.7 broadcast_in_dim.14
  2.3 9.6 %all-to-all-start = ((bf16[16,8,1024]{2,1,0:T(8,128)(2,1)}), bf16[16,8,1024]{2,1,0:T(8,128)(2,1)S(1)}, u32[]{:S(2)}, u32[]{:S(2)}) async-start(bf16[16,8,1024]{2,1,0:T(8,128)(2,1)} %broadcast_in_dim.14), calls=%async_computation | async-start | bytes 524288 | tf_op jit(solution)/shard_map/all_to_all | solution.py:29
  11.9 8.7 %all-to-all-done = bf16[16,8,1024]{2,1,0:T(8,128)(2,1)S(1)} async-done(((bf16[16,8,1024]{2,1,0:T(8,128)(2,1)}), bf16[16,8,1024]{2,1,0:T(8,128)(2,1)S(1)}, u32[]{:S(2)}, u32[]{:S(2)}) %all-to-all-start) | async-done | bytes 262176 | tf_op jit(solution)/shard_map/all_to_all | solution.py:29
  20.6 4.1 %all_gather.6 = bf16[256,1024]{1,0:T(8,128)(2,1)S(1)} all-gather(bf16[128,1024]{1,0:T(8,128)(2,1)S(1)} %bitcast.64), channel_id=1, replica_groups=mesh['zlo'=2,'y'=8,'core'=2,'zhi'=4,'x'=4] {'core'}, dimensions={0}, use_global_device_ids=true | all-gather | bytes 786432 | tf_op jit(solution)/shard_map/all_gather | solution.py:55
  24.7 0.0 copy-done.4
  24.7 0.2 convolution_convert_fusion.3
  24.9 0.0 copy-done.2
  24.9 0.0 copy-start.1
  24.9 0.4 convolution_convert_fusion.1
  25.4 0.3 fusion.23
  25.7 0.4 copy-done.1
  26.1 0.5 convolution_convert_fusion
  26.6 0.0 copy-done
  26.6 0.4 convolution_convert_fusion.2
  27.0 1.2 pad_maximum_fusion
  28.2 0.0 copy-start.7
  28.2 4.5 %all-to-all-start.1 = ((bf16[4,64,2816]{2,1,0:T(8,128)(2,1)}), bf16[4,64,2816]{2,1,0:T(8,128)(2,1)}, u32[]{:S(2)}, u32[]{:S(2)}) async-start(bf16[4,64,2816]{2,1,0:T(8,128)(2,1)} %bitcast.60), calls=%async_computation.1 | async-start | bytes 2883584 | tf_op jit(solution)/shard_map/all_to_all | solution.py:84
  32.7 0.0 copy-done.7
  32.7 0.1 fusion.37
  32.8 1.1 fusion.21
  33.9 0.3 fusion.25
  34.2 0.4 fusion.18
  34.6 0.9 pad_maximum_fusion.2
  35.5 16.3 %all-to-all-done.1 = bf16[4,64,2816]{2,1,0:T(8,128)(2,1)} async-done(((bf16[4,64,2816]{2,1,0:T(8,128)(2,1)}), bf16[4,64,2816]{2,1,0:T(8,128)(2,1)}, u32[]{:S(2)}, u32[]{:S(2)}) %all-to-all-start.1) | async-done | bytes 1441824 | tf_op jit(solution)/shard_map/all_to_all | solution.py:84
  51.8 0.0 copy-start.3
  51.8 1.9 %multiply_reduce_fusion = f32[64,2816]{1,0:T(8,128)S(1)} fusion(bf16[4,64,2816]{2,1,0:T(8,128)(2,1)} %all-to-all-done.1, f32[4]{0:T(128)S(1)} %bitcast.75), kind=kLoop, calls=%fused_computation | loop fusion | flops 1982464 | bytes 2162704 | tf_op jit(solution)/shard_map/reduce_sum | solution.py:110
  53.7 0.0 copy-done.3
  53.7 0.1 fusion.38
  53.8 0.0 copy-start.6
  53.8 18.8 %all_to_all.35 = bf16[4,16,2816]{2,1,0:T(8,128)(2,1)S(1)} all-to-all(bf16[4,16,2816]{2,1,0:T(8,128)(2,1)S(1)} %bitcast.62), channel_id=1, replica_groups=mesh['zlo'=2,'y'=8,'core'=2,'zhi'=4,'x'=4] {'zhi'}, dimensions={0} | all-to-all | bytes 720896 | tf_op jit(solution)/shard_map/all_to_all | solution.py:111
  72.6 0.1 multiply_reduce_fusion.1
  72.8 0.0 copy-done.6
  72.8 0.2 multiply_convert_fusion.2
  73.0 14.2 %all_to_all.36 = bf16[4,16,2816]{2,1,0:T(8,128)(2,1)S(1)} all-to-all(bf16[4,16,2816]{2,1,0:T(8,128)(2,1)S(1)} %broadcast_in_dim.15), channel_id=1, replica_groups=mesh['zlo'=2,'y'=8,'core'=2,'zhi'=4,'x'=4] {'zhi'}, dimensions={0} | all-to-all | bytes 720896 | tf_op jit(solution)/shard_map/all_to_all | solution.py:29
  87.2 0.1 broadcast_in_dim.17
  87.3 17.2 %all_to_all.37 = bf16[4,64,2816]{2,1,0:T(8,128)(2,1)S(1)} all-to-all(bf16[4,64,2816]{2,1,0:T(8,128)(2,1)S(1)} %broadcast_in_dim.17), channel_id=1, replica_groups=mesh['zlo'=2,'y'=8,'core'=2,'zhi'=4,'x'=4] {'x'}, dimensions={0} | all-to-all | bytes 2883584 | tf_op jit(solution)/shard_map/all_to_all | solution.py:29
  104.4 1.0 convolution_multiply_fusion
  105.5 0.5 fusion.3
  105.9 0.4 fusion.5
  106.4 0.3 fusion
  106.7 0.5 convolution_add_fusion
  107.2 0.1 pad_maximum_fusion.1
  107.2 9.9 %all_to_all.38 = f32[2,128,1152]{2,1,0:T(8,128)S(1)} all-to-all(f32[2,128,1152]{2,1,0:T(8,128)S(1)} %bitcast.61), channel_id=1, replica_groups=mesh['zlo'=2,'y'=8,'core'=2,'zhi'=4,'x'=4] {'core'}, dimensions={0} | all-to-all | bytes 2359296 | tf_op jit(solution)/shard_map/all_to_all | solution.py:35
  117.1 0.1 reduce_sum.38
  117.3 0.0 copy-start.5
  117.4 20.0 %all_to_all.39 = bf16[16,8,2048]{2,1,0:T(8,128)(2,1)S(1)} all-to-all(bf16[16,8,2048]{2,1,0:T(8,128)(2,1)S(1)} %pad_maximum_fusion.3), channel_id=1, replica_groups=mesh['zlo'=2,'y'=8,'core'=2,'zhi'=4,'x'=4] {'zlo','y'}, dimensions={0} | all-to-all | bytes 1048576 | tf_op jit(solution)/shard_map/all_to_all | solution.py:165
  137.4 0.1 convert_reduce_fusion
  137.5 0.6 slice.87
  138.1 4.3 %all_gather.7 = bf16[2,64,128]{2,1,0:T(8,128)(2,1)S(1)} all-gather(bf16[1,64,128]{2,1,0:T(8,128)(2,1)S(1)} %get-tuple-element.41), channel_id=1, replica_groups=mesh['zlo'=2,'y'=8,'core'=2,'zhi'=4,'x'=4] {'core'}, dimensions={0}, use_global_device_ids=true | all-gather | bytes 49152 | tf_op jit(solution)/shard_map/all_gather | solution.py:175
  142.4 0.1 copy.27
  142.5 0.9 convolution_bitcast_fusion
  143.4 0.0 copy-done.5
  143.4 0.8 fusion.2
  (16 shorter events, 0.2 us)
Async XLA Ops:
  0.6 26.0 %copy-start = (bf16[512,896]{1,0:T(8,128)(2,1)S(1)}, bf16[512,896]{1,0:T(8,128)(2,1)}, u32[]{:S(2)}) copy-start(bf16[512,896]{1,0:T(8,128)(2,1)} %param.9) | copy-start | bytes 2752516
  0.6 24.0 %copy-start.4 = (bf16[2,512,64]{1,2,0:T(8,128)(2,1)S(1)}, bf16[2,512,64]{1,2,0:T(8,128)(2,1)}, u32[]{:S(2)}) copy-start(bf16[2,512,64]{1,2,0:T(8,128)(2,1)} %param.12) | copy-start | bytes 393220
  0.7 24.3 %copy-start.2 = (bf16[512,896]{1,0:T(8,128)(2,1)S(1)}, bf16[512,896]{1,0:T(8,128)(2,1)}, u32[]{:S(2)}) copy-start(bf16[512,896]{1,0:T(8,128)(2,1)} %param.10) | copy-start | bytes 2752516
  2.3 18.3 %all-to-all-start = ((bf16[16,8,1024]{2,1,0:T(8,128)(2,1)}), bf16[16,8,1024]{2,1,0:T(8,128)(2,1)S(1)}, u32[]{:S(2)}, u32[]{:S(2)}) async-start(bf16[16,8,1024]{2,1,0:T(8,128)(2,1)} %broadcast_in_dim.14), calls=%async_computation | async-start | bytes 524288 | tf_op jit(solution)/shard_map/all_to_all | solution.py:29
  24.9 1.2 copy-start.1
  28.2 4.5 %copy-start.7 = (s32[2]{0:T(128)S(1)}, s32[2]{0:T(128)}, u32[]{:S(2)}) copy-start(s32[2]{0:T(128)} %param.14) | copy-start | bytes 28
  28.2 23.6 %all-to-all-start.1 = ((bf16[4,64,2816]{2,1,0:T(8,128)(2,1)}), bf16[4,64,2816]{2,1,0:T(8,128)(2,1)}, u32[]{:S(2)}, u32[]{:S(2)}) async-start(bf16[4,64,2816]{2,1,0:T(8,128)(2,1)} %bitcast.60), calls=%async_computation.1 | async-start | bytes 2883584 | tf_op jit(solution)/shard_map/all_to_all | solution.py:84
  51.8 1.9 %copy-start.3 = (f32[64,2816]{1,0:T(8,128)S(1)}, f32[64,2816]{1,0:T(8,128)}, u32[]{:S(2)}) copy-start(f32[64,2816]{1,0:T(8,128)} %pad_maximum_fusion.2) | copy-start | bytes 2162692
  53.8 19.0 %copy-start.6 = (bf16[2,64,896]{2,1,0:T(8,128)(2,1)S(1)}, bf16[2,64,896]{2,1,0:T(8,128)(2,1)}, u32[]{:S(2)}) copy-start(bf16[2,64,896]{2,1,0:T(8,128)(2,1)} %param.13) | copy-start | bytes 688132
  117.3 26.0 %copy-start.5 = (bf16[2,512,64]{1,2,0:T(8,128)(2,1)S(1)}, bf16[2,512,64]{1,2,0:T(8,128)(2,1)}, u32[]{:S(2)}) copy-start(bf16[2,512,64]{1,2,0:T(8,128)(2,1)} %param.12) | copy-start | bytes 393220

commit v6 on v1

v6 whole, which is shorter than its diff:
```python
import jax
import jax.numpy as jnp
import numpy as np
from jax import lax
from jax.sharding import Mesh, PartitionSpec as P

PIPE = ("zlo", "y", "core")
TENSOR = ("zhi", "x")
PIPE_LINKS = ("zlo", "y")
adapter_scale = 0.5
bf16 = jnp.bfloat16
f32 = jnp.float32


def product(left, right):
    return jnp.dot(left, right, preferred_element_type=f32)


def trailing_product(left, right):
    return lax.dot_general(left, right, (((1,), (1,)), ((), ())), preferred_element_type=f32)


def leading_product(left, right):
    return lax.dot_general(left, right, (((0,), (0,)), ((), ())), preferred_element_type=f32)


def gather_rows(value, axis):
    count = lax.axis_size(axis)
    blocks = jnp.broadcast_to(value[None], (count,) + value.shape)
    return lax.all_to_all(blocks, axis, 0, 0).reshape((count * value.shape[0],) + value.shape[1:])


def own_block(value, first_row, rows):
    return lax.dynamic_slice(
        value, (first_row, 0), (rows, value.shape[1]), allow_negative_indices=False
    )


def fence(*values):
    return lax.optimization_barrier(values)


def on_device(
    tokens,
    gate_weight,
    upward_weight,
    down_weight,
    adapter_first_factors,
    adapter_second_factors,
    adapter_of_block,
    cotangent,
):
    adapters, width, rank = adapter_first_factors.shape
    hidden_units = gate_weight.shape[1]
    columns = adapters * rank
    first = jnp.transpose(adapter_first_factors, (1, 0, 2)).reshape(width, columns)
    second = adapter_second_factors.reshape(columns, hidden_units)

    tokens, cotangent, *place = fence(
        tokens, cotangent, *(lax.axis_index(name) for name in ("core", "zhi", "x"))
    )
    both = jnp.concatenate([tokens, cotangent], axis=1)
    both = lax.all_gather(gather_rows(both, PIPE_LINKS), "core", axis=0, tiled=True)
    both, adapter_of_block, core, zhi, x = fence(both, adapter_of_block, *place)
    token_rows, adjoint_rows = both[:, :width], both[:, width:]

    own = np.arange(columns, dtype=np.int32) // rank
    masks = (own[None, :] == adapter_of_block[:, None]).astype(f32)
    own_mask = lax.dynamic_slice(masks, (x % 2, 0), (1, columns), allow_negative_indices=False)
    all_masks = jnp.broadcast_to(masks[None, :, None, :], (2, 2, 64, columns)).reshape(
        256, columns
    )
    fours = np.arange(4, dtype=np.int32)
    peers_x = (fours != x).astype(f32).reshape(4, 1, 1)
    peers_z = (fours != zhi).astype(f32).reshape(4, 1, 1)
    own_z, own_core, other_core = zhi * 16, core * 128, (1 - core) * 128
    core_is = jnp.stack([core == 0, core == 1]).astype(bf16).reshape(2, 1, 1)

    def hidden_parts(row_pair):
        token_part, adjoint_part = row_pair[:, :width], row_pair[:, width:]
        return [
            product(token_part, gate_weight),
            product(token_part, upward_weight),
            trailing_product(adjoint_part, down_weight),
            product(token_part, first),
        ]

    sent = jnp.concatenate([part.astype(bf16) for part in hidden_parts(both)], axis=1)
    parts = jnp.concatenate(hidden_parts(own_block(both, x * 64, 64)), axis=1)
    sent, parts, all_masks, own_mask, peers_x, peers_z, own_z, own_core, other_core, core_is = fence(
        sent, parts, all_masks, own_mask, peers_x, peers_z, own_z, own_core, other_core, core_is
    )
    came = lax.all_to_all(sent.reshape(4, 64, -1), "x", 0, 0)
    parts = parts + jnp.sum(came.astype(f32) * peers_x, axis=0)
    came = lax.all_to_all(parts.astype(bf16).reshape(4, 16, -1), "zhi", 0, 0)
    came, parts = fence(came, parts)
    parts = own_block(parts, own_z, 16) + jnp.sum(came.astype(f32) * peers_z, axis=0)

    gate = parts[:, :hidden_units]
    up_base = parts[:, hidden_units : 2 * hidden_units]
    grad_hidden = parts[:, 2 * hidden_units : 3 * hidden_units]
    low = (parts[:, 3 * hidden_units :] * own_mask).astype(bf16)
    up = up_base + adapter_scale * product(low, second)
    sig = jax.nn.sigmoid(gate)
    act = gate * sig
    hidden = (act * up).astype(bf16)
    grad_up = (grad_hidden * act).astype(bf16)
    grad_gate = (grad_hidden * up * sig * (1.0 + gate * (1.0 - sig))).astype(bf16)

    rows = jnp.concatenate([hidden, grad_gate, grad_up, low], axis=1)
    rows = gather_rows(gather_rows(rows, "zhi"), "x")
    grad_up_all = rows[:, 2 * hidden_units : 3 * hidden_units]
    low_parts = adapter_scale * trailing_product(grad_up_all, second) * all_masks
    low_parts = jnp.sum(lax.all_gather(low_parts, "core", axis=0), axis=0).astype(bf16)
    low_parts = jnp.transpose(low_parts.reshape(2, 16, 8, columns), (1, 0, 2, 3))
    low_parts, rows = fence(low_parts.reshape(16, 16, columns), rows)
    low_parts = lax.all_to_all(low_parts, PIPE_LINKS, 0, 0)

    hidden_all = rows[:, :hidden_units]
    grad_gate_all = rows[:, hidden_units : 2 * hidden_units]
    grad_up_all = rows[:, 2 * hidden_units : 3 * hidden_units]
    low_all = rows[:, 3 * hidden_units :]
    partial = jnp.concatenate(
        [
            product(hidden_all, down_weight),
            trailing_product(grad_gate_all, gate_weight)
            + trailing_product(grad_up_all, upward_weight),
        ],
        axis=1,
    )
    grad_b = (adapter_scale * leading_product(low_all, grad_up_all)).reshape(
        adapters, rank, hidden_units
    )
    swap = [(0, 1), (1, 0)]
    partial = own_block(partial, own_core, 128) + lax.ppermute(
        own_block(partial, other_core, 128), "core", swap
    )
    low_parts, partial, grad_b = fence(low_parts, partial.astype(bf16), grad_b)

    low_mine = jnp.sum(low_parts.astype(f32), axis=0).astype(bf16)
    low_own = jnp.sum(low_mine.reshape(2, 8, columns) * core_is, axis=0)
    wide = jnp.concatenate([low_mine[:8], low_mine[8:]], axis=1)
    sent = jnp.concatenate(
        [partial.reshape(16, 8, -1), jnp.broadcast_to(wide[None], (16,) + wide.shape)], axis=2
    )
    sent, low_own = fence(sent, low_own)
    came = lax.all_to_all(sent, PIPE_LINKS, 0, 0)
    came, low_own = fence(came, low_own)
    summed = jnp.sum(came[:, :, : 2 * width].astype(f32), axis=0)
    mixed = summed[:, :width].astype(bf16)
    grad_tokens = (summed[:, width:] + trailing_product(low_own, first)).astype(bf16)
    low_back = jnp.concatenate(
        [
            came[:, :, 2 * width : 2 * width + columns].reshape(128, columns),
            came[:, :, 2 * width + columns :].reshape(128, columns),
        ],
        axis=0,
    )
    grad_a = leading_product(token_rows, low_back).reshape(width, adapters, rank)
    return mixed, grad_tokens, jnp.transpose(grad_a, (1, 0, 2)), grad_b


def solution(mesh):
    parts = Mesh(mesh.devices.reshape(2, 8, 2, 4, 4), PIPE + TENSOR)
    in_specs = (
        P(PIPE, TENSOR),
        P(TENSOR, PIPE),
        P(TENSOR, PIPE),
        P(PIPE, TENSOR),
        P(None, TENSOR, None),
        P(None, None, PIPE),
        P(),
        P(PIPE, TENSOR),
    )
    out_specs = (
        P(PIPE, TENSOR),
        P(PIPE, TENSOR),
        P(None, TENSOR, None),
        P(None, None, PIPE),
    )
    return jax.shard_map(
        on_device, mesh=parts, in_specs=in_specs, out_specs=out_specs, check_vma=False
    )
```

time: 159 us -> 150 us (0.943); the launches traced: 158 us -> 147 us
  waiting for transfers between devices: 39.3 us -> 13.9 us
  blocking collectives: 76.4 us -> 95.1 us
  starting transfers between devices: 26.6 us -> 17.1 us
  matrix products: 6.08 us -> 10.2 us
    all_to_all x2 -> x3, blocking collectives: 35.2 us -> 52 us  [the longest x1 22.3 us: on_device(): came = lax.all_to_all(sent.reshape(4, 64, -1), 'x', 0, 0)]
    all_to_all x2 -> x1, waiting for transfers between devices: 20.9 us -> 5.17 us  [on_device(): low_parts = lax.all_to_all(low_parts, PIPE_LINKS, 0, 0)]
    all_to_all x2 -> x1, starting transfers between devices: 17.6 us -> 5.11 us  [on_device(): low_parts = lax.all_to_all(low_parts, PIPE_LINKS, 0, 0)]
    all_to_all x2 -> x1, waiting for transfers between devices: 18.4 us -> 8.73 us  [gather_rows(): lax.all_to_all(blocks, axis, 0, 0)]
    all_gather x1, blocking collectives: 3.8 us -> 7.7 us  [on_device(): lax.all_gather(low_parts, 'core', axis=0)]
    dot_general x5 -> x8, matrix products: 1.69 us -> 4.61 us  [product(): return jnp.dot(left, right, preferred_element_type=f32)]
    reduce_sum x6, other arithmetic: 4 us -> 1.28 us  [the longest x1 0.64 us: on_device(): jnp.sum(lax.all_gather(low_parts, 'core', axis=0), axis=0).astype(bf16)]
    ppermute x0 -> x1, starting transfers between devices: none -> 2.39 us  [on_device(): lax.ppermute(own_block(partial, other_core, 128), 'core', swap)]
  transfers between devices with their start and end apart: 4 -> 3, of which waited for: 4 -> 2; matrix products, arithmetic and copies ran while one was open for 2% -> 1% of each run, Pallas kernels for 0% -> 0%
where the time goes in v6:
time: 150 us; the launch traced here: 147 us
  blocking collectives  95.1 us (63%)
  starting transfers between devices  17.1 us (11%)
  waiting for transfers between devices  13.9 us (9%)
  matrix products  10.2 us (7%)
  other arithmetic  5.88 us (4%)
  local copies, waits for them, and re-layouts  4.08 us (3%)
    all_to_all x2, blocking collectives, gather_rows(): lax.all_to_all(blocks, axis, 0, 0)  31.3 us
    all_to_all x1, blocking collectives, on_device(): came = lax.all_to_all(sent.reshape(4, 64, -1), 'x', 0, 0)  22.3 us
    all_to_all x1, blocking collectives, on_device(): came = lax.all_to_all(parts.astype(bf16).reshape(4, 16, -1), 'zhi', 0, 0)  18.2 us
    all_to_all x1, blocking collectives, on_device(): came = lax.all_to_all(sent, PIPE_LINKS, 0, 0)  11.6 us
    all_to_all x1, starting transfers between devices, gather_rows(): lax.all_to_all(blocks, axis, 0, 0)  9.56 us
    all_to_all x1, waiting for transfers between devices, gather_rows(): lax.all_to_all(blocks, axis, 0, 0)  8.73 us
    all_gather x1, blocking collectives, on_device(): lax.all_gather(low_parts, 'core', axis=0)  7.7 us
    all_to_all x1, waiting for transfers between devices, on_device(): low_parts = lax.all_to_all(low_parts, PIPE_LINKS, 0, 0)  5.17 us
  transfers between devices with their start and end apart: 3, of which 2 were waited for; matrix products, arithmetic and copies ran while one was open for 1% of the time, Pallas kernels for 0%

profile of v6, /device:TPU:1, one launch (start us, length us, event | category | flops | bytes accessed | tf_op | source)
XLA Modules:
  0.0 147.2 jit_solution(10595246210997093355)
XLA Ops:
  0.6 0.0 copy-start
  0.6 0.0 copy-start.9
  0.7 0.0 copy-start.2
  0.7 0.9 pad_maximum_fusion.4
  1.5 0.7 broadcast_in_dim.12
  2.3 9.6 %all-to-all-start = ((bf16[16,8,1024]{2,1,0:T(8,128)(2,1)}), bf16[16,8,1024]{2,1,0:T(8,128)(2,1)S(1)}, u32[]{:S(2)}, u32[]{:S(2)}) async-start(bf16[16,8,1024]{2,1,0:T(8,128)(2,1)} %broadcast_in_dim.12), calls=%async_computation | async-start | bytes 524288 | tf_op jit(solution)/shard_map/all_to_all | solution.py:30
  11.8 8.7 %all-to-all-done = bf16[16,8,1024]{2,1,0:T(8,128)(2,1)S(1)} async-done(((bf16[16,8,1024]{2,1,0:T(8,128)(2,1)}), bf16[16,8,1024]{2,1,0:T(8,128)(2,1)S(1)}, u32[]{:S(2)}, u32[]{:S(2)}) %all-to-all-start) | async-done | bytes 262176 | tf_op jit(solution)/shard_map/all_to_all | solution.py:30
  20.6 4.1 %all_gather.9 = bf16[256,1024]{1,0:T(8,128)(2,1)S(1)} all-gather(bf16[128,1024]{1,0:T(8,128)(2,1)S(1)} %bitcast.64), channel_id=1, replica_groups=mesh['zlo'=2,'y'=8,'core'=2,'zhi'=4,'x'=4] {'core'}, dimensions={0}, use_global_device_ids=true | all-gather | bytes 786432 | tf_op jit(solution)/shard_map/all_gather | solution.py:63
  24.7 0.0 copy-done.9
  24.7 0.9 convolution_convert_fusion.3
  25.6 0.2 fusion.27
  25.7 0.0 copy-done.2
  25.7 0.0 copy-start.1
  25.7 0.3 fusion.29
  26.0 1.2 convolution_convert_fusion.1
  27.3 0.0 copy-done.1
  27.3 0.3 fusion.31
  27.6 1.2 convolution_convert_fusion.2
  28.8 0.0 copy-done
  28.8 1.2 convolution_convert_fusion
  30.0 0.0 copy-done.4
  30.0 0.4 fusion.20
  30.5 0.0 copy-start.8
  30.5 0.1 add_convert_fusion
  30.6 0.0 copy-done.12
  30.6 0.0 copy-done.13
  30.6 0.1 compare_convert_fusion.2
  30.7 0.8 copy-done.8
  31.5 1.3 pad_maximum_fusion
  32.8 22.3 %all_to_all.35 = bf16[4,64,2816]{2,1,0:T(8,128)(2,1)S(1)} all-to-all(bf16[4,64,2816]{2,1,0:T(8,128)(2,1)S(1)} %bitcast.61), channel_id=1, replica_groups=mesh['zlo'=2,'y'=8,'core'=2,'zhi'=4,'x'=4] {'x'}, dimensions={0} | all-to-all | bytes 2883584 | tf_op jit(solution)/shard_map/all_to_all | solution.py:93
  55.1 0.4 multiply_reduce_fusion
  55.4 0.1 fusion.41
  55.6 18.2 %all_to_all.36 = bf16[4,16,2816]{2,1,0:T(8,128)(2,1)S(1)} all-to-all(bf16[4,16,2816]{2,1,0:T(8,128)(2,1)S(1)} %bitcast.62), channel_id=1, replica_groups=mesh['zlo'=2,'y'=8,'core'=2,'zhi'=4,'x'=4] {'zhi'}, dimensions={0} | all-to-all | bytes 720896 | tf_op jit(solution)/shard_map/all_to_all | solution.py:95
  73.8 0.1 multiply_reduce_fusion.1
  74.0 0.0 copy-done.11
  74.0 0.2 multiply_convert_fusion.2
  74.2 14.6 %all_to_all.37 = bf16[4,16,2816]{2,1,0:T(8,128)(2,1)S(1)} all-to-all(bf16[4,16,2816]{2,1,0:T(8,128)(2,1)S(1)} %broadcast_in_dim.14), channel_id=1, replica_groups=mesh['zlo'=2,'y'=8,'core'=2,'zhi'=4,'x'=4] {'zhi'}, dimensions={0} | all-to-all | bytes 720896 | tf_op jit(solution)/shard_map/all_to_all | solution.py:30
  88.8 0.1 broadcast_in_dim.16
  88.9 16.6 %all_to_all.38 = bf16[4,64,2816]{2,1,0:T(8,128)(2,1)S(1)} all-to-all(bf16[4,64,2816]{2,1,0:T(8,128)(2,1)S(1)} %broadcast_in_dim.16), channel_id=1, replica_groups=mesh['zlo'=2,'y'=8,'core'=2,'zhi'=4,'x'=4] {'x'}, dimensions={0} | all-to-all | bytes 2883584 | tf_op jit(solution)/shard_map/all_to_all | solution.py:30
  105.6 0.3 fusion
  105.9 7.7 %all-gather = f32[512,128]{1,0:T(8,128)S(1)} all-gather(f32[256,128]{1,0:T(8,128)S(1)} %fusion), channel_id=2, replica_groups=mesh['zlo'=2,'y'=8,'core'=2,'zhi'=4,'x'=4] {'core'}, dimensions={0}, use_global_device_ids=true | all-gather | bytes 393216 | tf_op jit(solution)/shard_map/all_gather | solution.py:114
  113.6 0.6 reduce_sum.62
  114.2 1.5 %copy.20 = bf16[16,2,8,128]{3,2,1,0:T(8,128)(2,1)} copy(bf16[16,2,8,128]{3,2,0,1:T(8,128)(2,1)} %bitcast.72) | data formatting | bytes 131072 | tf_op jit(solution)/shard_map/transpose | solution.py:115
  115.7 0.4 fusion.10
  116.1 0.0 copy-start.6
  116.1 0.5 fusion.8
  116.6 0.3 copy-done.3
  116.9 0.5 convolution_add_fusion
  117.3 0.0 copy-done.6
  117.4 0.9 fusion.3
  118.2 2.4 %collective-permute-start = (f32[128,1024]{1,0:T(8,128)}, f32[128,1024]{1,0:T(8,128)}, u32[]{:S(2)}, u32[]{:S(2)}) collective-permute-start(f32[128,1024]{1,0:T(8,128)} %fusion.3), channel_id=1, source_target_pairs={{0,16},{16,0},{1,17},{17,1},{2,18},{18,2},{3,19},{19,3},{4,20},{20... | collective-permute-start | bytes 1572872 | tf_op jit(solution)/shard_map/ppermute | solution.py:135
  120.6 5.1 %all-to-all-start.5 = ((bf16[16,16,128]{2,1,0:T(8,128)(2,1)}), bf16[16,16,128]{2,1,0:T(8,128)(2,1)S(1)}, u32[]{:S(2)}, u32[]{:S(2)}) async-start(bf16[16,16,128]{2,1,0:T(8,128)(2,1)} %bitcast.55), calls=%async_computation.5 | async-start | bytes 131072 | tf_op jit(solution)/shard_map/all_to_all | solution.py:117
  125.7 1.0 convolution_multiply_fusion
  126.8 0.0 collective-permute-done
  126.8 0.0 copy-done.7
  126.8 1.2 fusion.6
  127.9 0.0 copy-start.5
  128.0 5.2 %all-to-all-done.5 = bf16[16,16,128]{2,1,0:T(8,128)(2,1)S(1)} async-done(((bf16[16,16,128]{2,1,0:T(8,128)(2,1)}), bf16[16,16,128]{2,1,0:T(8,128)(2,1)S(1)}, u32[]{:S(2)}, u32[]{:S(2)}) %all-to-all-start.5) | async-done | bytes 65568 | tf_op jit(solution)/shard_map/all_to_all | solution.py:117
  133.2 0.1 fusion.34
  133.3 11.6 %all_to_all.39 = bf16[16,8,1280]{2,1,0:T(8,128)(2,1)S(1)} all-to-all(bf16[16,8,1280]{2,1,0:T(8,128)(2,1)S(1)} %pad_maximum_fusion.2), channel_id=1, replica_groups=mesh['zlo'=2,'y'=8,'core'=2,'zhi'=4,'x'=4] {'zlo','y'}, dimensions={0} | all-to-all | bytes 655360 | tf_op jit(solution)/shard_map/all_to_all | solution.py:147
  144.9 0.6 slice.130
  145.5 0.0 copy-done.10
  145.5 0.7 fusion.2
  146.2 0.9 fusion.15
  (23 shorter events, 0.3 us)
Async XLA Ops:
  0.6 28.2 %copy-start = (bf16[896,512]{1,0:T(8,128)(2,1)S(1)}, bf16[896,512]{1,0:T(8,128)(2,1)}, u32[]{:S(2)}) copy-start(bf16[896,512]{1,0:T(8,128)(2,1)} %param.13) | copy-start | bytes 2752516
  0.6 24.1 %copy-start.9 = (bf16[2,512,64]{1,2,0:T(8,128)(2,1)S(1)}, bf16[2,512,64]{1,2,0:T(8,128)(2,1)}, u32[]{:S(2)}) copy-start(bf16[2,512,64]{1,2,0:T(8,128)(2,1)} %param.14) | copy-start | bytes 393220
  0.7 25.1 %copy-start.2 = (bf16[512,896]{1,0:T(8,128)(2,1)S(1)}, bf16[512,896]{1,0:T(8,128)(2,1)}, u32[]{:S(2)}) copy-start(bf16[512,896]{1,0:T(8,128)(2,1)} %param.12) | copy-start | bytes 2752516
  2.3 18.3 %all-to-all-start = ((bf16[16,8,1024]{2,1,0:T(8,128)(2,1)}), bf16[16,8,1024]{2,1,0:T(8,128)(2,1)S(1)}, u32[]{:S(2)}, u32[]{:S(2)}) async-start(bf16[16,8,1024]{2,1,0:T(8,128)(2,1)} %broadcast_in_dim.12), calls=%async_computation | async-start | bytes 524288 | tf_op jit(solution)/shard_map/all_to_all | solution.py:30
  24.7 5.3 %copy-start.4 = (bf16[256,1024]{1,0:T(8,128)(2,1)}, bf16[256,1024]{1,0:T(8,128)(2,1)S(1)}, u32[]{:S(2)}) copy-start(bf16[256,1024]{1,0:T(8,128)(2,1)S(1)} %all_gather.9) | copy-start | bytes 1572868
  25.7 1.5 %copy-start.1 = (bf16[512,896]{1,0:T(8,128)(2,1)S(1)}, bf16[512,896]{1,0:T(8,128)(2,1)}, u32[]{:S(2)}) copy-start(bf16[512,896]{1,0:T(8,128)(2,1)} %param.11) | copy-start | bytes 2752516
  28.8 1.8 %copy-start.12 = (s32[2]{0:T(128)S(1)}, s32[2]{0:T(128)}, u32[]{:S(2)}) copy-start(s32[2]{0:T(128)} %param.16) | copy-start | bytes 28
  28.8 1.8 %copy-start.13 = (s32[128]{0:T(128)S(1)}, s32[128]{0:T(128)}, u32[]{:S(2)}) copy-start(s32[128]{0:T(128)} %constant.52) | copy-start | bytes 1540
  30.5 1.0 copy-start.8
  55.6 18.4 %copy-start.11 = (bf16[2,64,896]{2,1,0:T(8,128)(2,1)S(1)}, bf16[2,64,896]{2,1,0:T(8,128)(2,1)}, u32[]{:S(2)}) copy-start(bf16[2,64,896]{2,1,0:T(8,128)(2,1)} %param.15) | copy-start | bytes 688132
  115.7 1.2 copy-start.3
  116.1 1.2 copy-start.6
  118.2 8.6 %copy-start.7 = (f32[256,512]{1,0:T(8,128)S(1)}, f32[256,512]{1,0:T(8,128)}, u32[]{:S(2)}) copy-start(f32[256,512]{1,0:T(8,128)} %copy-done.6) | copy-start | bytes 1572868
  118.2 8.5 %collective-permute-start = (f32[128,1024]{1,0:T(8,128)}, f32[128,1024]{1,0:T(8,128)}, u32[]{:S(2)}, u32[]{:S(2)}) collective-permute-start(f32[128,1024]{1,0:T(8,128)} %fusion.3), channel_id=1, source_target_pairs={{0,16},{16,0},{1,17},{17,1},{2,18},{18,2},{3,19},{19,3},{4,20},{20... | collective-permute-start | bytes 1572872 | tf_op jit(solution)/shard_map/ppermute | solution.py:135
  120.6 12.5 %all-to-all-start.5 = ((bf16[16,16,128]{2,1,0:T(8,128)(2,1)}), bf16[16,16,128]{2,1,0:T(8,128)(2,1)S(1)}, u32[]{:S(2)}, u32[]{:S(2)}) async-start(bf16[16,16,128]{2,1,0:T(8,128)(2,1)} %bitcast.55), calls=%async_computation.5 | async-start | bytes 131072 | tf_op jit(solution)/shard_map/all_to_all | solution.py:117
  126.8 18.7 %copy-start.10 = (bf16[2,512,64]{1,2,0:T(8,128)(2,1)S(1)}, bf16[2,512,64]{1,2,0:T(8,128)(2,1)}, u32[]{:S(2)}) copy-start(bf16[2,512,64]{1,2,0:T(8,128)(2,1)} %param.14) | copy-start | bytes 393220
  127.9 18.3 %copy-start.5 = (bf16[256,1024]{1,0:T(8,128)(2,1)S(1)}, bf16[256,1024]{1,0:T(8,128)(2,1)}, u32[]{:S(2)}) copy-start(bf16[256,1024]{1,0:T(8,128)(2,1)} %copy-done.4) | copy-start | bytes 1572868

commit v7 on v5

--- a/solution.py
+++ b/solution.py
@@ -29,10 +29,10 @@
     return lax.all_to_all(blocks, axis, 0, 0).reshape((count * value.shape[0],) + value.shape[1:])
 
 
-def scatter_sum(value, axis, sent):
-    count = lax.axis_size(axis)
-    blocks = value.astype(sent).reshape(count, value.shape[0] // count, value.shape[1])
-    return jnp.sum(lax.all_to_all(blocks, axis, 0, 0).astype(f32), axis=0)
+def own_block(value, first_row, rows):
+    return lax.dynamic_slice(
+        value, (first_row, 0), (rows, value.shape[1]), allow_negative_indices=False
+    )
 
 
 def on_device(
@@ -72,6 +72,8 @@
     block_mask = lax.dynamic_slice_in_dim(masks16, lax.axis_index("zlo"), 1, 0)
     own_columns = lax.axis_index("y") * columns
     own_rows_z = lax.axis_index("zhi") * 16
+    own_half = lax.axis_index("core") * 128
+    other_half = 128 - own_half
     fours = jnp.arange(4, dtype=jnp.int32)
     peers_x = (fours != lax.axis_index("x")).astype(f32).reshape(4, 1, 1)
     peers_z = (fours != lax.axis_index("zhi")).astype(f32).reshape(4, 1, 1)
@@ -91,6 +93,8 @@
         block_mask,
         own_columns,
         own_rows_z,
+        own_half,
+        other_half,
         peers_x,
         peers_z,
     ) = lax.optimization_barrier(
@@ -103,6 +107,8 @@
             block_mask,
             own_columns,
             own_rows_z,
+        own_half,
+        other_half,
             peers_x,
             peers_z,
         )
@@ -149,9 +155,11 @@
     grad_b = (adapter_scale * leading_product(low_all, grad_up_all)).reshape(
         adapters, rank, hidden_units
     )
-    partial, grad_b = lax.optimization_barrier((partial, grad_b))
-
-    summed = scatter_sum(partial, "core", f32)
+    summed = own_block(partial, own_half, 128) + lax.ppermute(
+        own_block(partial, other_half, 128), "core", [(0, 1), (1, 0)]
+    )
+    summed, grad_b = lax.optimization_barrier((summed, grad_b))
+
     packed = (summed[:quarter, 2 * width :] + summed[quarter:, 2 * width :]).astype(bf16)
     peers = lax.axis_size(PIPE_LINKS)
     wide = jnp.transpose(packed.reshape(-1, 8, columns), (1, 0, 2)).reshape(8, -1)

time: 145 us -> 143 us (0.986)
  blocking collectives: 88.4 us -> 78.5 us
  starting transfers between devices: 14 us -> 21.5 us
    all_to_all x1 -> x0, blocking collectives: 9.85 us -> none  [scatter_sum(): return jnp.sum(lax.all_to_all(blocks, axis, 0, 0).astype(f32), axis=0)]
    ppermute x0 -> x1, starting transfers between devices: none -> 7.46 us  [on_device(): lax.ppermute(own_block(partial, other_half, 128), 'core', [(0, 1), (1, 0)])]
  transfers between devices with their start and end apart: 2 -> 3, of which waited for: 2 -> 3; matrix products, arithmetic and copies ran while one was open for 2% -> 3% of each run, Pallas kernels for 0% -> 0%
where the time goes in v7:
time: 143 us; the launch traced here: 142 us
  blocking collectives  78.5 us (55%)
  waiting for transfers between devices  25.5 us (18%)
  starting transfers between devices  21.5 us (15%)
  matrix products  8.17 us (6%)
  other arithmetic  5.48 us (4%)
  local copies, waits for them, and re-layouts  2.17 us (2%)
    all_to_all x2, blocking collectives, gather_rows(): lax.all_to_all(blocks, axis, 0, 0)  31.6 us
    all_to_all x1, blocking collectives, on_device(): summed = jnp.sum(lax.all_to_all(sent, PIPE_LINKS, 0, 0).astype(f32), axis=0)  20 us
    all_to_all x1, blocking collectives, on_device(): came = lax.all_to_all(parts.astype(bf16).reshape(4, 16, -1), 'zhi', 0, 0)  18.5 us
    all_to_all x1, waiting for transfers between devices, on_device(): came = lax.all_to_all(sent.reshape(4, 64, -1), 'x', 0, 0)  16.3 us
    all_to_all x1, starting transfers between devices, gather_rows(): lax.all_to_all(blocks, axis, 0, 0)  9.56 us
    all_to_all x1, waiting for transfers between devices, gather_rows(): lax.all_to_all(blocks, axis, 0, 0)  8.67 us
    ppermute x1, starting transfers between devices, on_device(): lax.ppermute(own_block(partial, other_half, 128), 'core', [(0, 1), (1, 0)])  7.46 us
    all_to_all x1, starting transfers between devices, on_device(): came = lax.all_to_all(sent.reshape(4, 64, -1), 'x', 0, 0)  4.45 us
  transfers between devices with their start and end apart: 3, of which 3 were waited for; matrix products, arithmetic and copies ran while one was open for 3% of the time, Pallas kernels for 0%

profile of v7, /device:TPU:1, one launch (start us, length us, event | category | flops | bytes accessed | tf_op | source)
XLA Modules:
  0.0 142.4 jit_solution(1707284416891127496)
XLA Ops:
  0.6 0.0 copy-start
  0.6 0.0 copy-start.4
  0.7 0.0 copy-start.2
  0.7 0.9 pad_maximum_fusion.5
  1.5 0.7 broadcast_in_dim.14
  2.3 9.6 %all-to-all-start = ((bf16[16,8,1024]{2,1,0:T(8,128)(2,1)}), bf16[16,8,1024]{2,1,0:T(8,128)(2,1)S(1)}, u32[]{:S(2)}, u32[]{:S(2)}) async-start(bf16[16,8,1024]{2,1,0:T(8,128)(2,1)} %broadcast_in_dim.14), calls=%async_computation | async-start | bytes 524288 | tf_op jit(solution)/shard_map/all_to_all | solution.py:29
  11.9 8.7 %all-to-all-done = bf16[16,8,1024]{2,1,0:T(8,128)(2,1)S(1)} async-done(((bf16[16,8,1024]{2,1,0:T(8,128)(2,1)}), bf16[16,8,1024]{2,1,0:T(8,128)(2,1)S(1)}, u32[]{:S(2)}, u32[]{:S(2)}) %all-to-all-start) | async-done | bytes 262176 | tf_op jit(solution)/shard_map/all_to_all | solution.py:29
  20.6 4.1 %all_gather.6 = bf16[256,1024]{1,0:T(8,128)(2,1)S(1)} all-gather(bf16[128,1024]{1,0:T(8,128)(2,1)S(1)} %bitcast.62), channel_id=1, replica_groups=mesh['zlo'=2,'y'=8,'core'=2,'zhi'=4,'x'=4] {'core'}, dimensions={0}, use_global_device_ids=true | all-gather | bytes 786432 | tf_op jit(solution)/shard_map/all_gather | solution.py:55
  24.7 0.0 copy-done.4
  24.7 0.2 convolution_convert_fusion.3
  24.9 0.0 copy-done.2
  24.9 0.0 copy-start.1
  24.9 0.4 convolution_convert_fusion.1
  25.4 0.3 fusion.23
  25.7 0.4 copy-done.1
  26.1 0.5 convolution_convert_fusion
  26.6 0.0 copy-done
  26.6 0.4 convolution_convert_fusion.2
  27.0 1.2 pad_maximum_fusion
  28.2 0.0 copy-start.7
  28.3 4.4 %all-to-all-start.1 = ((bf16[4,64,2816]{2,1,0:T(8,128)(2,1)}), bf16[4,64,2816]{2,1,0:T(8,128)(2,1)}, u32[]{:S(2)}, u32[]{:S(2)}) async-start(bf16[4,64,2816]{2,1,0:T(8,128)(2,1)} %bitcast.59), calls=%async_computation.1 | async-start | bytes 2883584 | tf_op jit(solution)/shard_map/all_to_all | solution.py:86
  32.7 0.0 copy-done.7
  32.7 0.1 fusion.36
  32.8 1.1 fusion.21
  33.9 0.3 fusion.25
  34.2 0.4 fusion.18
  34.6 0.9 pad_maximum_fusion.2
  35.5 16.3 %all-to-all-done.1 = bf16[4,64,2816]{2,1,0:T(8,128)(2,1)} async-done(((bf16[4,64,2816]{2,1,0:T(8,128)(2,1)}), bf16[4,64,2816]{2,1,0:T(8,128)(2,1)}, u32[]{:S(2)}, u32[]{:S(2)}) %all-to-all-start.1) | async-done | bytes 1441824 | tf_op jit(solution)/shard_map/all_to_all | solution.py:86
  51.8 0.0 copy-start.3
  51.8 1.9 %multiply_reduce_fusion = f32[64,2816]{1,0:T(8,128)S(1)} fusion(bf16[4,64,2816]{2,1,0:T(8,128)(2,1)} %all-to-all-done.1, f32[4]{0:T(128)S(1)} %bitcast.73), kind=kLoop, calls=%fused_computation | loop fusion | flops 1982464 | bytes 2162704 | tf_op jit(solution)/shard_map/reduce_sum | solution.py:116
  53.7 0.0 copy-done.3
  53.7 0.1 fusion.37
  53.8 0.0 copy-start.6
  53.8 18.5 %all_to_all.30 = bf16[4,16,2816]{2,1,0:T(8,128)(2,1)S(1)} all-to-all(bf16[4,16,2816]{2,1,0:T(8,128)(2,1)S(1)} %bitcast.60), channel_id=1, replica_groups=mesh['zlo'=2,'y'=8,'core'=2,'zhi'=4,'x'=4] {'zhi'}, dimensions={0} | all-to-all | bytes 720896 | tf_op jit(solution)/shard_map/all_to_all | solution.py:117
  72.3 0.1 multiply_reduce_fusion.1
  72.5 0.0 copy-done.6
  72.5 0.2 multiply_convert_fusion.2
  72.7 14.5 %all_to_all.31 = bf16[4,16,2816]{2,1,0:T(8,128)(2,1)S(1)} all-to-all(bf16[4,16,2816]{2,1,0:T(8,128)(2,1)S(1)} %broadcast_in_dim.15), channel_id=1, replica_groups=mesh['zlo'=2,'y'=8,'core'=2,'zhi'=4,'x'=4] {'zhi'}, dimensions={0} | all-to-all | bytes 720896 | tf_op jit(solution)/shard_map/all_to_all | solution.py:29
  87.2 0.1 broadcast_in_dim.17
  87.3 17.2 %all_to_all.32 = bf16[4,64,2816]{2,1,0:T(8,128)(2,1)S(1)} all-to-all(bf16[4,64,2816]{2,1,0:T(8,128)(2,1)S(1)} %broadcast_in_dim.17), channel_id=1, replica_groups=mesh['zlo'=2,'y'=8,'core'=2,'zhi'=4,'x'=4] {'x'}, dimensions={0} | all-to-all | bytes 2883584 | tf_op jit(solution)/shard_map/all_to_all | solution.py:29
  104.4 0.5 fusion.3
  104.9 0.4 fusion.5
  105.3 0.3 fusion
  105.6 0.5 convolution_add_fusion
  106.1 0.1 pad_maximum_fusion.1
  106.2 0.1 constant_dynamic-slice_fusion
  106.3 7.5 %collective-permute-start = (f32[128,1152]{1,0:T(8,128)S(1)}, f32[128,1152]{1,0:T(8,128)S(1)}, u32[]{:S(2)}, u32[]{:S(2)}) collective-permute-start(f32[128,1152]{1,0:T(8,128)S(1)} %constant_dynamic-slice_fusion), channel_id=1, source_target_pairs={{0,16},{16,0},{1,17},{17,1},{2,18},{18,2},{3,19},{19,3},{4,20},{20... | collective-permute-start | bytes 1769480 | tf_op jit(solution)/shard_map/ppermute | solution.py:158
  113.7 1.0 convolution_multiply_fusion
  114.8 0.6 collective-permute-done
  115.4 0.1 dynamic-slice_add_fusion
  115.6 0.0 copy-start.5
  115.6 20.0 %all_to_all.33 = bf16[16,8,2048]{2,1,0:T(8,128)(2,1)S(1)} all-to-all(bf16[16,8,2048]{2,1,0:T(8,128)(2,1)S(1)} %pad_maximum_fusion.3), channel_id=1, replica_groups=mesh['zlo'=2,'y'=8,'core'=2,'zhi'=4,'x'=4] {'zlo','y'}, dimensions={0} | all-to-all | bytes 1048576 | tf_op jit(solution)/shard_map/all_to_all | solution.py:173
  135.6 0.1 convert_reduce_fusion
  135.7 0.6 slice.85
  136.3 4.3 %all_gather.7 = bf16[2,64,128]{2,1,0:T(8,128)(2,1)S(1)} all-gather(bf16[1,64,128]{2,1,0:T(8,128)(2,1)S(1)} %get-tuple-element.45), channel_id=1, replica_groups=mesh['zlo'=2,'y'=8,'core'=2,'zhi'=4,'x'=4] {'core'}, dimensions={0}, use_global_device_ids=true | all-gather | bytes 49152 | tf_op jit(solution)/shard_map/all_gather | solution.py:183
  140.6 0.1 copy.24
  140.7 0.9 convolution_bitcast_fusion
  141.6 0.0 copy-done.5
  141.6 0.8 fusion.2
  (16 shorter events, 0.2 us)
Async XLA Ops:
  0.6 26.0 %copy-start = (bf16[512,896]{1,0:T(8,128)(2,1)S(1)}, bf16[512,896]{1,0:T(8,128)(2,1)}, u32[]{:S(2)}) copy-start(bf16[512,896]{1,0:T(8,128)(2,1)} %param.9) | copy-start | bytes 2752516
  0.6 24.0 %copy-start.4 = (bf16[2,512,64]{1,2,0:T(8,128)(2,1)S(1)}, bf16[2,512,64]{1,2,0:T(8,128)(2,1)}, u32[]{:S(2)}) copy-start(bf16[2,512,64]{1,2,0:T(8,128)(2,1)} %param.12) | copy-start | bytes 393220
  0.7 24.3 %copy-start.2 = (bf16[512,896]{1,0:T(8,128)(2,1)S(1)}, bf16[512,896]{1,0:T(8,128)(2,1)}, u32[]{:S(2)}) copy-start(bf16[512,896]{1,0:T(8,128)(2,1)} %param.10) | copy-start | bytes 2752516
  2.3 18.3 %all-to-all-start = ((bf16[16,8,1024]{2,1,0:T(8,128)(2,1)}), bf16[16,8,1024]{2,1,0:T(8,128)(2,1)S(1)}, u32[]{:S(2)}, u32[]{:S(2)}) async-start(bf16[16,8,1024]{2,1,0:T(8,128)(2,1)} %broadcast_in_dim.14), calls=%async_computation | async-start | bytes 524288 | tf_op jit(solution)/shard_map/all_to_all | solution.py:29
  24.9 1.2 copy-start.1
  28.2 4.5 %copy-start.7 = (s32[2]{0:T(128)S(1)}, s32[2]{0:T(128)}, u32[]{:S(2)}) copy-start(s32[2]{0:T(128)} %param.14) | copy-start | bytes 28
  28.3 23.6 %all-to-all-start.1 = ((bf16[4,64,2816]{2,1,0:T(8,128)(2,1)}), bf16[4,64,2816]{2,1,0:T(8,128)(2,1)}, u32[]{:S(2)}, u32[]{:S(2)}) async-start(bf16[4,64,2816]{2,1,0:T(8,128)(2,1)} %bitcast.59), calls=%async_computation.1 | async-start | bytes 2883584 | tf_op jit(solution)/shard_map/all_to_all | solution.py:86
  51.8 1.9 %copy-start.3 = (f32[64,2816]{1,0:T(8,128)S(1)}, f32[64,2816]{1,0:T(8,128)}, u32[]{:S(2)}) copy-start(f32[64,2816]{1,0:T(8,128)} %pad_maximum_fusion.2) | copy-start | bytes 2162692
  53.8 18.7 %copy-start.6 = (bf16[2,64,896]{2,1,0:T(8,128)(2,1)S(1)}, bf16[2,64,896]{2,1,0:T(8,128)(2,1)}, u32[]{:S(2)}) copy-start(bf16[2,64,896]{2,1,0:T(8,128)(2,1)} %param.13) | copy-start | bytes 688132
  106.3 9.1 %collective-permute-start = (f32[128,1152]{1,0:T(8,128)S(1)}, f32[128,1152]{1,0:T(8,128)S(1)}, u32[]{:S(2)}, u32[]{:S(2)}) collective-permute-start(f32[128,1152]{1,0:T(8,128)S(1)} %constant_dynamic-slice_fusion), channel_id=1, source_target_pairs={{0,16},{16,0},{1,17},{17,1},{2,18},{18,2},{3,19},{19,3},{4,20},{20... | collective-permute-start | bytes 1769480 | tf_op jit(solution)/shard_map/ppermute | solution.py:158
  115.6 26.0 %copy-start.5 = (bf16[2,512,64]{1,2,0:T(8,128)(2,1)S(1)}, bf16[2,512,64]{1,2,0:T(8,128)(2,1)}, u32[]{:S(2)}) copy-start(bf16[2,512,64]{1,2,0:T(8,128)(2,1)} %param.12) | copy-start | bytes 393220

commit v8 on v2

--- a/solution.py
+++ b/solution.py
@@ -1,6 +1,8 @@
 import jax
 import jax.numpy as jnp
 from jax import lax
+from jax.experimental import pallas as pl
+from jax.experimental.pallas import tpu as pltpu
 from jax.sharding import Mesh, PartitionSpec as P
 
 PIPE = ("zlo", "y", "core")
@@ -29,10 +31,85 @@
     return lax.all_to_all(blocks, axis, 0, 0).reshape((count * value.shape[0],) + value.shape[1:])
 
 
-def scatter_sum(value, axis, sent):
-    count = lax.axis_size(axis)
-    blocks = value.astype(sent).reshape(count, value.shape[0] // count, value.shape[1])
-    return jnp.sum(lax.all_to_all(blocks, axis, 0, 0).astype(f32), axis=0)
+def own_block(value, first_row, rows):
+    return lax.dynamic_slice(
+        value, (first_row, 0), (rows, value.shape[1]), allow_negative_indices=False
+    )
+
+
+def on_chip(kernel, out_shape, scalars, *arrays, scratch=()):
+    return pl.pallas_call(
+        kernel,
+        out_shape=out_shape,
+        in_specs=[pl.BlockSpec(memory_space=pltpu.SMEM)] * len(scalars)
+        + [pl.BlockSpec(memory_space=pltpu.VMEM)] * len(arrays),
+        out_specs=[pl.BlockSpec(memory_space=pltpu.VMEM)] * len(out_shape),
+        scratch_shapes=scratch,
+        compiler_params=pltpu.CompilerParams(vmem_limit_bytes=40 * 2**20),
+    )(*scalars, *arrays)
+
+
+def first_products(both, gate, up, down, first, sent, own, product_of):
+    width, units = gate.shape
+    own_rows = own.shape[0]
+    start = pl.multiple_of(lax.axis_index("x") * own_rows, own_rows)
+
+    def put(value, at):
+        size = value.shape[1]
+        product_of[:, :size] = value
+        sent[:, at : at + size] = value.astype(bf16)
+        own[:, at : at + size] = product_of[pl.ds(start, own_rows), :size]
+
+    for at in range(0, units, 256):
+        to = min(at + 256, units)
+        put(product(both[:, :width], gate[:, at:to]), at)
+        put(product(both[:, :width], up[:, at:to]), units + at)
+        put(trailing_product(both[:, width:], down[at:to, :]), 2 * units + at)
+    put(trailing_product(both[:, :width], first[...]), 3 * units)
+
+
+def sum_of_blocks(came, own, index, rows):
+    total = own
+    for peer in range(came.shape[0]):
+        factor = jnp.where(index == peer, 0.0, 1.0).astype(f32)
+        total = total + came[peer, rows, :].astype(f32) * factor
+    return total
+
+
+def middle_sum(came, own, sent, next_own):
+    x, zhi = lax.axis_index("x"), lax.axis_index("zhi")
+    size = next_own.shape[0]
+    for block in range(own.shape[0] // size):
+        rows = pl.ds(block * size, size)
+        total = sum_of_blocks(came, own[rows, :], x, rows)
+        sent[rows, :] = total.astype(bf16)
+
+        @pl.when(zhi == block)
+        def _():
+            next_own[...] = total
+
+
+def elementwise(adapter_of_block, came, own, second, rows):
+    columns, units = second.shape
+    size = own.shape[0]
+    whole = sum_of_blocks(came, own[...], lax.axis_index("zhi"), pl.ds(0, size))
+    adapter = adapter_of_block[lax.rem(lax.axis_index("x"), 2)]
+    column = lax.broadcasted_iota(jnp.int32, (size, columns), 1)
+    chosen = (column >= adapter * (columns // 2)) & (column < (adapter + 1) * (columns // 2))
+    low = jnp.where(chosen, whole[:, 3 * units :], 0.0).astype(bf16)
+    gate = whole[:, :units]
+    grad_hidden = whole[:, 2 * units : 3 * units]
+    up = whole[:, units : 2 * units] + adapter_scale * product(low, second[...])
+    sig = jax.nn.sigmoid(gate)
+    act = gate * sig
+    hidden = (act * up).astype(bf16)
+    grad_up = (grad_hidden * act).astype(bf16)
+    grad_gate = (grad_hidden * up * sig * (1.0 + gate * (1.0 - sig))).astype(bf16)
+    for copy in range(rows.shape[0]):
+        rows[copy, :, :units] = hidden
+        rows[copy, :, units : 2 * units] = grad_gate
+        rows[copy, :, 2 * units : 3 * units] = grad_up
+        rows[copy, :, 3 * units :] = low
 
 
 def on_device(
@@ -51,43 +128,68 @@
     first = jnp.transpose(adapter_first_factors, (1, 0, 2)).reshape(width, columns)
     second = adapter_second_factors.reshape(columns, hidden_units)
 
+    both = jnp.concatenate([tokens, cotangent], axis=1)
+    both = lax.all_gather(gather_rows(both, PIPE_LINKS), "core", axis=0, tiled=True)
+    token_rows = both[:, :width]
+    row_total = both.shape[0]
+    all_columns = 3 * hidden_units + columns
+
+    first_flat = jnp.transpose(adapter_first_factors, (0, 2, 1)).reshape(columns, width)
+    sent, own = on_chip(
+        first_products,
+        [
+            jax.ShapeDtypeStruct((row_total, all_columns), bf16),
+            jax.ShapeDtypeStruct((row_total // 4, all_columns), f32),
+        ],
+        [],
+        both,
+        gate_weight,
+        upward_weight,
+        down_weight,
+        first_flat,
+        scratch=[pltpu.VMEM((row_total, 256), f32)],
+    )
+    came = lax.all_to_all(sent.reshape(4, row_total // 4, -1), "x", 0, 0)
+    sent, own = on_chip(
+        middle_sum,
+        [
+            jax.ShapeDtypeStruct((row_total // 4, all_columns), bf16),
+            jax.ShapeDtypeStruct((row_total // 16, all_columns), f32),
+        ],
+        [],
+        came,
+        own,
+    )
+    came = lax.all_to_all(sent.reshape(4, row_total // 16, -1), "zhi", 0, 0)
+    (rows,) = on_chip(
+        elementwise,
+        [jax.ShapeDtypeStruct((4, row_total // 16, all_columns), bf16)],
+        [adapter_of_block],
+        came,
+        own,
+        second,
+    )
+    rows = lax.all_to_all(rows, "zhi", 0, 0).reshape(row_total // 4, -1)
+    rows = gather_rows(rows, "x")
+
     own = jnp.arange(columns, dtype=jnp.int32) // rank
     masks = (own[None, :] == adapter_of_block[:, None]).astype(f32)
-    own_mask = lax.dynamic_slice_in_dim(masks, lax.axis_index("x") % 2, 1, 0)
-    block_mask = lax.dynamic_slice_in_dim(masks, lax.axis_index("zlo"), 1, 0)
-    both = jnp.concatenate([tokens, cotangent], axis=1)
+    masks16 = masks.astype(bf16)
+    block_mask = lax.dynamic_slice_in_dim(masks16, lax.axis_index("zlo"), 1, 0)
     own_columns = lax.axis_index("y") * columns
-    masks16, block_mask = masks.astype(bf16), block_mask.astype(bf16)
-    both, masks, masks16, own_mask, block_mask, own_columns = lax.optimization_barrier(
-        (both, masks, masks16, own_mask, block_mask, own_columns)
-    )
-    both = lax.all_gather(gather_rows(both, PIPE_LINKS), "core", axis=0, tiled=True)
-    token_rows, adjoint_rows = both[:, :width], both[:, width:]
-
-    parts = jnp.concatenate(
-        [
-            product(token_rows, gate_weight).astype(bf16),
-            product(token_rows, upward_weight).astype(bf16),
-            trailing_product(adjoint_rows, down_weight).astype(bf16),
-            product(token_rows, first).astype(bf16),
-        ],
-        axis=1,
-    )
-    parts = scatter_sum(scatter_sum(parts, "x", bf16), "zhi", f32)
-
-    gate = parts[:, :hidden_units]
-    up_base = parts[:, hidden_units : 2 * hidden_units]
-    grad_hidden = parts[:, 2 * hidden_units : 3 * hidden_units]
-    low = (parts[:, 3 * hidden_units :] * own_mask).astype(bf16)
-    up = up_base + adapter_scale * product(low, second)
-    sig = jax.nn.sigmoid(gate)
-    act = gate * sig
-    hidden = (act * up).astype(bf16)
-    grad_up = (grad_hidden * act).astype(bf16)
-    grad_gate = (grad_hidden * up * sig * (1.0 + gate * (1.0 - sig))).astype(bf16)
-
-    rows = jnp.concatenate([hidden, grad_gate, grad_up, low], axis=1)
-    rows = gather_rows(gather_rows(rows, "zhi"), "x")
+    own_half = lax.axis_index("core") * 128
+    other_half = 128 - own_half
+    (
+        rows,
+        masks,
+        masks16,
+        block_mask,
+        own_columns,
+        own_half,
+        other_half,
+    ) = lax.optimization_barrier(
+        (rows, masks, masks16, block_mask, own_columns, own_half, other_half)
+    )
     hidden_all = rows[:, :hidden_units]
     grad_gate_all = rows[:, hidden_units : 2 * hidden_units]
     grad_up_all = rows[:, 2 * hidden_units : 3 * hidden_units]
@@ -109,9 +211,11 @@
     grad_b = (adapter_scale * leading_product(low_all, grad_up_all)).reshape(
         adapters, rank, hidden_units
     )
-    partial, grad_b = lax.optimization_barrier((partial, grad_b))
-
-    summed = scatter_sum(partial, "core", f32)
+    summed = own_block(partial, own_half, 128) + lax.ppermute(
+        own_block(partial, other_half, 128), "core", [(0, 1), (1, 0)]
+    )
+    summed, grad_b = lax.optimization_barrier((summed, grad_b))
+
     packed = (summed[:quarter, 2 * width :] + summed[quarter:, 2 * width :]).astype(bf16)
     peers = lax.axis_size(PIPE_LINKS)
     wide = jnp.transpose(packed.reshape(-1, 8, columns), (1, 0, 2)).reshape(8, -1)

time: 150 us -> 145 us (0.967)
  blocking collectives: 136 us -> 100 us
  waiting for transfers between devices: 0 us -> 14.2 us
  starting transfers between devices: 0 us -> 12.3 us
  other arithmetic: 4.78 us -> 1.17 us
  local copies, waits for them, and re-layouts: 0.96 us -> 4.45 us
  matrix products: 6.96 us -> 9.59 us
  Pallas kernels: 0 us -> 2.32 us
    all_to_all x3 -> x1, blocking collectives: 46.5 us -> 18.1 us  [gather_rows(): lax.all_to_all(blocks, axis, 0, 0)]
    all_to_all x0 -> x1, waiting for transfers between devices: none -> 14.2 us  [gather_rows(): lax.all_to_all(blocks, axis, 0, 0)]
    ppermute x0 -> x1, starting transfers between devices: none -> 7.96 us  [on_device(): lax.ppermute(own_block(partial, other_half, 128), 'core', [(0, 1), (1, 0)])]
    all_to_all x0 -> x1, starting transfers between devices: none -> 4.32 us  [gather_rows(): lax.all_to_all(blocks, axis, 0, 0)]
    all_to_all x3, blocking collectives: 58.8 us -> 55 us  [the longest x1 22.3 us: on_device(): came = lax.all_to_all(sent.reshape(4, row_total // 4, -1), 'x', 0, 0)]
    all_to_all x1, blocking collectives: 22.4 us -> 19.3 us  [on_device(): summed = jnp.sum(lax.all_to_all(sent, PIPE_LINKS, 0, 0).astype(f32), axis=0)]
    dot_general x5 -> x4, matrix products: 2.48 us -> 5.07 us  [trailing_product(): lax.dot_general(left, right, (((1,), (1,)), ((), ())), preferred_element_...]
    unnamed x12 -> x16, local copies, waits for them, and re-layouts: 0.04 us -> 2.39 us
  transfers between devices with their start and end apart: 0 -> 2, of which waited for: 0 -> 1; matrix products, arithmetic and copies ran while one was open for 0% -> 1% of each run, Pallas kernels for 0% -> 0%
where the time goes in v8:
time: 145 us
  blocking collectives  100 us (69%)
  waiting for transfers between devices  14.2 us (10%)
  starting transfers between devices  12.3 us (8%)
  matrix products  9.59 us (7%)
  local copies, waits for them, and re-layouts  4.45 us (3%)
  Pallas kernels  2.32 us (2%)
    all_to_all x1, blocking collectives, on_device(): came = lax.all_to_all(sent.reshape(4, row_total // 4, -1), 'x', 0, 0)  22.3 us
    all_to_all x1, blocking collectives, on_device(): summed = jnp.sum(lax.all_to_all(sent, PIPE_LINKS, 0, 0).astype(f32), axis=0)  19.3 us
    all_to_all x1, blocking collectives, gather_rows(): lax.all_to_all(blocks, axis, 0, 0)  18.1 us
    all_to_all x1, blocking collectives, on_device(): came = lax.all_to_all(sent.reshape(4, row_total // 16, -1), 'zhi', 0, 0)  18.1 us
    all_to_all x1, blocking collectives, on_device(): rows = lax.all_to_all(rows, 'zhi', 0, 0).reshape(row_total // 4, -1)  14.6 us
    all_to_all x1, waiting for transfers between devices, gather_rows(): lax.all_to_all(blocks, axis, 0, 0)  14.2 us
    ppermute x1, starting transfers between devices, on_device(): lax.ppermute(own_block(partial, other_half, 128), 'core', [(0, 1), (1, 0)])  7.96 us
    dot_general x4, matrix products, trailing_product(): lax.dot_general(left, right, (((1,), (1,)), ((), ())), preferred_element_...  5.07 us
  transfers between devices with their start and end apart: 2, of which 1 were waited for; matrix products, arithmetic and copies ran while one was open for 1% of the time, Pallas kernels for 0%

profile of v8, /device:TPU:1, one launch (start us, length us, event | category | flops | bytes accessed | tf_op | source)
XLA Modules:
  0.0 144.8 jit_solution(11336096470032712463)
XLA Ops:
  0.6 0.0 copy-start
  0.6 0.0 copy-start.6
  0.7 0.8 pad_maximum_fusion.2
  1.5 18.1 %all_to_all.30 = bf16[16,8,1024]{2,1,0:T(8,128)(2,1)S(1)} all-to-all(bf16[16,8,1024]{2,1,0:T(8,128)(2,1)S(1)} %broadcast_in_dim.12), channel_id=1, replica_groups=mesh['zlo'=2,'y'=8,'core'=2,'zhi'=4,'x'=4] {'zlo','y'}, dimensions={0} | all-to-all | bytes 524288 | tf_op jit(solution)/shard_map/all_to_all | solution.py:31
  19.6 4.1 %all_gather.6.both = bf16[256,1024]{1,0:T(8,128)(2,1)S(1)} all-gather(bf16[128,1024]{1,0:T(8,128)(2,1)S(1)} %bitcast.51), channel_id=1, replica_groups=mesh['zlo'=2,'y'=8,'core'=2,'zhi'=4,'x'=4] {'core'}, dimensions={0}, use_global_device_ids=true | all-gather | bytes 786432 | tf_op jit(solution)/shard_map/all_gather | solution.py:132
  23.7 0.0 copy-done
  23.7 0.0 copy-done.6
  23.7 0.0 copy-start.1
  23.7 1.2 copy-done.1
  24.9 0.0 copy-start.3
  24.9 1.2 copy-done.3
  26.1 1.3 shard_map.111
  27.4 22.3 %all_to_all.31.came = bf16[4,64,2816]{2,1,0:T(8,128)(2,1)S(1)} all-to-all(bf16[4,64,2816]{2,1,0:T(8,128)(2,1)S(1)} %bitcast.44), channel_id=1, replica_groups=mesh['zlo'=2,'y'=8,'core'=2,'zhi'=4,'x'=4] {'x'}, dimensions={0} | all-to-all | bytes 2883584 | tf_op jit(solution)/shard_map/all_to_all | solution.py:152
  49.6 0.0 copy-start.5
  49.6 0.0 copy-start.7
  49.6 0.3 shard_map.112
  50.0 18.1 %all_to_all.32.came = bf16[4,16,2816]{2,1,0:T(8,128)(2,1)S(1)} all-to-all(bf16[4,16,2816]{2,1,0:T(8,128)(2,1)S(1)} %bitcast.49), channel_id=1, replica_groups=mesh['zlo'=2,'y'=8,'core'=2,'zhi'=4,'x'=4] {'zhi'}, dimensions={0} | all-to-all | bytes 720896 | tf_op jit(solution)/shard_map/all_to_all | solution.py:163
  68.0 0.0 copy-done.5
  68.0 0.0 copy-done.7
  68.0 0.7 shard_map.113
  68.8 14.6 %all_to_all.33 = bf16[4,16,2816]{2,1,0:T(8,128)(2,1)S(1)} all-to-all(bf16[4,16,2816]{2,1,0:T(8,128)(2,1)S(1)} %shard_map.113), channel_id=1, replica_groups=mesh['zlo'=2,'y'=8,'core'=2,'zhi'=4,'x'=4] {'zhi'}, dimensions={0} | all-to-all | bytes 720896 | tf_op jit(solution)/shard_map/all_to_all | solution.py:172
  83.4 1.2 broadcast_in_dim.14
  84.6 4.3 %all-to-all-start.4 = ((bf16[4,64,2816]{2,1,0:T(8,128)(2,1)}), bf16[4,64,2816]{2,1,0:T(8,128)(2,1)}, u32[]{:S(2)}, u32[]{:S(2)}) async-start(bf16[4,64,2816]{2,1,0:T(8,128)(2,1)} %broadcast_in_dim.14), calls=%async_computation.4 | async-start | bytes 2883584 | tf_op jit(solution)/shard_map/all_to_all | solution.py:31
  88.9 0.0 copy-start.2
  89.0 0.1 fusion.16
  89.0 14.2 %all-to-all-done.4 = bf16[4,64,2816]{2,1,0:T(8,128)(2,1)} async-done(((bf16[4,64,2816]{2,1,0:T(8,128)(2,1)}), bf16[4,64,2816]{2,1,0:T(8,128)(2,1)}, u32[]{:S(2)}, u32[]{:S(2)}) %all-to-all-start.4) | async-done | bytes 1441824 | tf_op jit(solution)/shard_map/all_to_all | solution.py:31
  103.2 1.5 %fusion.2 = f32[256,512]{1,0:T(8,128)S(1)} fusion(bf16[512,896]{1,0:T(8,128)(2,1)S(1)} %copy-done, bf16[256,2816]{1,0:T(8,128)(2,1)} %bitcast.7), kind=kOutput, calls=%fused_computation.12 | convolution fusion | flops 234881024 | bytes 1900544 | tf_op jit(solution)/shard_map/dot_general | solution.py:21
  104.7 0.0 copy-done.2
  104.7 0.0 copy-start.4
  104.7 1.5 %fusion.4 = f32[256,512]{1,0:T(8,128)S(1)} fusion(bf16[896,512]{1,0:T(8,128)(2,1)S(1)} %copy-done.2, bf16[256,2816]{1,0:T(8,128)(2,1)} %bitcast.7), kind=kOutput, calls=%fused_computation.14 | convolution fusion | flops 234881024 | bytes 1900544 | tf_op jit(solution)/shard_map/dot_general | solution.py:17
  106.3 1.3 fusion
  107.6 0.0 copy-done.4
  107.6 1.5 %convolution_add_fusion = f32[256,512]{1,0:T(8,128)S(1)} fusion(f32[256,512]{1,0:T(8,128)S(1)} %fusion.2, bf16[512,896]{1,0:T(8,128)(2,1)S(1)} %copy-done.4, bf16[256,2816]{1,0:T(8,128)(2,1)} %bitcast.7), kind=kOutput, calls=%fused_computation | convolution fusion | flops 235012096 | bytes 2424832 | tf_op jit(solution)/shard_map/dot_general | solution.py:21
  109.1 0.1 pad_maximum_fusion
  109.2 0.1 constant_dynamic-slice_fusion
  109.3 8.0 %collective-permute-start = (f32[128,1152]{1,0:T(8,128)S(1)}, f32[128,1152]{1,0:T(8,128)S(1)}, u32[]{:S(2)}, u32[]{:S(2)}) collective-permute-start(f32[128,1152]{1,0:T(8,128)S(1)} %constant_dynamic-slice_fusion), channel_id=1, source_target_pairs={{0,16},{16,0},{1,17},{17,1},{2,18},{18,2},{3,19},{19,3},{4,20},{20... | collective-permute-start | bytes 1769480 | tf_op jit(solution)/shard_map/ppermute | solution.py:214
  117.2 2.1 %convolution_multiply_fusion = f32[128,896]{1,0:T(8,128)} fusion(bf16[256,2816]{1,0:T(8,128)(2,1)} %bitcast.7), kind=kOutput, calls=%fused_computation.1 | convolution fusion | flops 58834944 | bytes 983040 | tf_op jit(solution)/shard_map/dot_general | solution.py:25
  119.3 0.0 collective-permute-done
  119.3 0.1 dynamic-slice_add_fusion
  119.5 19.3 %all_to_all.34 = bf16[16,8,2048]{2,1,0:T(8,128)(2,1)S(1)} all-to-all(bf16[16,8,2048]{2,1,0:T(8,128)(2,1)S(1)} %pad_maximum_fusion.1), channel_id=1, replica_groups=mesh['zlo'=2,'y'=8,'core'=2,'zhi'=4,'x'=4] {'zlo','y'}, dimensions={0} | all-to-all | bytes 1048576 | tf_op jit(solution)/shard_map/all_to_all | solution.py:229
  138.9 0.1 convert_reduce_fusion
  139.0 0.6 slice.48
  139.6 3.4 %all_gather.7 = bf16[2,64,128]{2,1,0:T(8,128)(2,1)S(1)} all-gather(bf16[1,64,128]{2,1,0:T(8,128)(2,1)S(1)} %get-tuple-element.30), channel_id=1, replica_groups=mesh['zlo'=2,'y'=8,'core'=2,'zhi'=4,'x'=4] {'core'}, dimensions={0}, use_global_device_ids=true | all-gather | bytes 49152 | tf_op jit(solution)/shard_map/all_gather | solution.py:239
  143.0 0.1 copy.20
  143.1 0.9 convolution_bitcast_fusion
  144.0 0.8 fusion.1
  (11 shorter events, 0.2 us)
Async XLA Ops:
  0.6 23.1 %copy-start = (bf16[512,896]{1,0:T(8,128)(2,1)S(1)}, bf16[512,896]{1,0:T(8,128)(2,1)}, u32[]{:S(2)}) copy-start(bf16[512,896]{1,0:T(8,128)(2,1)} %gate.1) | copy-start | bytes 2752516
  0.6 23.1 %copy-start.6 = (bf16[2,512,64]{1,2,0:T(8,128)(2,1)S(1)}, bf16[2,512,64]{1,2,0:T(8,128)(2,1)}, u32[]{:S(2)}) copy-start(bf16[2,512,64]{1,2,0:T(8,128)(2,1)} %param.12) | copy-start | bytes 393220
  23.7 1.2 copy-start.1
  24.9 1.2 copy-start.3
  49.6 18.4 %copy-start.5 = (bf16[2,64,896]{2,1,0:T(8,128)(2,1)S(1)}, bf16[2,64,896]{2,1,0:T(8,128)(2,1)}, u32[]{:S(2)}) copy-start(bf16[2,64,896]{2,1,0:T(8,128)(2,1)} %param.13) | copy-start | bytes 688132
  49.6 18.4 %copy-start.7 = (s32[2]{0:T(128)S(1)}, s32[2]{0:T(128)}, u32[]{:S(2)}) copy-start(s32[2]{0:T(128)} %adapter_of_block.1) | copy-start | bytes 28
  84.6 18.6 %all-to-all-start.4 = ((bf16[4,64,2816]{2,1,0:T(8,128)(2,1)}), bf16[4,64,2816]{2,1,0:T(8,128)(2,1)}, u32[]{:S(2)}, u32[]{:S(2)}) async-start(bf16[4,64,2816]{2,1,0:T(8,128)(2,1)} %broadcast_in_dim.14), calls=%async_computation.4 | async-start | bytes 2883584 | tf_op jit(solution)/shard_map/all_to_all | solution.py:31
  88.9 15.8 %copy-start.2 = (bf16[896,512]{1,0:T(8,128)(2,1)S(1)}, bf16[896,512]{1,0:T(8,128)(2,1)}, u32[]{:S(2)}) copy-start(bf16[896,512]{1,0:T(8,128)(2,1)} %down.1) | copy-start | bytes 2752516
  104.7 2.9 %copy-start.4 = (bf16[512,896]{1,0:T(8,128)(2,1)S(1)}, bf16[512,896]{1,0:T(8,128)(2,1)}, u32[]{:S(2)}) copy-start(bf16[512,896]{1,0:T(8,128)(2,1)} %up.1) | copy-start | bytes 2752516
  109.3 10.1 %collective-permute-start = (f32[128,1152]{1,0:T(8,128)S(1)}, f32[128,1152]{1,0:T(8,128)S(1)}, u32[]{:S(2)}, u32[]{:S(2)}) collective-permute-start(f32[128,1152]{1,0:T(8,128)S(1)} %constant_dynamic-slice_fusion), channel_id=1, source_target_pairs={{0,16},{16,0},{1,17},{17,1},{2,18},{18,2},{3,19},{19,3},{4,20},{20... | collective-permute-start | bytes 1769480 | tf_op jit(solution)/shard_map/ppermute | solution.py:214

commit v9 on v8

v9 whole, which is shorter than its diff:
```python
import jax
import jax.numpy as jnp
from jax import lax
from jax.experimental import pallas as pl
from jax.experimental.pallas import tpu as pltpu
from jax.sharding import Mesh, PartitionSpec as P

PIPE = ("zlo", "y", "core")
TENSOR = ("zhi", "x")
PIPE_LINKS = ("zlo", "y")
adapter_scale = 0.5
bf16 = jnp.bfloat16
f32 = jnp.float32


def product(left, right):
    return jnp.dot(left, right, preferred_element_type=f32)


def trailing_product(left, right):
    return lax.dot_general(left, right, (((1,), (1,)), ((), ())), preferred_element_type=f32)


def leading_product(left, right):
    return lax.dot_general(left, right, (((0,), (0,)), ((), ())), preferred_element_type=f32)


def gather_rows(value, axis):
    count = lax.axis_size(axis)
    blocks = jnp.broadcast_to(value[None], (count,) + value.shape)
    return lax.all_to_all(blocks, axis, 0, 0).reshape((count * value.shape[0],) + value.shape[1:])


def own_block(value, first_row, rows):
    return lax.dynamic_slice(
        value, (first_row, 0), (rows, value.shape[1]), allow_negative_indices=False
    )


def on_chip(kernel, out_shape, scalars, arrays, far=(), scratch=()):
    return pl.pallas_call(
        kernel,
        out_shape=out_shape,
        in_specs=[pl.BlockSpec(memory_space=pltpu.SMEM)] * len(scalars)
        + [pl.BlockSpec(memory_space=pltpu.VMEM)] * len(arrays)
        + [pl.BlockSpec(memory_space=pltpu.HBM)] * len(far),
        out_specs=[pl.BlockSpec(memory_space=pltpu.VMEM)] * len(out_shape),
        scratch_shapes=scratch,
        compiler_params=pltpu.CompilerParams(vmem_limit_bytes=40 * 2**20),
    )(*scalars, *arrays, *(pltpu.with_memory_space_constraint(array, pltpu.HBM) for array in far))


def near_and_done(*arrays):
    return [pltpu.VMEM(array.shape, array.dtype) for array in arrays] + [
        pltpu.SemaphoreType.DMA((len(arrays),))
    ]


def chosen_columns(adapter, rows, columns, rank):
    column = lax.broadcasted_iota(jnp.int32, (rows, columns), 1)
    return (column >= adapter * rank) & (column < (adapter + 1) * rank)


def first_products(both, gate, first, up_far, down_far, sent, own, product_of, up, down, done):
    fetch_up = pltpu.make_async_copy(up_far, up, done.at[0])
    fetch_down = pltpu.make_async_copy(down_far, down, done.at[1])
    fetch_up.start()
    fetch_down.start()
    width, units = gate.shape
    own_rows = own.shape[0]
    start = pl.multiple_of(lax.axis_index("x") * own_rows, own_rows)

    def put(value, at):
        size = value.shape[1]
        product_of[:, :size] = value
        sent[:, at : at + size] = value.astype(bf16)
        own[:, at : at + size] = product_of[pl.ds(start, own_rows), :size]

    chunks = [(at, min(at + 256, units)) for at in range(0, units, 256)]
    for at, to in chunks:
        put(product(both[:, :width], gate[:, at:to]), at)
    put(trailing_product(both[:, :width], first[...]), 3 * units)
    fetch_up.wait()
    for at, to in chunks:
        put(product(both[:, :width], up[:, at:to]), units + at)
    fetch_down.wait()
    for at, to in chunks:
        put(trailing_product(both[:, width:], down[at:to, :]), 2 * units + at)


def sum_of_blocks(came, own, index, rows):
    total = own
    for peer in range(came.shape[0]):
        factor = jnp.where(index == peer, 0.0, 1.0).astype(f32)
        total = total + came[peer, rows, :].astype(f32) * factor
    return total


def middle_sum(came, own, sent, next_own):
    x, zhi = lax.axis_index("x"), lax.axis_index("zhi")
    size = next_own.shape[0]
    for block in range(own.shape[0] // size):
        rows = pl.ds(block * size, size)
        total = sum_of_blocks(came, own[rows, :], x, rows)
        sent[rows, :] = total.astype(bf16)

        @pl.when(zhi == block)
        def _():
            next_own[...] = total


def elementwise(adapter_of_block, came, own, second, rows):
    columns, units = second.shape
    size = own.shape[0]
    whole = sum_of_blocks(came, own[...], lax.axis_index("zhi"), pl.ds(0, size))
    adapter = adapter_of_block[lax.rem(lax.axis_index("x"), 2)]
    chosen = chosen_columns(adapter, size, columns, columns // 2)
    low = jnp.where(chosen, whole[:, 3 * units :], 0.0).astype(bf16)
    gate = whole[:, :units]
    grad_hidden = whole[:, 2 * units : 3 * units]
    up = whole[:, units : 2 * units] + adapter_scale * product(low, second[...])
    sig = jax.nn.sigmoid(gate)
    act = gate * sig
    hidden = (act * up).astype(bf16)
    grad_up = (grad_hidden * act).astype(bf16)
    grad_gate = (grad_hidden * up * sig * (1.0 + gate * (1.0 - sig))).astype(bf16)
    for copy in range(rows.shape[0]):
        rows[copy, :, :units] = hidden
        rows[copy, :, units : 2 * units] = grad_gate
        rows[copy, :, 2 * units : 3 * units] = grad_up
        rows[copy, :, 3 * units :] = low


def last_products(adapter_of_block, rows, gate, up, down, second, own, other, product_of):
    width, units = gate.shape
    columns = second.shape[0]
    half, quarter = rows.shape[0] // 2, rows.shape[0] // 4
    core = lax.axis_index("core")
    own_start = pl.multiple_of(core * half, half)
    other_start = pl.multiple_of((1 - core) * half, half)

    def put(at, size):
        own[:, at : at + size] = product_of[pl.ds(own_start, half), :size]
        other[:, at : at + size] = product_of[pl.ds(other_start, half), :size]

    grad_up = rows[:, 2 * units : 3 * units]
    value = adapter_scale * trailing_product(grad_up, second[...])
    for block in range(4):
        adapter = adapter_of_block[block % 2]
        part = value[block * quarter : (block + 1) * quarter, :]
        part = jnp.where(chosen_columns(adapter, quarter, columns, columns // 2), part, 0.0)
        product_of[pl.ds(block * quarter, quarter), :columns] = part
    put(2 * width, columns)
    grad_gate = rows[:, units : 2 * units]
    for at in range(0, width, 256):
        product_of[...] = trailing_product(grad_gate, gate[at : at + 256, :]) + trailing_product(
            grad_up, up[at : at + 256, :]
        )
        put(width + at, 256)
    for at in range(0, width, 256):
        product_of[...] = product(rows[:, :units], down[:, at : at + 256])
        put(at, 256)


def core_sum(own, came, sent):
    total = own[...] + came[...]
    peers, rows, _ = sent.shape
    columns = 128
    sums = total.shape[1] - columns
    half = total.shape[0] // 2
    packed = (total[:half, sums:] + total[half:, sums:]).astype(bf16).astype(f32)
    wide = jnp.concatenate(
        [packed[at : at + rows, :] for at in range(0, half, rows)], axis=1
    ).astype(bf16)
    for peer in range(peers):
        sent[peer, :, :sums] = total[peer * rows : (peer + 1) * rows, :sums].astype(bf16)
        sent[peer, :, sums:] = wide


def pipe_sum(came, sums, packed):
    total = came[0].astype(f32)
    for peer in range(1, came.shape[0]):
        total = total + came[peer].astype(f32)
    rows, size = sums.shape
    sums[...] = total[:, :size]
    columns = packed.shape[1]
    packed[...] = jnp.concatenate(
        [total[:, at : at + columns] for at in range(size, total.shape[1], columns)], axis=0
    ).astype(bf16)


def outputs(adapter_of_block, sums, packed, both, first, mixed, grad_tokens, grad_a):
    rows = sums.shape[0]
    columns, width = first.shape
    cores, quarter, _ = packed.shape
    rank = columns // 2
    masks = [
        chosen_columns(adapter_of_block[block], quarter, columns, rank) for block in range(2)
    ]
    core, zlo, y = (lax.axis_index(name) for name in ("core", "zlo", "y"))
    mixed[...] = sums[:, :width].astype(bf16)
    low_own = packed[core, pl.ds(pl.multiple_of(y * rows, rows), rows), :]
    own_mask = chosen_columns(adapter_of_block[zlo], rows, columns, rank)
    low_own = jnp.where(own_mask, low_own.astype(f32), 0.0).astype(bf16)
    grad_tokens[...] = (sums[:, width:] + product(low_own, first[...])).astype(bf16)
    low_back = jnp.concatenate(
        [
            jnp.where(mask, packed[at].astype(f32), 0.0).astype(bf16)
            for at in range(cores)
            for mask in masks
        ],
        axis=0,
    )
    grad_a[...] = leading_product(low_back, both[:, :width])


def on_device(
    tokens,
    gate_weight,
    upward_weight,
    down_weight,
    adapter_first_factors,
    adapter_second_factors,
    adapter_of_block,
    cotangent,
):
    adapters, width, rank = adapter_first_factors.shape
    hidden_units = gate_weight.shape[1]
    columns = adapters * rank
    second = adapter_second_factors.reshape(columns, hidden_units)

    both = jnp.concatenate([tokens, cotangent], axis=1)
    both = lax.all_gather(gather_rows(both, PIPE_LINKS), "core", axis=0, tiled=True)
    row_total = both.shape[0]
    all_columns = 3 * hidden_units + columns

    first_flat = jnp.transpose(adapter_first_factors, (0, 2, 1)).reshape(columns, width)
    sent, own = on_chip(
        first_products,
        [
            jax.ShapeDtypeStruct((row_total, all_columns), bf16),
            jax.ShapeDtypeStruct((row_total // 4, all_columns), f32),
        ],
        [],
        [both, gate_weight, first_flat],
        far=[upward_weight, down_weight],
        scratch=[pltpu.VMEM((row_total, 256), f32), *near_and_done(upward_weight, down_weight)],
    )
    came = lax.all_to_all(sent.reshape(4, row_total // 4, -1), "x", 0, 0)
    sent, own = on_chip(
        middle_sum,
        [
            jax.ShapeDtypeStruct((row_total // 4, all_columns), bf16),
            jax.ShapeDtypeStruct((row_total // 16, all_columns), f32),
        ],
        [],
        [came, own],
    )
    came = lax.all_to_all(sent.reshape(4, row_total // 16, -1), "zhi", 0, 0)
    (rows,) = on_chip(
        elementwise,
        [jax.ShapeDtypeStruct((4, row_total // 16, all_columns), bf16)],
        [adapter_of_block],
        [came, own, second],
    )
    rows = lax.all_to_all(rows, "zhi", 0, 0).reshape(row_total // 4, -1)
    rows = gather_rows(rows, "x")

    own, other = on_chip(
        last_products,
        [jax.ShapeDtypeStruct((row_total // 2, 2 * width + columns), f32)] * 2,
        [adapter_of_block],
        [rows, gate_weight, upward_weight, down_weight, second],
        scratch=[pltpu.VMEM((row_total, 256), f32)],
    )
    came = lax.ppermute(other, "core", [(0, 1), (1, 0)])
    grad_up_all = rows[:, 2 * hidden_units : 3 * hidden_units]
    grad_b = adapter_scale * leading_product(rows[:, 3 * hidden_units :], grad_up_all)
    grad_b = grad_b.reshape(adapters, rank, hidden_units)
    came, grad_b = lax.optimization_barrier((came, grad_b))

    peers = lax.axis_size(PIPE_LINKS)
    (sent,) = on_chip(
        core_sum,
        [jax.ShapeDtypeStruct((peers, row_total // 2 // peers, 4 * width), bf16)],
        [],
        [own, came],
    )
    came = lax.all_to_all(sent, PIPE_LINKS, 0, 0)
    sums, packed = on_chip(
        pipe_sum,
        [
            jax.ShapeDtypeStruct((tokens.shape[0], 2 * width), f32),
            jax.ShapeDtypeStruct((row_total // 4, columns), bf16),
        ],
        [],
        [came],
    )
    packed = lax.all_gather(packed, "core", axis=0)
    mixed, grad_tokens, grad_a = on_chip(
        outputs,
        [
            jax.ShapeDtypeStruct((tokens.shape[0], width), bf16),
            jax.ShapeDtypeStruct((tokens.shape[0], width), bf16),
            jax.ShapeDtypeStruct((columns, width), f32),
        ],
        [adapter_of_block],
        [sums, packed, both, first_flat],
    )
    grad_a = jnp.transpose(grad_a.reshape(adapters, rank, width), (0, 2, 1))
    return mixed, grad_tokens, grad_a, grad_b


def solution(mesh):
    parts = Mesh(mesh.devices.reshape(2, 8, 2, 4, 4), PIPE + TENSOR)
    in_specs = (
        P(PIPE, TENSOR),
        P(TENSOR, PIPE),
        P(TENSOR, PIPE),
        P(PIPE, TENSOR),
        P(None, TENSOR, None),
        P(None, None, PIPE),
        P(),
        P(PIPE, TENSOR),
    )
    out_specs = (
        P(PIPE, TENSOR),
        P(PIPE, TENSOR),
        P(None, TENSOR, None),
        P(None, None, PIPE),
    )
    return jax.shard_map(
        on_device, mesh=parts, in_specs=in_specs, out_specs=out_specs, check_vma=False
    )
```

time: 145 us -> 135 us (0.931)
  blocking collectives: 100 us -> 117 us
  waiting for transfers between devices: 14.2 us -> 0.58 us
  matrix products: 9.59 us -> 1.02 us
  starting transfers between devices: 12.3 us -> 7.32 us
  Pallas kernels: 2.32 us -> 7.04 us
  local copies, waits for them, and re-layouts: 4.45 us -> 0.14 us
    all_to_all x1 -> x2, blocking collectives: 18.1 us -> 35.5 us  [gather_rows(): lax.all_to_all(blocks, axis, 0, 0)]
    all_to_all x1 -> x0, waiting for transfers between devices: 14.2 us -> none  [gather_rows(): lax.all_to_all(blocks, axis, 0, 0)]
    dot_general x5 -> x0, matrix products: 6.61 us -> none  [the longest x4 5.07 us: trailing_product(): lax.dot_general(left, right, (((1,), (1,)), ((), ())), preferred_element_...]
    pallas_call x3 -> x7, Pallas kernels: 2.32 us -> 7.04 us  [on_chip(): pl.pallas_call(kernel, out_shape=out_shape, in_specs=[pl.BlockSpec(memory...]
    all_to_all x1 -> x0, starting transfers between devices: 4.32 us -> none  [gather_rows(): lax.all_to_all(blocks, axis, 0, 0)]
    unnamed x16 -> x12, local copies, waits for them, and re-layouts: 2.39 us -> 0.03 us
    dot_general x2 -> x1, matrix products: 2.98 us -> 1.02 us  [leading_product(): lax.dot_general(left, right, (((0,), (0,)), ((), ())), preferred_element_...]
  transfers between devices with their start and end apart: 2 -> 1, of which waited for: 1 -> 1; matrix products, arithmetic and copies ran while one was open for 1% -> 1% of each run, Pallas kernels for 0% -> 0%
where the time goes in v9:
time: 135 us
  blocking collectives  117 us (87%)
  starting transfers between devices  7.32 us (5%)
  Pallas kernels  7.04 us (5%)
    all_to_all x2, blocking collectives, gather_rows(): lax.all_to_all(blocks, axis, 0, 0)  35.5 us
    all_to_all x1, blocking collectives, on_device(): came = lax.all_to_all(sent.reshape(4, row_total // 4, -1), 'x', 0, 0)  22.3 us
    all_to_all x1, blocking collectives, on_device(): came = lax.all_to_all(sent, PIPE_LINKS, 0, 0)  18.4 us
    all_to_all x1, blocking collectives, on_device(): came = lax.all_to_all(sent.reshape(4, row_total // 16, -1), 'zhi', 0, 0)  18.1 us
    all_to_all x1, blocking collectives, on_device(): rows = lax.all_to_all(rows, 'zhi', 0, 0).reshape(row_total // 4, -1)  14.7 us
    ppermute x1, starting transfers between devices, on_device(): came = lax.ppermute(other, 'core', [(0, 1), (1, 0)])  7.32 us
    pallas_call x7, Pallas kernels, on_chip(): pl.pallas_call(kernel, out_shape=out_shape, in_specs=[pl.BlockSpec(memory...  7.04 us
    all_gather x1, blocking collectives, on_device(): packed = lax.all_gather(packed, 'core', axis=0)  4.3 us
  transfers between devices with their start and end apart: 1, of which 1 were waited for; matrix products, arithmetic and copies ran while one was open for 1% of the time, Pallas kernels for 0%

profile of v9, /device:TPU:1, one launch (start us, length us, event | category | flops | bytes accessed | tf_op | source)
XLA Modules:
  0.0 135.1 jit_solution(9019426536561803609)
XLA Ops:
  0.6 0.0 copy-start
  0.6 0.0 copy-start.4
  0.7 0.8 pad_maximum_fusion
  1.5 18.1 %all_to_all.30 = bf16[16,8,1024]{2,1,0:T(8,128)(2,1)S(1)} all-to-all(bf16[16,8,1024]{2,1,0:T(8,128)(2,1)S(1)} %broadcast_in_dim.6), channel_id=1, replica_groups=mesh['zlo'=2,'y'=8,'core'=2,'zhi'=4,'x'=4] {'zlo','y'}, dimensions={0} | all-to-all | bytes 524288 | tf_op jit(solution)/shard_map/all_to_all | solution.py:31
  19.6 4.1 %all_gather.9.both = bf16[256,1024]{1,0:T(8,128)(2,1)S(1)} all-gather(bf16[128,1024]{1,0:T(8,128)(2,1)S(1)} %bitcast.24), channel_id=1, replica_groups=mesh['zlo'=2,'y'=8,'core'=2,'zhi'=4,'x'=4] {'core'}, dimensions={0}, use_global_device_ids=true | all-gather | bytes 786432 | tf_op jit(solution)/shard_map/all_gather | solution.py:233
  23.7 0.0 copy-done
  23.7 0.0 copy-done.4
  23.7 2.6 %shard_map.111 = (bf16[256,2816]{1,0:T(8,128)(2,1)S(1)}, f32[64,2816]{1,0:T(8,128)S(1)}) custom-call(bf16[256,1024]{1,0:T(8,128)(2,1)S(1)} %all_gather.9.both, bf16[512,896]{1,0:T(8,128)(2,1)S(1)} %copy-done, bf16[128,512]{1,0:T(8,128)(2,1)S(1)} %bitcast.19, bf16[512,896]{1,0:T(8,128)(2,1)} %up.1, bf16[896,512]{1,0:T(8,128)(2,1)} %down.1), custom_call_target="tpu_custom_call" | custom-call | tf_op jit(solution)/shard_map/pallas_call | solution.py:41
  26.3 22.3 %all_to_all.31.came = bf16[4,64,2816]{2,1,0:T(8,128)(2,1)S(1)} all-to-all(bf16[4,64,2816]{2,1,0:T(8,128)(2,1)S(1)} %bitcast.16), channel_id=1, replica_groups=mesh['zlo'=2,'y'=8,'core'=2,'zhi'=4,'x'=4] {'x'}, dimensions={0} | all-to-all | bytes 2883584 | tf_op jit(solution)/shard_map/all_to_all | solution.py:249
  48.5 0.0 copy-start.3
  48.5 0.0 copy-start.5
  48.5 0.3 shard_map.112
  48.9 18.1 %all_to_all.32.came = bf16[4,16,2816]{2,1,0:T(8,128)(2,1)S(1)} all-to-all(bf16[4,16,2816]{2,1,0:T(8,128)(2,1)S(1)} %bitcast.21), channel_id=1, replica_groups=mesh['zlo'=2,'y'=8,'core'=2,'zhi'=4,'x'=4] {'zhi'}, dimensions={0} | all-to-all | bytes 720896 | tf_op jit(solution)/shard_map/all_to_all | solution.py:259
  66.9 0.0 copy-done.3
  66.9 0.0 copy-done.5
  66.9 0.7 shard_map.113
  67.7 14.7 %all_to_all.33 = bf16[4,16,2816]{2,1,0:T(8,128)(2,1)S(1)} all-to-all(bf16[4,16,2816]{2,1,0:T(8,128)(2,1)S(1)} %shard_map.113), channel_id=1, replica_groups=mesh['zlo'=2,'y'=8,'core'=2,'zhi'=4,'x'=4] {'zhi'}, dimensions={0} | all-to-all | bytes 720896 | tf_op jit(solution)/shard_map/all_to_all | solution.py:266
  82.4 0.1 broadcast_in_dim.15
  82.5 0.0 copy-start.1
  82.5 0.0 copy-start.2
  82.5 17.4 %all_to_all.34 = bf16[4,64,2816]{2,1,0:T(8,128)(2,1)S(1)} all-to-all(bf16[4,64,2816]{2,1,0:T(8,128)(2,1)S(1)} %broadcast_in_dim.15), channel_id=1, replica_groups=mesh['zlo'=2,'y'=8,'core'=2,'zhi'=4,'x'=4] {'x'}, dimensions={0} | all-to-all | bytes 2883584 | tf_op jit(solution)/shard_map/all_to_all | solution.py:31
  99.9 0.0 copy-done.1
  99.9 0.0 copy-done.2
  99.9 1.8 %shard_map.114 = (f32[128,1152]{1,0:T(8,128)S(1)}, f32[128,1152]{1,0:T(8,128)S(1)}) custom-call(s32[2]{0:T(128)S(1)} %copy-done.5, bf16[256,2816]{1,0:T(8,128)(2,1)S(1)} %bitcast.14, bf16[512,896]{1,0:T(8,128)(2,1)S(1)} %copy-done, bf16[512,896]{1,0:T(8,128)(2,1)S(1)} %copy-done.1, bf16[896,512]{1,0:T(8,128)(2,1)S(1)} %copy-done.2, bf16[128,896]{1,0:T(8,128)(2,1)S(1)} %bitcast.18), custom_call_target="tpu_custom_call" | custom-call | tf_op jit(solution)/shard_map/pallas_call | solution.py:41
  101.8 7.3 %collective-permute-start = (f32[128,1152]{1,0:T(8,128)S(1)}, f32[128,1152]{1,0:T(8,128)S(1)}, u32[]{:S(2)}, u32[]{:S(2)}) collective-permute-start(f32[128,1152]{1,0:T(8,128)S(1)} %get-tuple-element.22), channel_id=1, source_target_pairs={{0,16},{16,0},{1,17},{17,1},{2,18},{18,2},{3,19},{19,3},{4,20},{20... | collective-permute-start | bytes 1769480 | tf_op jit(solution)/shard_map/ppermute | solution.py:276
  109.1 1.0 convolution_multiply_fusion
  110.1 0.6 collective-permute-done.came
  110.7 0.1 shard_map.115
  110.8 18.4 %all_to_all.35.came = bf16[16,8,2048]{2,1,0:T(8,128)(2,1)S(1)} all-to-all(bf16[16,8,2048]{2,1,0:T(8,128)(2,1)S(1)} %shard_map.115), channel_id=1, replica_groups=mesh['zlo'=2,'y'=8,'core'=2,'zhi'=4,'x'=4] {'zlo','y'}, dimensions={0} | all-to-all | bytes 1048576 | tf_op jit(solution)/shard_map/all_to_all | solution.py:289
  129.2 0.1 shard_map.116
  129.3 4.3 %all-gather = bf16[128,128]{1,0:T(8,128)(2,1)S(1)} all-gather(bf16[64,128]{1,0:T(8,128)(2,1)S(1)} %get-tuple-element.25), channel_id=2, replica_groups=mesh['zlo'=2,'y'=8,'core'=2,'zhi'=4,'x'=4] {'core'}, dimensions={0}, use_global_device_ids=true | all-gather | bytes 49152 | tf_op jit(solution)/shard_map/all_gather | solution.py:299
  133.6 1.5 %shard_map.117 = (bf16[8,512]{1,0:T(8,128)(2,1)}, bf16[8,512]{1,0:T(8,128)(2,1)}, f32[128,512]{1,0:T(8,128)}) custom-call(s32[2]{0:T(128)S(1)} %copy-done.5, f32[8,1024]{1,0:T(8,128)S(1)} %get-tuple-element.24.sums, bf16[2,64,128]{2,1,0:T(8,128)(2,1)S(1)} %bitcast.22, bf16[256,1024]{1,0:T(8,128)(2,1)S(1)} %all_gather.9.both, bf16[128,512]{1,0:T(8,128)(2,1)S(1)} %bitcast.20), custom_call_target="tpu_custom_call" | custom-call | tf_op jit(solution)/shard_map/pallas_call | solution.py:41
  (1 shorter events, 0.0 us)
Async XLA Ops:
  0.6 23.1 %copy-start = (bf16[512,896]{1,0:T(8,128)(2,1)S(1)}, bf16[512,896]{1,0:T(8,128)(2,1)}, u32[]{:S(2)}) copy-start(bf16[512,896]{1,0:T(8,128)(2,1)} %gate.3) | copy-start | bytes 2752516
  0.6 23.1 %copy-start.4 = (bf16[2,512,64]{1,2,0:T(8,128)(2,1)S(1)}, bf16[2,512,64]{1,2,0:T(8,128)(2,1)}, u32[]{:S(2)}) copy-start(bf16[2,512,64]{1,2,0:T(8,128)(2,1)} %param.12) | copy-start | bytes 393220
  48.5 18.4 %copy-start.3 = (bf16[2,64,896]{2,1,0:T(8,128)(2,1)S(1)}, bf16[2,64,896]{2,1,0:T(8,128)(2,1)}, u32[]{:S(2)}) copy-start(bf16[2,64,896]{2,1,0:T(8,128)(2,1)} %param.13) | copy-start | bytes 688132
  48.5 18.4 %copy-start.5 = (s32[2]{0:T(128)S(1)}, s32[2]{0:T(128)}, u32[]{:S(2)}) copy-start(s32[2]{0:T(128)} %adapter_of_block.5) | copy-start | bytes 28
  82.5 17.5 %copy-start.1 = (bf16[512,896]{1,0:T(8,128)(2,1)S(1)}, bf16[512,896]{1,0:T(8,128)(2,1)}, u32[]{:S(2)}) copy-start(bf16[512,896]{1,0:T(8,128)(2,1)} %up.1) | copy-start | bytes 2752516
  82.5 17.4 %copy-start.2 = (bf16[896,512]{1,0:T(8,128)(2,1)S(1)}, bf16[896,512]{1,0:T(8,128)(2,1)}, u32[]{:S(2)}) copy-start(bf16[896,512]{1,0:T(8,128)(2,1)} %down.1) | copy-start | bytes 2752516
  101.8 8.9 %collective-permute-start = (f32[128,1152]{1,0:T(8,128)S(1)}, f32[128,1152]{1,0:T(8,128)S(1)}, u32[]{:S(2)}, u32[]{:S(2)}) collective-permute-start(f32[128,1152]{1,0:T(8,128)S(1)} %get-tuple-element.22), channel_id=1, source_target_pairs={{0,16},{16,0},{1,17},{17,1},{2,18},{18,2},{3,19},{19,3},{4,20},{20... | collective-permute-start | bytes 1769480 | tf_op jit(solution)/shard_map/ppermute | solution.py:276

commit v10 on v9

--- a/solution.py
+++ b/solution.py
@@ -9,6 +9,7 @@
 TENSOR = ("zhi", "x")
 PIPE_LINKS = ("zlo", "y")
 adapter_scale = 0.5
+sent_scale = 16.0
 bf16 = jnp.bfloat16
 f32 = jnp.float32
 
@@ -37,23 +38,16 @@
     )
 
 
-def on_chip(kernel, out_shape, scalars, arrays, far=(), scratch=()):
+def on_chip(kernel, out_shape, scalars, arrays, scratch=()):
     return pl.pallas_call(
         kernel,
         out_shape=out_shape,
         in_specs=[pl.BlockSpec(memory_space=pltpu.SMEM)] * len(scalars)
-        + [pl.BlockSpec(memory_space=pltpu.VMEM)] * len(arrays)
-        + [pl.BlockSpec(memory_space=pltpu.HBM)] * len(far),
+        + [pl.BlockSpec(memory_space=pltpu.VMEM)] * len(arrays),
         out_specs=[pl.BlockSpec(memory_space=pltpu.VMEM)] * len(out_shape),
         scratch_shapes=scratch,
         compiler_params=pltpu.CompilerParams(vmem_limit_bytes=40 * 2**20),
-    )(*scalars, *arrays, *(pltpu.with_memory_space_constraint(array, pltpu.HBM) for array in far))
-
-
-def near_and_done(*arrays):
-    return [pltpu.VMEM(array.shape, array.dtype) for array in arrays] + [
-        pltpu.SemaphoreType.DMA((len(arrays),))
-    ]
+    )(*scalars, *arrays)
 
 
 def chosen_columns(adapter, rows, columns, rank):
@@ -61,58 +55,20 @@
     return (column >= adapter * rank) & (column < (adapter + 1) * rank)
 
 
-def first_products(both, gate, first, up_far, down_far, sent, own, product_of, up, down, done):
-    fetch_up = pltpu.make_async_copy(up_far, up, done.at[0])
-    fetch_down = pltpu.make_async_copy(down_far, down, done.at[1])
-    fetch_up.start()
-    fetch_down.start()
-    width, units = gate.shape
-    own_rows = own.shape[0]
-    start = pl.multiple_of(lax.axis_index("x") * own_rows, own_rows)
-
-    def put(value, at):
-        size = value.shape[1]
-        product_of[:, :size] = value
-        sent[:, at : at + size] = value.astype(bf16)
-        own[:, at : at + size] = product_of[pl.ds(start, own_rows), :size]
-
-    chunks = [(at, min(at + 256, units)) for at in range(0, units, 256)]
-    for at, to in chunks:
-        put(product(both[:, :width], gate[:, at:to]), at)
-    put(trailing_product(both[:, :width], first[...]), 3 * units)
-    fetch_up.wait()
-    for at, to in chunks:
-        put(product(both[:, :width], up[:, at:to]), units + at)
-    fetch_down.wait()
-    for at, to in chunks:
-        put(trailing_product(both[:, width:], down[at:to, :]), 2 * units + at)
-
-
-def sum_of_blocks(came, own, index, rows):
-    total = own
-    for peer in range(came.shape[0]):
-        factor = jnp.where(index == peer, 0.0, 1.0).astype(f32)
-        total = total + came[peer, rows, :].astype(f32) * factor
+def scatter_sum(value, axis):
+    count = lax.axis_size(axis)
+    blocks = value.astype(jnp.float16).reshape(count, value.shape[0] // count, -1)
+    came = lax.all_to_all(blocks, axis, 0, 0).astype(f32)
+    total = came[0]
+    for peer in range(1, count):
+        total = total + came[peer]
     return total
 
 
-def middle_sum(came, own, sent, next_own):
-    x, zhi = lax.axis_index("x"), lax.axis_index("zhi")
-    size = next_own.shape[0]
-    for block in range(own.shape[0] // size):
-        rows = pl.ds(block * size, size)
-        total = sum_of_blocks(came, own[rows, :], x, rows)
-        sent[rows, :] = total.astype(bf16)
-
-        @pl.when(zhi == block)
-        def _():
-            next_own[...] = total
-
-
-def elementwise(adapter_of_block, came, own, second, rows):
+def elementwise(adapter_of_block, scaled, second, rows):
     columns, units = second.shape
-    size = own.shape[0]
-    whole = sum_of_blocks(came, own[...], lax.axis_index("zhi"), pl.ds(0, size))
+    size = scaled.shape[0]
+    whole = scaled[...] * (1 / sent_scale)
     adapter = adapter_of_block[lax.rem(lax.axis_index("x"), 2)]
     chosen = chosen_columns(adapter, size, columns, columns // 2)
     low = jnp.where(chosen, whole[:, 3 * units :], 0.0).astype(bf16)
@@ -231,37 +187,26 @@
 
     both = jnp.concatenate([tokens, cotangent], axis=1)
     both = lax.all_gather(gather_rows(both, PIPE_LINKS), "core", axis=0, tiled=True)
+    token_rows, adjoint_rows = both[:, :width], both[:, width:]
     row_total = both.shape[0]
     all_columns = 3 * hidden_units + columns
 
     first_flat = jnp.transpose(adapter_first_factors, (0, 2, 1)).reshape(columns, width)
-    sent, own = on_chip(
-        first_products,
-        [
-            jax.ShapeDtypeStruct((row_total, all_columns), bf16),
-            jax.ShapeDtypeStruct((row_total // 4, all_columns), f32),
-        ],
-        [],
-        [both, gate_weight, first_flat],
-        far=[upward_weight, down_weight],
-        scratch=[pltpu.VMEM((row_total, 256), f32), *near_and_done(upward_weight, down_weight)],
-    )
-    came = lax.all_to_all(sent.reshape(4, row_total // 4, -1), "x", 0, 0)
-    sent, own = on_chip(
-        middle_sum,
-        [
-            jax.ShapeDtypeStruct((row_total // 4, all_columns), bf16),
-            jax.ShapeDtypeStruct((row_total // 16, all_columns), f32),
-        ],
-        [],
-        [came, own],
-    )
-    came = lax.all_to_all(sent.reshape(4, row_total // 16, -1), "zhi", 0, 0)
+    parts = jnp.concatenate(
+        [
+            (product(token_rows, gate_weight) * sent_scale).astype(jnp.float16),
+            (product(token_rows, upward_weight) * sent_scale).astype(jnp.float16),
+            (trailing_product(adjoint_rows, down_weight) * sent_scale).astype(jnp.float16),
+            (trailing_product(token_rows, first_flat) * sent_scale).astype(jnp.float16),
+        ],
+        axis=1,
+    )
+    parts = scatter_sum(scatter_sum(parts, "x"), "zhi")
     (rows,) = on_chip(
         elementwise,
         [jax.ShapeDtypeStruct((4, row_total // 16, all_columns), bf16)],
         [adapter_of_block],
-        [came, own, second],
+        [parts, second],
     )
     rows = lax.all_to_all(rows, "zhi", 0, 0).reshape(row_total // 4, -1)
     rows = gather_rows(rows, "x")

time: 135 us -> 135 us (level)
  Pallas kernels: 7.04 us -> 4.15 us
  matrix products: 1.02 us -> 2.6 us
    pallas_call x7 -> x5, Pallas kernels: 7.04 us -> 4.15 us  [on_chip(): pl.pallas_call(kernel, out_shape=out_shape, in_specs=[pl.BlockSpec(memory...]
    dot_general x0 -> x4, matrix products: none -> 1.58 us  [the longest x2 0.88 us: product(): return jnp.dot(left, right, preferred_element_type=f32)]
where the time goes in v10:
time: 135 us
  blocking collectives  117 us (87%)
  starting transfers between devices  7.45 us (6%)
  Pallas kernels  4.15 us (3%)
  matrix products  2.6 us (2%)
  other arithmetic  1.74 us (1%)
    all_to_all x2, blocking collectives, scatter_sum(): came = lax.all_to_all(blocks, axis, 0, 0).astype(f32)  40.5 us
    all_to_all x2, blocking collectives, gather_rows(): lax.all_to_all(blocks, axis, 0, 0)  35.2 us
    all_to_all x1, blocking collectives, on_device(): came = lax.all_to_all(sent, PIPE_LINKS, 0, 0)  18.4 us
    all_to_all x1, blocking collectives, on_device(): rows = lax.all_to_all(rows, 'zhi', 0, 0).reshape(row_total // 4, -1)  14.6 us
    ppermute x1, starting transfers between devices, on_device(): came = lax.ppermute(other, 'core', [(0, 1), (1, 0)])  7.45 us
    all_gather x1, blocking collectives, on_device(): packed = lax.all_gather(packed, 'core', axis=0)  4.3 us
    all_gather x1, blocking collectives, on_device(): lax.all_gather(gather_rows(both, PIPE_LINKS), 'core', axis=0, tiled=True)  4.27 us
    pallas_call x5, Pallas kernels, on_chip(): pl.pallas_call(kernel, out_shape=out_shape, in_specs=[pl.BlockSpec(memory...  4.15 us
  transfers between devices with their start and end apart: 1, of which 1 were waited for; matrix products, arithmetic and copies ran while one was open for 1% of the time, Pallas kernels for 0%

profile of v10, /device:TPU:1, one launch (start us, length us, event | category | flops | bytes accessed | tf_op | source)
XLA Modules:
  0.0 135.1 jit_solution(5240933749643724447)
XLA Ops:
  0.6 0.0 copy-start.4
  0.6 0.0 copy-start.1
  0.7 0.8 pad_maximum_fusion.1
  1.5 18.1 %all_to_all.30 = bf16[16,8,1024]{2,1,0:T(8,128)(2,1)S(1)} all-to-all(bf16[16,8,1024]{2,1,0:T(8,128)(2,1)S(1)} %broadcast_in_dim.6), channel_id=1, replica_groups=mesh['zlo'=2,'y'=8,'core'=2,'zhi'=4,'x'=4] {'zlo','y'}, dimensions={0} | all-to-all | bytes 524288 | tf_op jit(solution)/shard_map/all_to_all | solution.py:32
  19.6 0.0 copy-start
  19.6 4.3 %all_gather.9.both = bf16[256,1024]{1,0:T(8,128)(2,1)S(1)} all-gather(bf16[128,1024]{1,0:T(8,128)(2,1)S(1)} %bitcast.30), channel_id=1, replica_groups=mesh['zlo'=2,'y'=8,'core'=2,'zhi'=4,'x'=4] {'core'}, dimensions={0}, use_global_device_ids=true | all-gather | bytes 786432 | tf_op jit(solution)/shard_map/all_gather | solution.py:189
  23.8 0.0 copy-done.4
  23.9 0.2 fusion.3
  24.1 0.0 copy-done.1
  24.1 0.0 copy-start.2
  24.1 0.4 fusion.1
  24.6 0.0 copy-done
  24.6 0.5 fusion.2
  25.0 0.2 copy-done.2
  25.3 0.4 fusion
  25.7 0.5 pad_maximum_fusion
  26.2 22.2 %all_to_all.31 = f16[4,64,2816]{2,1,0:T(8,128)(2,1)S(1)} all-to-all(f16[4,64,2816]{2,1,0:T(8,128)(2,1)S(1)} %bitcast.27), channel_id=1, replica_groups=mesh['zlo'=2,'y'=8,'core'=2,'zhi'=4,'x'=4] {'x'}, dimensions={0} | all-to-all | bytes 2883584 | tf_op jit(solution)/shard_map/all_to_all | solution.py:61
  48.5 0.2 convert_element_type.29
  48.7 0.1 fusion.4
  48.8 0.0 copy-start.3
  48.9 0.0 copy-start.5
  48.9 18.2 %all_to_all.32 = f16[4,16,2816]{2,1,0:T(8,128)(2,1)S(1)} all-to-all(f16[4,16,2816]{2,1,0:T(8,128)(2,1)S(1)} %bitcast.28), channel_id=1, replica_groups=mesh['zlo'=2,'y'=8,'core'=2,'zhi'=4,'x'=4] {'zhi'}, dimensions={0} | all-to-all | bytes 720896 | tf_op jit(solution)/shard_map/all_to_all | solution.py:61
  67.2 0.0 copy-done.3
  67.2 0.0 copy-done.5
  67.2 0.7 shard_map.111
  67.9 14.6 %all_to_all.33 = bf16[4,16,2816]{2,1,0:T(8,128)(2,1)S(1)} all-to-all(bf16[4,16,2816]{2,1,0:T(8,128)(2,1)S(1)} %shard_map.111), channel_id=1, replica_groups=mesh['zlo'=2,'y'=8,'core'=2,'zhi'=4,'x'=4] {'zhi'}, dimensions={0} | all-to-all | bytes 720896 | tf_op jit(solution)/shard_map/all_to_all | solution.py:211
  82.6 0.1 broadcast_in_dim.15
  82.7 17.2 %all_to_all.34 = bf16[4,64,2816]{2,1,0:T(8,128)(2,1)S(1)} all-to-all(bf16[4,64,2816]{2,1,0:T(8,128)(2,1)S(1)} %broadcast_in_dim.15), channel_id=1, replica_groups=mesh['zlo'=2,'y'=8,'core'=2,'zhi'=4,'x'=4] {'x'}, dimensions={0} | all-to-all | bytes 2883584 | tf_op jit(solution)/shard_map/all_to_all | solution.py:32
  99.8 1.8 %shard_map.112 = (f32[128,1152]{1,0:T(8,128)S(1)}, f32[128,1152]{1,0:T(8,128)S(1)}) custom-call(s32[2]{0:T(128)S(1)} %copy-done.5, bf16[256,2816]{1,0:T(8,128)(2,1)S(1)} %bitcast.20, bf16[512,896]{1,0:T(8,128)(2,1)S(1)} %copy-done.2, bf16[512,896]{1,0:T(8,128)(2,1)S(1)} %copy-done.1, bf16[896,512]{1,0:T(8,128)(2,1)S(1)} %copy-done, bf16[128,896]{1,0:T(8,128)(2,1)S(1)} %bitcast.23), custom_call_target="tpu_custom_call" | custom-call | tf_op jit(solution)/shard_map/pallas_call | solution.py:42
  101.7 7.5 %collective-permute-start = (f32[128,1152]{1,0:T(8,128)S(1)}, f32[128,1152]{1,0:T(8,128)S(1)}, u32[]{:S(2)}, u32[]{:S(2)}) collective-permute-start(f32[128,1152]{1,0:T(8,128)S(1)} %get-tuple-element.14), channel_id=1, source_target_pairs={{0,16},{16,0},{1,17},{17,1},{2,18},{18,2},{3,19},{19,3},{4,20},{20... | collective-permute-start | bytes 1769480 | tf_op jit(solution)/shard_map/ppermute | solution.py:221
  109.1 1.0 convolution_multiply_fusion.3
  110.1 0.6 collective-permute-done.came
  110.7 0.1 shard_map.113
  110.8 18.4 %all_to_all.35.came = bf16[16,8,2048]{2,1,0:T(8,128)(2,1)S(1)} all-to-all(bf16[16,8,2048]{2,1,0:T(8,128)(2,1)S(1)} %shard_map.113), channel_id=1, replica_groups=mesh['zlo'=2,'y'=8,'core'=2,'zhi'=4,'x'=4] {'zlo','y'}, dimensions={0} | all-to-all | bytes 1048576 | tf_op jit(solution)/shard_map/all_to_all | solution.py:234
  129.2 0.1 shard_map.114
  129.3 4.3 %all-gather = bf16[128,128]{1,0:T(8,128)(2,1)S(1)} all-gather(bf16[64,128]{1,0:T(8,128)(2,1)S(1)} %get-tuple-element.17), channel_id=2, replica_groups=mesh['zlo'=2,'y'=8,'core'=2,'zhi'=4,'x'=4] {'core'}, dimensions={0}, use_global_device_ids=true | all-gather | bytes 49152 | tf_op jit(solution)/shard_map/all_gather | solution.py:244
  133.6 1.5 %shard_map.115 = (bf16[8,512]{1,0:T(8,128)(2,1)}, bf16[8,512]{1,0:T(8,128)(2,1)}, f32[128,512]{1,0:T(8,128)}) custom-call(s32[2]{0:T(128)S(1)} %copy-done.5, f32[8,1024]{1,0:T(8,128)S(1)} %get-tuple-element.16.sums, bf16[2,64,128]{2,1,0:T(8,128)(2,1)S(1)} %bitcast.26, bf16[256,1024]{1,0:T(8,128)(2,1)S(1)} %all_gather.9.both, bf16[128,512]{1,0:T(8,128)(2,1)S(1)} %bitcast.25), custom_call_target="tpu_custom_call" | custom-call | tf_op jit(solution)/shard_map/pallas_call | solution.py:42
  (3 shorter events, 0.1 us)
Async XLA Ops:
  0.6 23.2 %copy-start.4 = (bf16[2,512,64]{1,2,0:T(8,128)(2,1)S(1)}, bf16[2,512,64]{1,2,0:T(8,128)(2,1)}, u32[]{:S(2)}) copy-start(bf16[2,512,64]{1,2,0:T(8,128)(2,1)} %param.12) | copy-start | bytes 393220
  0.6 23.4 %copy-start.1 = (bf16[512,896]{1,0:T(8,128)(2,1)S(1)}, bf16[512,896]{1,0:T(8,128)(2,1)}, u32[]{:S(2)}) copy-start(bf16[512,896]{1,0:T(8,128)(2,1)} %up.1) | copy-start | bytes 2752516
  19.6 5.0 %copy-start = (bf16[896,512]{1,0:T(8,128)(2,1)S(1)}, bf16[896,512]{1,0:T(8,128)(2,1)}, u32[]{:S(2)}) copy-start(bf16[896,512]{1,0:T(8,128)(2,1)} %down.1) | copy-start | bytes 2752516
  24.1 1.2 copy-start.2
  48.8 18.3 %copy-start.3 = (bf16[2,64,896]{2,1,0:T(8,128)(2,1)S(1)}, bf16[2,64,896]{2,1,0:T(8,128)(2,1)}, u32[]{:S(2)}) copy-start(bf16[2,64,896]{2,1,0:T(8,128)(2,1)} %param.13) | copy-start | bytes 688132
  48.9 18.3 %copy-start.5 = (s32[2]{0:T(128)S(1)}, s32[2]{0:T(128)}, u32[]{:S(2)}) copy-start(s32[2]{0:T(128)} %adapter_of_block.5) | copy-start | bytes 28
  101.7 9.1 %collective-permute-start = (f32[128,1152]{1,0:T(8,128)S(1)}, f32[128,1152]{1,0:T(8,128)S(1)}, u32[]{:S(2)}, u32[]{:S(2)}) collective-permute-start(f32[128,1152]{1,0:T(8,128)S(1)} %get-tuple-element.14), channel_id=1, source_target_pairs={{0,16},{16,0},{1,17},{17,1},{2,18},{18,2},{3,19},{19,3},{4,20},{20... | collective-permute-start | bytes 1769480 | tf_op jit(solution)/shard_map/ppermute | solution.py:221

commit v11 on v10

--- a/solution.py
+++ b/solution.py
@@ -58,11 +58,7 @@
 def scatter_sum(value, axis):
     count = lax.axis_size(axis)
     blocks = value.astype(jnp.float16).reshape(count, value.shape[0] // count, -1)
-    came = lax.all_to_all(blocks, axis, 0, 0).astype(f32)
-    total = came[0]
-    for peer in range(1, count):
-        total = total + came[peer]
-    return total
+    return jnp.sum(lax.all_to_all(blocks, axis, 0, 0).astype(f32), axis=0)
 
 
 def elementwise(adapter_of_block, scaled, second, rows):
@@ -97,7 +93,7 @@
 
     def put(at, size):
         own[:, at : at + size] = product_of[pl.ds(own_start, half), :size]
-        other[:, at : at + size] = product_of[pl.ds(other_start, half), :size]
+        other[:, at : at + size] = product_of[pl.ds(other_start, half), :size].astype(bf16)
 
     grad_up = rows[:, 2 * units : 3 * units]
     value = adapter_scale * trailing_product(grad_up, second[...])
@@ -119,7 +115,7 @@
 
 
 def core_sum(own, came, sent):
-    total = own[...] + came[...]
+    total = own[...] + came[...].astype(f32)
     peers, rows, _ = sent.shape
     columns = 128
     sums = total.shape[1] - columns
@@ -213,7 +209,10 @@
 
     own, other = on_chip(
         last_products,
-        [jax.ShapeDtypeStruct((row_total // 2, 2 * width + columns), f32)] * 2,
+        [
+            jax.ShapeDtypeStruct((row_total // 2, 2 * width + columns), kind)
+            for kind in (f32, bf16)
+        ],
         [adapter_of_block],
         [rows, gate_weight, upward_weight, down_weight, second],
         scratch=[pltpu.VMEM((row_total, 256), f32)],

time: 135 us -> 135 us (level)
  no operation moved by 1% of the time
where the time goes in v11:
time: 135 us; the launch traced here: 134 us
  blocking collectives  117 us (87%)
  starting transfers between devices  7.46 us (6%)
  Pallas kernels  4.15 us (3%)
  matrix products  2.61 us (2%)
  other arithmetic  1.57 us (1%)
    all_to_all x2, blocking collectives, scatter_sum(): return jnp.sum(lax.all_to_all(blocks, axis, 0, 0).astype(f32), axis=0)  40.5 us
    all_to_all x2, blocking collectives, gather_rows(): lax.all_to_all(blocks, axis, 0, 0)  35.2 us
    all_to_all x1, blocking collectives, on_device(): came = lax.all_to_all(sent, PIPE_LINKS, 0, 0)  18.4 us
    all_to_all x1, blocking collectives, on_device(): rows = lax.all_to_all(rows, 'zhi', 0, 0).reshape(row_total // 4, -1)  14.6 us
    ppermute x1, starting transfers between devices, on_device(): came = lax.ppermute(other, 'core', [(0, 1), (1, 0)])  7.46 us
    all_gather x1, blocking collectives, on_device(): packed = lax.all_gather(packed, 'core', axis=0)  4.3 us
    all_gather x1, blocking collectives, on_device(): lax.all_gather(gather_rows(both, PIPE_LINKS), 'core', axis=0, tiled=True)  4.27 us
    pallas_call x5, Pallas kernels, on_chip(): pl.pallas_call(kernel, out_shape=out_shape, in_specs=[pl.BlockSpec(memory...  4.15 us
  transfers between devices with their start and end apart: 1, of which 1 were waited for; matrix products, arithmetic and copies ran while one was open for 1% of the time, Pallas kernels for 0%

profile of v11, /device:TPU:1, one launch (start us, length us, event | category | flops | bytes accessed | tf_op | source)
XLA Modules:
  0.0 134.5 jit_solution(4390494788345426102)
XLA Ops:
  0.6 0.0 copy-start.4
  0.6 0.0 copy-start.1
  0.7 0.8 pad_maximum_fusion.1
  1.5 18.1 %all_to_all.30 = bf16[16,8,1024]{2,1,0:T(8,128)(2,1)S(1)} all-to-all(bf16[16,8,1024]{2,1,0:T(8,128)(2,1)S(1)} %broadcast_in_dim.6), channel_id=1, replica_groups=mesh['zlo'=2,'y'=8,'core'=2,'zhi'=4,'x'=4] {'zlo','y'}, dimensions={0} | all-to-all | bytes 524288 | tf_op jit(solution)/shard_map/all_to_all | solution.py:32
  19.6 0.0 copy-start
  19.6 4.3 %all_gather.9.both = bf16[256,1024]{1,0:T(8,128)(2,1)S(1)} all-gather(bf16[128,1024]{1,0:T(8,128)(2,1)S(1)} %bitcast.28), channel_id=1, replica_groups=mesh['zlo'=2,'y'=8,'core'=2,'zhi'=4,'x'=4] {'core'}, dimensions={0}, use_global_device_ids=true | all-gather | bytes 786432 | tf_op jit(solution)/shard_map/all_gather | solution.py:185
  23.8 0.0 copy-done.4
  23.9 0.2 fusion.3
  24.1 0.0 copy-done.1
  24.1 0.0 copy-start.2
  24.1 0.4 fusion.1
  24.6 0.0 copy-done
  24.6 0.5 fusion.2
  25.0 0.2 copy-done.2
  25.3 0.4 fusion
  25.7 0.5 pad_maximum_fusion
  26.2 22.2 %all_to_all.31 = f16[4,64,2816]{2,1,0:T(8,128)(2,1)S(1)} all-to-all(f16[4,64,2816]{2,1,0:T(8,128)(2,1)S(1)} %bitcast.25), channel_id=1, replica_groups=mesh['zlo'=2,'y'=8,'core'=2,'zhi'=4,'x'=4] {'x'}, dimensions={0} | all-to-all | bytes 2883584 | tf_op jit(solution)/shard_map/all_to_all | solution.py:61
  48.5 0.2 convert_reduce_fusion
  48.7 0.0 copy-start.3
  48.7 0.0 copy-start.5
  48.7 18.2 %all_to_all.32 = f16[4,16,2816]{2,1,0:T(8,128)(2,1)S(1)} all-to-all(f16[4,16,2816]{2,1,0:T(8,128)(2,1)S(1)} %bitcast.27), channel_id=1, replica_groups=mesh['zlo'=2,'y'=8,'core'=2,'zhi'=4,'x'=4] {'zhi'}, dimensions={0} | all-to-all | bytes 720896 | tf_op jit(solution)/shard_map/all_to_all | solution.py:61
  67.0 0.0 copy-done.3
  67.0 0.0 copy-done.5
  67.0 0.7 shard_map.111
  67.7 14.6 %all_to_all.33 = bf16[4,16,2816]{2,1,0:T(8,128)(2,1)S(1)} all-to-all(bf16[4,16,2816]{2,1,0:T(8,128)(2,1)S(1)} %shard_map.111), channel_id=1, replica_groups=mesh['zlo'=2,'y'=8,'core'=2,'zhi'=4,'x'=4] {'zhi'}, dimensions={0} | all-to-all | bytes 720896 | tf_op jit(solution)/shard_map/all_to_all | solution.py:207
  82.4 0.1 broadcast_in_dim.15
  82.5 17.2 %all_to_all.34 = bf16[4,64,2816]{2,1,0:T(8,128)(2,1)S(1)} all-to-all(bf16[4,64,2816]{2,1,0:T(8,128)(2,1)S(1)} %broadcast_in_dim.15), channel_id=1, replica_groups=mesh['zlo'=2,'y'=8,'core'=2,'zhi'=4,'x'=4] {'x'}, dimensions={0} | all-to-all | bytes 2883584 | tf_op jit(solution)/shard_map/all_to_all | solution.py:32
  99.6 1.9 %shard_map.112 = (f32[128,1152]{1,0:T(8,128)S(1)}, bf16[128,1152]{1,0:T(8,128)(2,1)S(1)}) custom-call(s32[2]{0:T(128)S(1)} %copy-done.5, bf16[256,2816]{1,0:T(8,128)(2,1)S(1)} %bitcast.18, bf16[512,896]{1,0:T(8,128)(2,1)S(1)} %copy-done.2, bf16[512,896]{1,0:T(8,128)(2,1)S(1)} %copy-done.1, bf16[896,512]{1,0:T(8,128)(2,1)S(1)} %copy-done, ...), custom_call_target="tpu_custom_call" | custom-call | tf_op jit(solution)/shard_map/pallas_call | solution.py:42
  101.5 7.5 %collective-permute-start = (bf16[128,1152]{1,0:T(8,128)(2,1)S(1)}, bf16[128,1152]{1,0:T(8,128)(2,1)S(1)}, u32[]{:S(2)}, u32[]{:S(2)}) collective-permute-start(bf16[128,1152]{1,0:T(8,128)(2,1)S(1)} %get-tuple-element.14), channel_id=1, source_target_pairs={{0,16},{16,0},{1,17},{17,1},{2,18},{18,2},{3,19},{19,3},{4,20},{20... | collective-permute-start | bytes 884744 | tf_op jit(solution)/shard_map/ppermute | solution.py:220
  109.0 1.0 convolution_multiply_fusion.3
  110.0 0.2 collective-permute-done.came
  110.1 0.1 shard_map.113
  110.2 18.4 %all_to_all.35.came = bf16[16,8,2048]{2,1,0:T(8,128)(2,1)S(1)} all-to-all(bf16[16,8,2048]{2,1,0:T(8,128)(2,1)S(1)} %shard_map.113), channel_id=1, replica_groups=mesh['zlo'=2,'y'=8,'core'=2,'zhi'=4,'x'=4] {'zlo','y'}, dimensions={0} | all-to-all | bytes 1048576 | tf_op jit(solution)/shard_map/all_to_all | solution.py:233
  128.6 0.1 shard_map.114
  128.7 4.3 %all-gather = bf16[128,128]{1,0:T(8,128)(2,1)S(1)} all-gather(bf16[64,128]{1,0:T(8,128)(2,1)S(1)} %get-tuple-element.17), channel_id=2, replica_groups=mesh['zlo'=2,'y'=8,'core'=2,'zhi'=4,'x'=4] {'core'}, dimensions={0}, use_global_device_ids=true | all-gather | bytes 49152 | tf_op jit(solution)/shard_map/all_gather | solution.py:243
  133.0 1.5 %shard_map.115 = (bf16[8,512]{1,0:T(8,128)(2,1)}, bf16[8,512]{1,0:T(8,128)(2,1)}, f32[128,512]{1,0:T(8,128)}) custom-call(s32[2]{0:T(128)S(1)} %copy-done.5, f32[8,1024]{1,0:T(8,128)S(1)} %get-tuple-element.16.sums, bf16[2,64,128]{2,1,0:T(8,128)(2,1)S(1)} %bitcast.24, bf16[256,1024]{1,0:T(8,128)(2,1)S(1)} %all_gather.9.both, bf16[128,512]{1,0:T(8,128)(2,1)S(1)} %bitcast.23), custom_call_target="tpu_custom_call" | custom-call | tf_op jit(solution)/shard_map/pallas_call | solution.py:42
  (3 shorter events, 0.1 us)
Async XLA Ops:
  0.6 23.2 %copy-start.4 = (bf16[2,512,64]{1,2,0:T(8,128)(2,1)S(1)}, bf16[2,512,64]{1,2,0:T(8,128)(2,1)}, u32[]{:S(2)}) copy-start(bf16[2,512,64]{1,2,0:T(8,128)(2,1)} %param.12) | copy-start | bytes 393220
  0.6 23.4 %copy-start.1 = (bf16[512,896]{1,0:T(8,128)(2,1)S(1)}, bf16[512,896]{1,0:T(8,128)(2,1)}, u32[]{:S(2)}) copy-start(bf16[512,896]{1,0:T(8,128)(2,1)} %up.1) | copy-start | bytes 2752516
  19.6 5.0 %copy-start = (bf16[896,512]{1,0:T(8,128)(2,1)S(1)}, bf16[896,512]{1,0:T(8,128)(2,1)}, u32[]{:S(2)}) copy-start(bf16[896,512]{1,0:T(8,128)(2,1)} %down.1) | copy-start | bytes 2752516
  24.1 1.2 copy-start.2
  48.7 18.3 %copy-start.3 = (bf16[2,64,896]{2,1,0:T(8,128)(2,1)S(1)}, bf16[2,64,896]{2,1,0:T(8,128)(2,1)}, u32[]{:S(2)}) copy-start(bf16[2,64,896]{2,1,0:T(8,128)(2,1)} %param.13) | copy-start | bytes 688132
  48.7 18.3 %copy-start.5 = (s32[2]{0:T(128)S(1)}, s32[2]{0:T(128)}, u32[]{:S(2)}) copy-start(s32[2]{0:T(128)} %adapter_of_block.5) | copy-start | bytes 28
  101.5 8.7 %collective-permute-start = (bf16[128,1152]{1,0:T(8,128)(2,1)S(1)}, bf16[128,1152]{1,0:T(8,128)(2,1)S(1)}, u32[]{:S(2)}, u32[]{:S(2)}) collective-permute-start(bf16[128,1152]{1,0:T(8,128)(2,1)S(1)} %get-tuple-element.14), channel_id=1, source_target_pairs={{0,16},{16,0},{1,17},{17,1},{2,18},{18,2},{3,19},{19,3},{4,20},{20... | collective-permute-start | bytes 884744 | tf_op jit(solution)/shard_map/ppermute | solution.py:220

commit v12 on v11

--- a/solution.py
+++ b/solution.py
@@ -9,7 +9,7 @@
 TENSOR = ("zhi", "x")
 PIPE_LINKS = ("zlo", "y")
 adapter_scale = 0.5
-sent_scale = 16.0
+sent_scale = 64.0
 bf16 = jnp.bfloat16
 f32 = jnp.float32
 
@@ -38,14 +38,13 @@
     )
 
 
-def on_chip(kernel, out_shape, scalars, arrays, scratch=()):
+def on_chip(kernel, out_shape, scalars, arrays):
     return pl.pallas_call(
         kernel,
         out_shape=out_shape,
         in_specs=[pl.BlockSpec(memory_space=pltpu.SMEM)] * len(scalars)
         + [pl.BlockSpec(memory_space=pltpu.VMEM)] * len(arrays),
         out_specs=[pl.BlockSpec(memory_space=pltpu.VMEM)] * len(out_shape),
-        scratch_shapes=scratch,
         compiler_params=pltpu.CompilerParams(vmem_limit_bytes=40 * 2**20),
     )(*scalars, *arrays)
 
@@ -83,35 +82,31 @@
         rows[copy, :, 3 * units :] = low
 
 
-def last_products(adapter_of_block, rows, gate, up, down, second, own, other, product_of):
+def last_products(adapter_of_block, rows, gate, up, down, second, own, other):
     width, units = gate.shape
     columns = second.shape[0]
     half, quarter = rows.shape[0] // 2, rows.shape[0] // 4
-    core = lax.axis_index("core")
-    own_start = pl.multiple_of(core * half, half)
-    other_start = pl.multiple_of((1 - core) * half, half)
-
-    def put(at, size):
-        own[:, at : at + size] = product_of[pl.ds(own_start, half), :size]
-        other[:, at : at + size] = product_of[pl.ds(other_start, half), :size].astype(bf16)
+    is_first = lax.axis_index("core") == 0
+
+    def put(value, at):
+        low_half, high_half = value[:half], value[half:]
+        columns_at = slice(at, at + value.shape[1])
+        own[:, columns_at] = jnp.where(is_first, low_half, high_half)
+        other[:, columns_at] = jnp.where(is_first, high_half, low_half).astype(bf16)
 
     grad_up = rows[:, 2 * units : 3 * units]
     value = adapter_scale * trailing_product(grad_up, second[...])
-    for block in range(4):
-        adapter = adapter_of_block[block % 2]
-        part = value[block * quarter : (block + 1) * quarter, :]
-        part = jnp.where(chosen_columns(adapter, quarter, columns, columns // 2), part, 0.0)
-        product_of[pl.ds(block * quarter, quarter), :columns] = part
-    put(2 * width, columns)
+    masks = [
+        chosen_columns(adapter_of_block[block % 2], quarter, columns, columns // 2)
+        for block in range(4)
+    ]
+    put(jnp.where(jnp.concatenate(masks, axis=0), value, 0.0), 2 * width)
     grad_gate = rows[:, units : 2 * units]
     for at in range(0, width, 256):
-        product_of[...] = trailing_product(grad_gate, gate[at : at + 256, :]) + trailing_product(
-            grad_up, up[at : at + 256, :]
-        )
-        put(width + at, 256)
+        value = trailing_product(grad_gate, gate[at : at + 256, :])
+        put(value + trailing_product(grad_up, up[at : at + 256, :]), width + at)
     for at in range(0, width, 256):
-        product_of[...] = product(rows[:, :units], down[:, at : at + 256])
-        put(at, 256)
+        put(product(rows[:, :units], down[:, at : at + 256]), at)
 
 
 def core_sum(own, came, sent):
@@ -215,7 +210,6 @@
         ],
         [adapter_of_block],
         [rows, gate_weight, upward_weight, down_weight, second],
-        scratch=[pltpu.VMEM((row_total, 256), f32)],
     )
     came = lax.ppermute(other, "core", [(0, 1), (1, 0)])
     grad_up_all = rows[:, 2 * hidden_units : 3 * hidden_units]

time: 135 us -> 135 us (level)
  no operation moved by 1% of the time
where the time goes in v12:
time: 135 us; the launch traced here: 134 us
  blocking collectives  117 us (87%)
  starting transfers between devices  7.46 us (6%)
  Pallas kernels  3.95 us (3%)
  matrix products  2.6 us (2%)
  other arithmetic  1.57 us (1%)
    all_to_all x2, blocking collectives, scatter_sum(): return jnp.sum(lax.all_to_all(blocks, axis, 0, 0).astype(f32), axis=0)  40.5 us
    all_to_all x2, blocking collectives, gather_rows(): lax.all_to_all(blocks, axis, 0, 0)  35.2 us
    all_to_all x1, blocking collectives, on_device(): came = lax.all_to_all(sent, PIPE_LINKS, 0, 0)  18.4 us
    all_to_all x1, blocking collectives, on_device(): rows = lax.all_to_all(rows, 'zhi', 0, 0).reshape(row_total // 4, -1)  14.6 us
    ppermute x1, starting transfers between devices, on_device(): came = lax.ppermute(other, 'core', [(0, 1), (1, 0)])  7.46 us
    all_gather x1, blocking collectives, on_device(): packed = lax.all_gather(packed, 'core', axis=0)  4.3 us
    all_gather x1, blocking collectives, on_device(): lax.all_gather(gather_rows(both, PIPE_LINKS), 'core', axis=0, tiled=True)  4.27 us
    pallas_call x5, Pallas kernels, on_chip(): pl.pallas_call(kernel, out_shape=out_shape, in_specs=[pl.BlockSpec(memory...  3.95 us
  transfers between devices with their start and end apart: 1, of which 1 were waited for; matrix products, arithmetic and copies ran while one was open for 1% of the time, Pallas kernels for 0%

profile of v12, /device:TPU:1, one launch (start us, length us, event | category | flops | bytes accessed | tf_op | source)
XLA Modules:
  0.0 134.3 jit_solution(7794073427729188163)
XLA Ops:
  0.6 0.0 copy-start.4
  0.6 0.0 copy-start.1
  0.7 0.8 pad_maximum_fusion.1
  1.5 18.1 %all_to_all.30 = bf16[16,8,1024]{2,1,0:T(8,128)(2,1)S(1)} all-to-all(bf16[16,8,1024]{2,1,0:T(8,128)(2,1)S(1)} %broadcast_in_dim.6), channel_id=1, replica_groups=mesh['zlo'=2,'y'=8,'core'=2,'zhi'=4,'x'=4] {'zlo','y'}, dimensions={0} | all-to-all | bytes 524288 | tf_op jit(solution)/shard_map/all_to_all | solution.py:32
  19.6 0.0 copy-start
  19.6 4.3 %all_gather.9.both = bf16[256,1024]{1,0:T(8,128)(2,1)S(1)} all-gather(bf16[128,1024]{1,0:T(8,128)(2,1)S(1)} %bitcast.28), channel_id=1, replica_groups=mesh['zlo'=2,'y'=8,'core'=2,'zhi'=4,'x'=4] {'core'}, dimensions={0}, use_global_device_ids=true | all-gather | bytes 786432 | tf_op jit(solution)/shard_map/all_gather | solution.py:180
  23.8 0.0 copy-done.4
  23.9 0.2 fusion.3
  24.1 0.0 copy-done.1
  24.1 0.0 copy-start.2
  24.1 0.4 fusion.1
  24.6 0.0 copy-done
  24.6 0.5 fusion.2
  25.0 0.2 copy-done.2
  25.3 0.4 fusion
  25.7 0.5 pad_maximum_fusion
  26.2 22.2 %all_to_all.31 = f16[4,64,2816]{2,1,0:T(8,128)(2,1)S(1)} all-to-all(f16[4,64,2816]{2,1,0:T(8,128)(2,1)S(1)} %bitcast.25), channel_id=1, replica_groups=mesh['zlo'=2,'y'=8,'core'=2,'zhi'=4,'x'=4] {'x'}, dimensions={0} | all-to-all | bytes 2883584 | tf_op jit(solution)/shard_map/all_to_all | solution.py:60
  48.5 0.2 convert_reduce_fusion
  48.7 0.0 copy-start.3
  48.7 0.0 copy-start.5
  48.7 18.2 %all_to_all.32 = f16[4,16,2816]{2,1,0:T(8,128)(2,1)S(1)} all-to-all(f16[4,16,2816]{2,1,0:T(8,128)(2,1)S(1)} %bitcast.27), channel_id=1, replica_groups=mesh['zlo'=2,'y'=8,'core'=2,'zhi'=4,'x'=4] {'zhi'}, dimensions={0} | all-to-all | bytes 720896 | tf_op jit(solution)/shard_map/all_to_all | solution.py:60
  67.0 0.0 copy-done.3
  67.0 0.0 copy-done.5
  67.0 0.7 shard_map.111
  67.7 14.6 %all_to_all.33 = bf16[4,16,2816]{2,1,0:T(8,128)(2,1)S(1)} all-to-all(bf16[4,16,2816]{2,1,0:T(8,128)(2,1)S(1)} %shard_map.111), channel_id=1, replica_groups=mesh['zlo'=2,'y'=8,'core'=2,'zhi'=4,'x'=4] {'zhi'}, dimensions={0} | all-to-all | bytes 720896 | tf_op jit(solution)/shard_map/all_to_all | solution.py:202
  82.4 0.1 broadcast_in_dim.15
  82.5 17.2 %all_to_all.34 = bf16[4,64,2816]{2,1,0:T(8,128)(2,1)S(1)} all-to-all(bf16[4,64,2816]{2,1,0:T(8,128)(2,1)S(1)} %broadcast_in_dim.15), channel_id=1, replica_groups=mesh['zlo'=2,'y'=8,'core'=2,'zhi'=4,'x'=4] {'x'}, dimensions={0} | all-to-all | bytes 2883584 | tf_op jit(solution)/shard_map/all_to_all | solution.py:32
  99.6 1.7 %shard_map.112 = (f32[128,1152]{1,0:T(8,128)S(1)}, bf16[128,1152]{1,0:T(8,128)(2,1)S(1)}) custom-call(s32[2]{0:T(128)S(1)} %copy-done.5, bf16[256,2816]{1,0:T(8,128)(2,1)S(1)} %bitcast.18, bf16[512,896]{1,0:T(8,128)(2,1)S(1)} %copy-done.2, bf16[512,896]{1,0:T(8,128)(2,1)S(1)} %copy-done.1, bf16[896,512]{1,0:T(8,128)(2,1)S(1)} %copy-done, ...), custom_call_target="tpu_custom_call" | custom-call | tf_op jit(solution)/shard_map/pallas_call | solution.py:42
  101.3 7.5 %collective-permute-start = (bf16[128,1152]{1,0:T(8,128)(2,1)S(1)}, bf16[128,1152]{1,0:T(8,128)(2,1)S(1)}, u32[]{:S(2)}, u32[]{:S(2)}) collective-permute-start(bf16[128,1152]{1,0:T(8,128)(2,1)S(1)} %get-tuple-element.14), channel_id=1, source_target_pairs={{0,16},{16,0},{1,17},{17,1},{2,18},{18,2},{3,19},{19,3},{4,20},{20... | collective-permute-start | bytes 884744 | tf_op jit(solution)/shard_map/ppermute | solution.py:214
  108.8 1.0 convolution_multiply_fusion.3
  109.8 0.2 collective-permute-done.came
  109.9 0.1 shard_map.113
  110.0 18.4 %all_to_all.35.came = bf16[16,8,2048]{2,1,0:T(8,128)(2,1)S(1)} all-to-all(bf16[16,8,2048]{2,1,0:T(8,128)(2,1)S(1)} %shard_map.113), channel_id=1, replica_groups=mesh['zlo'=2,'y'=8,'core'=2,'zhi'=4,'x'=4] {'zlo','y'}, dimensions={0} | all-to-all | bytes 1048576 | tf_op jit(solution)/shard_map/all_to_all | solution.py:227
  128.4 0.1 shard_map.114
  128.5 4.3 %all-gather = bf16[128,128]{1,0:T(8,128)(2,1)S(1)} all-gather(bf16[64,128]{1,0:T(8,128)(2,1)S(1)} %get-tuple-element.17), channel_id=2, replica_groups=mesh['zlo'=2,'y'=8,'core'=2,'zhi'=4,'x'=4] {'core'}, dimensions={0}, use_global_device_ids=true | all-gather | bytes 49152 | tf_op jit(solution)/shard_map/all_gather | solution.py:237
  132.8 1.5 %shard_map.115 = (bf16[8,512]{1,0:T(8,128)(2,1)}, bf16[8,512]{1,0:T(8,128)(2,1)}, f32[128,512]{1,0:T(8,128)}) custom-call(s32[2]{0:T(128)S(1)} %copy-done.5, f32[8,1024]{1,0:T(8,128)S(1)} %get-tuple-element.16.sums, bf16[2,64,128]{2,1,0:T(8,128)(2,1)S(1)} %bitcast.24, bf16[256,1024]{1,0:T(8,128)(2,1)S(1)} %all_gather.9.both, bf16[128,512]{1,0:T(8,128)(2,1)S(1)} %bitcast.23), custom_call_target="tpu_custom_call" | custom-call | tf_op jit(solution)/shard_map/pallas_call | solution.py:42
  (3 shorter events, 0.1 us)
Async XLA Ops:
  0.6 23.2 %copy-start.4 = (bf16[2,512,64]{1,2,0:T(8,128)(2,1)S(1)}, bf16[2,512,64]{1,2,0:T(8,128)(2,1)}, u32[]{:S(2)}) copy-start(bf16[2,512,64]{1,2,0:T(8,128)(2,1)} %param.12) | copy-start | bytes 393220
  0.6 23.4 %copy-start.1 = (bf16[512,896]{1,0:T(8,128)(2,1)S(1)}, bf16[512,896]{1,0:T(8,128)(2,1)}, u32[]{:S(2)}) copy-start(bf16[512,896]{1,0:T(8,128)(2,1)} %up.1) | copy-start | bytes 2752516
  19.6 5.0 %copy-start = (bf16[896,512]{1,0:T(8,128)(2,1)S(1)}, bf16[896,512]{1,0:T(8,128)(2,1)}, u32[]{:S(2)}) copy-start(bf16[896,512]{1,0:T(8,128)(2,1)} %down.1) | copy-start | bytes 2752516
  24.1 1.2 copy-start.2
  48.7 18.3 %copy-start.3 = (bf16[2,64,896]{2,1,0:T(8,128)(2,1)S(1)}, bf16[2,64,896]{2,1,0:T(8,128)(2,1)}, u32[]{:S(2)}) copy-start(bf16[2,64,896]{2,1,0:T(8,128)(2,1)} %param.13) | copy-start | bytes 688132
  48.7 18.3 %copy-start.5 = (s32[2]{0:T(128)S(1)}, s32[2]{0:T(128)}, u32[]{:S(2)}) copy-start(s32[2]{0:T(128)} %adapter_of_block.5) | copy-start | bytes 28
  101.3 8.7 %collective-permute-start = (bf16[128,1152]{1,0:T(8,128)(2,1)S(1)}, bf16[128,1152]{1,0:T(8,128)(2,1)S(1)}, u32[]{:S(2)}, u32[]{:S(2)}) collective-permute-start(bf16[128,1152]{1,0:T(8,128)(2,1)S(1)} %get-tuple-element.14), channel_id=1, source_target_pairs={{0,16},{16,0},{1,17},{17,1},{2,18},{18,2},{3,19},{19,3},{4,20},{20... | collective-permute-start | bytes 884744 | tf_op jit(solution)/shard_map/ppermute | solution.py:214

commit v13 on v12

--- a/solution.py
+++ b/solution.py
@@ -102,11 +102,11 @@
     ]
     put(jnp.where(jnp.concatenate(masks, axis=0), value, 0.0), 2 * width)
     grad_gate = rows[:, units : 2 * units]
-    for at in range(0, width, 256):
-        value = trailing_product(grad_gate, gate[at : at + 256, :])
-        put(value + trailing_product(grad_up, up[at : at + 256, :]), width + at)
-    for at in range(0, width, 256):
-        put(product(rows[:, :units], down[:, at : at + 256]), at)
+    for at in range(0, width, 512):
+        value = trailing_product(grad_gate, gate[at : at + 512, :])
+        put(value + trailing_product(grad_up, up[at : at + 512, :]), width + at)
+    for at in range(0, width, 512):
+        put(product(rows[:, :units], down[:, at : at + 512]), at)
 
 
 def core_sum(own, came, sent):
@@ -136,7 +136,20 @@
     ).astype(bf16)
 
 
-def outputs(adapter_of_block, sums, packed, both, first, mixed, grad_tokens, grad_a):
+def outputs(
+    adapter_of_block,
+    sums,
+    packed,
+    both,
+    first,
+    mixed_far,
+    grad_tokens_far,
+    grad_a_far,
+    mixed,
+    grad_tokens,
+    grad_a,
+    done,
+):
     rows = sums.shape[0]
     columns, width = first.shape
     cores, quarter, _ = packed.shape
@@ -144,21 +157,30 @@
     masks = [
         chosen_columns(adapter_of_block[block], quarter, columns, rank) for block in range(2)
     ]
+    low_back = jnp.concatenate(
+        [
+            jnp.where(mask, packed[at].astype(f32), 0.0).astype(bf16)
+            for at in range(cores)
+            for mask in masks
+        ],
+        axis=0,
+    )
+    grad_a[...] = leading_product(low_back, both[:, :width])
+    write_grad_a = pltpu.make_async_copy(grad_a, grad_a_far, done.at[0])
+    write_grad_a.start()
+    mixed[...] = sums[:, :width].astype(bf16)
+    write_mixed = pltpu.make_async_copy(mixed, mixed_far, done.at[1])
+    write_mixed.start()
     core, zlo, y = (lax.axis_index(name) for name in ("core", "zlo", "y"))
-    mixed[...] = sums[:, :width].astype(bf16)
     low_own = packed[core, pl.ds(pl.multiple_of(y * rows, rows), rows), :]
     own_mask = chosen_columns(adapter_of_block[zlo], rows, columns, rank)
     low_own = jnp.where(own_mask, low_own.astype(f32), 0.0).astype(bf16)
     grad_tokens[...] = (sums[:, width:] + product(low_own, first[...])).astype(bf16)
-    low_back = jnp.concatenate(
-        [
-            jnp.where(mask, packed[at].astype(f32), 0.0).astype(bf16)
-            for at in range(cores)
-            for mask in masks
-        ],
-        axis=0,
-    )
-    grad_a[...] = leading_product(low_back, both[:, :width])
+    write_grad_tokens = pltpu.make_async_copy(grad_tokens, grad_tokens_far, done.at[2])
+    write_grad_tokens.start()
+    write_grad_a.wait()
+    write_mixed.wait()
+    write_grad_tokens.wait()
 
 
 def on_device(
@@ -235,16 +257,20 @@
         [came],
     )
     packed = lax.all_gather(packed, "core", axis=0)
-    mixed, grad_tokens, grad_a = on_chip(
+    results = [
+        jax.ShapeDtypeStruct((tokens.shape[0], width), bf16),
+        jax.ShapeDtypeStruct((tokens.shape[0], width), bf16),
+        jax.ShapeDtypeStruct((columns, width), f32),
+    ]
+    mixed, grad_tokens, grad_a = pl.pallas_call(
         outputs,
-        [
-            jax.ShapeDtypeStruct((tokens.shape[0], width), bf16),
-            jax.ShapeDtypeStruct((tokens.shape[0], width), bf16),
-            jax.ShapeDtypeStruct((columns, width), f32),
-        ],
-        [adapter_of_block],
-        [sums, packed, both, first_flat],
-    )
+        out_shape=results,
+        in_specs=[pl.BlockSpec(memory_space=pltpu.SMEM)]
+        + [pl.BlockSpec(memory_space=pltpu.VMEM)] * 4,
+        out_specs=[pl.BlockSpec(memory_space=pl.ANY)] * 3,
+        scratch_shapes=[pltpu.VMEM(result.shape, result.dtype) for result in results]
+        + [pltpu.SemaphoreType.DMA((3,))],
+    )(adapter_of_block, sums, packed, both, first_flat)
     grad_a = jnp.transpose(grad_a.reshape(adapters, rank, width), (0, 2, 1))
     return mixed, grad_tokens, grad_a, grad_b
 

time: 135 us -> 136 us (level)
    pallas_call x0 -> x1, Pallas kernels: none -> 2.06 us  [on_device(): pl.pallas_call(outputs, out_shape=results, in_specs=[pl.BlockSpec(memory_...]
    pallas_call x5 -> x4, Pallas kernels: 3.95 us -> 2.49 us  [on_chip(): pl.pallas_call(kernel, out_shape=out_shape, in_specs=[pl.BlockSpec(memory...]
where the time goes in v13:
time: 136 us
  blocking collectives  117 us (86%)
  starting transfers between devices  7.55 us (6%)
  Pallas kernels  4.55 us (3%)
  matrix products  2.6 us (2%)
  other arithmetic  1.57 us (1%)
    all_to_all x2, blocking collectives, scatter_sum(): return jnp.sum(lax.all_to_all(blocks, axis, 0, 0).astype(f32), axis=0)  40.5 us
    all_to_all x2, blocking collectives, gather_rows(): lax.all_to_all(blocks, axis, 0, 0)  35.2 us
    all_to_all x1, blocking collectives, on_device(): came = lax.all_to_all(sent, PIPE_LINKS, 0, 0)  18.5 us
    all_to_all x1, blocking collectives, on_device(): rows = lax.all_to_all(rows, 'zhi', 0, 0).reshape(row_total // 4, -1)  14.7 us
    ppermute x1, starting transfers between devices, on_device(): came = lax.ppermute(other, 'core', [(0, 1), (1, 0)])  7.55 us
    all_gather x1, blocking collectives, on_device(): packed = lax.all_gather(packed, 'core', axis=0)  4.42 us
    all_gather x1, blocking collectives, on_device(): lax.all_gather(gather_rows(both, PIPE_LINKS), 'core', axis=0, tiled=True)  4.27 us
  transfers between devices with their start and end apart: 1, of which 1 were waited for; matrix products, arithmetic and copies ran while one was open for 1% of the time, Pallas kernels for 0%

profile of v13, /device:TPU:1, one launch (start us, length us, event | category | flops | bytes accessed | tf_op | source)
XLA Modules:
  0.0 135.7 jit_solution(8594543701622220704)
XLA Ops:
  0.6 0.0 copy-start.7
  0.6 0.0 copy-start.1
  0.7 0.8 pad_maximum_fusion.1
  1.5 18.1 %all_to_all.30 = bf16[16,8,1024]{2,1,0:T(8,128)(2,1)S(1)} all-to-all(bf16[16,8,1024]{2,1,0:T(8,128)(2,1)S(1)} %broadcast_in_dim.6), channel_id=1, replica_groups=mesh['zlo'=2,'y'=8,'core'=2,'zhi'=4,'x'=4] {'zlo','y'}, dimensions={0} | all-to-all | bytes 524288 | tf_op jit(solution)/shard_map/all_to_all | solution.py:32
  19.6 0.0 copy-start
  19.6 4.3 %all_gather.9.both = bf16[256,1024]{1,0:T(8,128)(2,1)S(1)} all-gather(bf16[128,1024]{1,0:T(8,128)(2,1)S(1)} %bitcast.25), channel_id=1, replica_groups=mesh['zlo'=2,'y'=8,'core'=2,'zhi'=4,'x'=4] {'core'}, dimensions={0}, use_global_device_ids=true | all-gather | bytes 786432 | tf_op jit(solution)/shard_map/all_gather | solution.py:202
  23.9 0.0 copy-start.6
  23.9 0.0 copy-done.7
  23.9 0.2 fusion.3
  24.1 0.0 copy-done.1
  24.1 0.0 copy-start.2
  24.1 0.4 fusion.1
  24.6 0.0 copy-done
  24.6 0.5 fusion.2
  25.0 0.0 copy-done.6
  25.1 0.2 copy-done.2
  25.3 0.4 fusion
  25.7 0.5 pad_maximum_fusion
  26.2 22.3 %all_to_all.31 = f16[4,64,2816]{2,1,0:T(8,128)(2,1)S(1)} all-to-all(f16[4,64,2816]{2,1,0:T(8,128)(2,1)S(1)} %bitcast.22), channel_id=1, replica_groups=mesh['zlo'=2,'y'=8,'core'=2,'zhi'=4,'x'=4] {'x'}, dimensions={0} | all-to-all | bytes 2883584 | tf_op jit(solution)/shard_map/all_to_all | solution.py:60
  48.5 0.2 convert_reduce_fusion
  48.7 0.0 copy-start.3
  48.7 0.0 copy-start.5
  48.8 18.2 %all_to_all.32 = f16[4,16,2816]{2,1,0:T(8,128)(2,1)S(1)} all-to-all(f16[4,16,2816]{2,1,0:T(8,128)(2,1)S(1)} %bitcast.24), channel_id=1, replica_groups=mesh['zlo'=2,'y'=8,'core'=2,'zhi'=4,'x'=4] {'zhi'}, dimensions={0} | all-to-all | bytes 720896 | tf_op jit(solution)/shard_map/all_to_all | solution.py:60
  67.0 0.0 copy-done.3
  67.0 0.0 copy-done.5
  67.0 0.7 shard_map.111
  67.7 14.7 %all_to_all.33 = bf16[4,16,2816]{2,1,0:T(8,128)(2,1)S(1)} all-to-all(bf16[4,16,2816]{2,1,0:T(8,128)(2,1)S(1)} %shard_map.111), channel_id=1, replica_groups=mesh['zlo'=2,'y'=8,'core'=2,'zhi'=4,'x'=4] {'zhi'}, dimensions={0} | all-to-all | bytes 720896 | tf_op jit(solution)/shard_map/all_to_all | solution.py:224
  82.4 0.1 broadcast_in_dim.15
  82.5 17.1 %all_to_all.34 = bf16[4,64,2816]{2,1,0:T(8,128)(2,1)S(1)} all-to-all(bf16[4,64,2816]{2,1,0:T(8,128)(2,1)S(1)} %broadcast_in_dim.15), channel_id=1, replica_groups=mesh['zlo'=2,'y'=8,'core'=2,'zhi'=4,'x'=4] {'x'}, dimensions={0} | all-to-all | bytes 2883584 | tf_op jit(solution)/shard_map/all_to_all | solution.py:32
  99.5 1.7 %shard_map.112 = (f32[128,1152]{1,0:T(8,128)S(1)}, bf16[128,1152]{1,0:T(8,128)(2,1)S(1)}) custom-call(s32[2]{0:T(128)S(1)} %copy-done.5, bf16[256,2816]{1,0:T(8,128)(2,1)S(1)} %bitcast.18, bf16[512,896]{1,0:T(8,128)(2,1)S(1)} %copy-done.2, bf16[512,896]{1,0:T(8,128)(2,1)S(1)} %copy-done.1, bf16[896,512]{1,0:T(8,128)(2,1)S(1)} %copy-done, ...), custom_call_target="tpu_custom_call" | custom-call | tf_op jit(solution)/shard_map/pallas_call | solution.py:42
  101.2 7.6 %collective-permute-start = (bf16[128,1152]{1,0:T(8,128)(2,1)S(1)}, bf16[128,1152]{1,0:T(8,128)(2,1)S(1)}, u32[]{:S(2)}, u32[]{:S(2)}) collective-permute-start(bf16[128,1152]{1,0:T(8,128)(2,1)S(1)} %get-tuple-element.14), channel_id=1, source_target_pairs={{0,16},{16,0},{1,17},{17,1},{2,18},{18,2},{3,19},{19,3},{4,20},{20... | collective-permute-start | bytes 884744 | tf_op jit(solution)/shard_map/ppermute | solution.py:236
  108.8 1.0 convolution_multiply_fusion.3
  109.8 0.2 collective-permute-done.came
  110.0 0.1 shard_map.113
  110.0 18.5 %all_to_all.35.came = bf16[16,8,2048]{2,1,0:T(8,128)(2,1)S(1)} all-to-all(bf16[16,8,2048]{2,1,0:T(8,128)(2,1)S(1)} %shard_map.113), channel_id=1, replica_groups=mesh['zlo'=2,'y'=8,'core'=2,'zhi'=4,'x'=4] {'zlo','y'}, dimensions={0} | all-to-all | bytes 1048576 | tf_op jit(solution)/shard_map/all_to_all | solution.py:249
  128.5 0.1 shard_map.114
  128.6 0.0 copy-start.4
  128.6 0.6 copy-done.4
  129.2 4.4 %all-gather = bf16[128,128]{1,0:T(8,128)(2,1)} all-gather(bf16[64,128]{1,0:T(8,128)(2,1)S(1)} %get-tuple-element.17), channel_id=2, replica_groups=mesh['zlo'=2,'y'=8,'core'=2,'zhi'=4,'x'=4] {'core'}, dimensions={0}, use_global_device_ids=true | all-gather | bytes 49152 | tf_op jit(solution)/shard_map/all_gather | solution.py:259
  133.6 2.1 %shard_map.115 = (bf16[8,512]{1,0:T(8,128)(2,1)}, bf16[8,512]{1,0:T(8,128)(2,1)}, f32[128,512]{1,0:T(8,128)}) custom-call(s32[2]{0:T(128)} %adapter_of_block.5, f32[8,1024]{1,0:T(8,128)} %copy-done.4, bf16[2,64,128]{2,1,0:T(8,128)(2,1)} %bitcast.29, bf16[256,1024]{1,0:T(8,128)(2,1)} %copy-done.6, bf16[128,512]{1,0:T(8,128)(2,1)} %bitcast.27), custom_call_target="tpu_custom_call" | custom-call | tf_op jit(solution)/shard_map/pallas_call | solution.py:265
  (3 shorter events, 0.1 us)
Async XLA Ops:
  0.6 23.2 %copy-start.7 = (bf16[2,512,64]{1,2,0:T(8,128)(2,1)S(1)}, bf16[2,512,64]{1,2,0:T(8,128)(2,1)}, u32[]{:S(2)}) copy-start(bf16[2,512,64]{1,2,0:T(8,128)(2,1)} %param.12) | copy-start | bytes 393220
  0.6 23.4 %copy-start.1 = (bf16[512,896]{1,0:T(8,128)(2,1)S(1)}, bf16[512,896]{1,0:T(8,128)(2,1)}, u32[]{:S(2)}) copy-start(bf16[512,896]{1,0:T(8,128)(2,1)} %up.1) | copy-start | bytes 2752516
  19.6 5.0 %copy-start = (bf16[896,512]{1,0:T(8,128)(2,1)S(1)}, bf16[896,512]{1,0:T(8,128)(2,1)}, u32[]{:S(2)}) copy-start(bf16[896,512]{1,0:T(8,128)(2,1)} %down.1) | copy-start | bytes 2752516
  23.9 1.2 copy-start.6
  24.1 1.2 copy-start.2
  48.7 18.3 %copy-start.3 = (bf16[2,64,896]{2,1,0:T(8,128)(2,1)S(1)}, bf16[2,64,896]{2,1,0:T(8,128)(2,1)}, u32[]{:S(2)}) copy-start(bf16[2,64,896]{2,1,0:T(8,128)(2,1)} %param.13) | copy-start | bytes 688132
  48.7 18.3 %copy-start.5 = (s32[2]{0:T(128)S(1)}, s32[2]{0:T(128)}, u32[]{:S(2)}) copy-start(s32[2]{0:T(128)} %adapter_of_block.5) | copy-start | bytes 28
  101.2 8.7 %collective-permute-start = (bf16[128,1152]{1,0:T(8,128)(2,1)S(1)}, bf16[128,1152]{1,0:T(8,128)(2,1)S(1)}, u32[]{:S(2)}, u32[]{:S(2)}) collective-permute-start(bf16[128,1152]{1,0:T(8,128)(2,1)S(1)} %get-tuple-element.14), channel_id=1, source_target_pairs={{0,16},{16,0},{1,17},{17,1},{2,18},{18,2},{3,19},{19,3},{4,20},{20... | collective-permute-start | bytes 884744 | tf_op jit(solution)/shard_map/ppermute | solution.py:236
  128.6 0.6 copy-start.4

commit v14 on v12

--- a/solution.py
+++ b/solution.py
@@ -58,6 +58,19 @@
     count = lax.axis_size(axis)
     blocks = value.astype(jnp.float16).reshape(count, value.shape[0] // count, -1)
     return jnp.sum(lax.all_to_all(blocks, axis, 0, 0).astype(f32), axis=0)
+
+
+def first_blocks(tokens_far, cotangent_far, sent, tokens, cotangent, done):
+    fetch_tokens = pltpu.make_async_copy(tokens_far, tokens, done.at[0])
+    fetch_cotangent = pltpu.make_async_copy(cotangent_far, cotangent, done.at[1])
+    fetch_tokens.start()
+    fetch_cotangent.start()
+    fetch_tokens.wait()
+    fetch_cotangent.wait()
+    width = tokens.shape[1]
+    for peer in range(sent.shape[0]):
+        sent[peer, :, :width] = tokens[...]
+        sent[peer, :, width:] = cotangent[...]
 
 
 def elementwise(adapter_of_block, scaled, second, rows):
@@ -176,8 +189,16 @@
     columns = adapters * rank
     second = adapter_second_factors.reshape(columns, hidden_units)
 
-    both = jnp.concatenate([tokens, cotangent], axis=1)
-    both = lax.all_gather(gather_rows(both, PIPE_LINKS), "core", axis=0, tiled=True)
+    peers, pipe_rows = lax.axis_size(PIPE_LINKS), tokens.shape[0]
+    sent = pl.pallas_call(
+        first_blocks,
+        out_shape=jax.ShapeDtypeStruct((peers, pipe_rows, 2 * width), bf16),
+        in_specs=[pl.BlockSpec(memory_space=pl.ANY)] * 2,
+        out_specs=pl.BlockSpec(memory_space=pltpu.VMEM),
+        scratch_shapes=[pltpu.VMEM(tokens.shape, bf16)] * 2 + [pltpu.SemaphoreType.DMA((2,))],
+    )(*(pltpu.with_memory_space_constraint(array, pltpu.HBM) for array in (tokens, cotangent)))
+    both = lax.all_to_all(sent, PIPE_LINKS, 0, 0).reshape(peers * pipe_rows, 2 * width)
+    both = lax.all_gather(both, "core", axis=0, tiled=True)
     token_rows, adjoint_rows = both[:, :width], both[:, width:]
     row_total = both.shape[0]
     all_columns = 3 * hidden_units + columns

time: 135 us -> 136 us (level)
  Pallas kernels: 3.95 us -> 5.51 us
    all_to_all x0 -> x1, blocking collectives: none -> 18.3 us  [on_device(): lax.all_to_all(sent, PIPE_LINKS, 0, 0).reshape(peers * pipe_rows, 2 * width)]
    all_to_all x2 -> x1, blocking collectives: 35.2 us -> 17.3 us  [gather_rows(): lax.all_to_all(blocks, axis, 0, 0)]
    pallas_call x0 -> x1, Pallas kernels: none -> 1.54 us  [on_device(): pl.pallas_call(first_blocks, out_shape=jax.ShapeDtypeStruct((peers, pipe_...]
where the time goes in v14:
time: 136 us; the launch traced here: 135 us
  blocking collectives  118 us (87%)
  starting transfers between devices  7.32 us (5%)
  Pallas kernels  5.51 us (4%)
  matrix products  2.61 us (2%)
    all_to_all x2, blocking collectives, scatter_sum(): return jnp.sum(lax.all_to_all(blocks, axis, 0, 0).astype(f32), axis=0)  40.5 us
    all_to_all x1, blocking collectives, on_device(): lax.all_to_all(sent, PIPE_LINKS, 0, 0).reshape(peers * pipe_rows, 2 * width)  18.3 us
    all_to_all x1, blocking collectives, on_device(): came = lax.all_to_all(sent, PIPE_LINKS, 0, 0)  18.3 us
    all_to_all x1, blocking collectives, gather_rows(): lax.all_to_all(blocks, axis, 0, 0)  17.3 us
    all_to_all x1, blocking collectives, on_device(): rows = lax.all_to_all(rows, 'zhi', 0, 0).reshape(row_total // 4, -1)  14.7 us
    ppermute x1, starting transfers between devices, on_device(): came = lax.ppermute(other, 'core', [(0, 1), (1, 0)])  7.32 us
    all_gather x1, blocking collectives, on_device(): packed = lax.all_gather(packed, 'core', axis=0)  4.3 us
    all_gather x1, blocking collectives, on_device(): both = lax.all_gather(both, 'core', axis=0, tiled=True)  4.27 us
  transfers between devices with their start and end apart: 1, of which 1 were waited for; matrix products, arithmetic and copies ran while one was open for 1% of the time, Pallas kernels for 0%

profile of v14, /device:TPU:1, one launch (start us, length us, event | category | flops | bytes accessed | tf_op | source)
XLA Modules:
  0.0 135.2 jit_solution(15424450273279991624)
XLA Ops:
  0.6 0.0 copy-start.4
  0.6 0.0 copy-start.1
  0.7 1.5 %shard_map.111 = bf16[16,8,1024]{2,1,0:T(8,128)(2,1)} custom-call(bf16[8,512]{1,0:T(8,128)(2,1)} %tokens_far.1, bf16[8,512]{1,0:T(8,128)(2,1)} %cotangent_far.1), custom_call_target="tpu_custom_call" | custom-call | tf_op jit(solution)/shard_map/pallas_call | solution.py:193
  2.2 18.3 %all_to_all.30 = bf16[16,8,1024]{2,1,0:T(8,128)(2,1)S(1)} all-to-all(bf16[16,8,1024]{2,1,0:T(8,128)(2,1)} %shard_map.111), channel_id=1, replica_groups=mesh['zlo'=2,'y'=8,'core'=2,'zhi'=4,'x'=4] {'zlo','y'}, dimensions={0} | all-to-all | bytes 524288 | tf_op jit(solution)/shard_map/all_to_all | solution.py:200
  20.5 0.0 copy-start
  20.5 4.3 %all_gather.9.both = bf16[256,1024]{1,0:T(8,128)(2,1)S(1)} all-gather(bf16[128,1024]{1,0:T(8,128)(2,1)S(1)} %bitcast.28), channel_id=1, replica_groups=mesh['zlo'=2,'y'=8,'core'=2,'zhi'=4,'x'=4] {'core'}, dimensions={0}, use_global_device_ids=true | all-gather | bytes 786432 | tf_op jit(solution)/shard_map/all_gather | solution.py:201
  24.8 0.0 copy-done.4
  24.8 0.2 fusion.3
  25.0 0.0 copy-done.1
  25.0 0.0 copy-start.2
  25.0 0.4 fusion.1
  25.5 0.0 copy-done
  25.5 0.5 fusion.2
  26.0 0.2 copy-done.2
  26.2 0.4 fusion
  26.7 0.5 pad_maximum_fusion
  27.1 22.3 %all_to_all.31 = f16[4,64,2816]{2,1,0:T(8,128)(2,1)S(1)} all-to-all(f16[4,64,2816]{2,1,0:T(8,128)(2,1)S(1)} %bitcast.25), channel_id=1, replica_groups=mesh['zlo'=2,'y'=8,'core'=2,'zhi'=4,'x'=4] {'x'}, dimensions={0} | all-to-all | bytes 2883584 | tf_op jit(solution)/shard_map/all_to_all | solution.py:60
  49.4 0.2 convert_reduce_fusion
  49.6 0.0 copy-start.3
  49.6 0.0 copy-start.5
  49.7 18.2 %all_to_all.32 = f16[4,16,2816]{2,1,0:T(8,128)(2,1)S(1)} all-to-all(f16[4,16,2816]{2,1,0:T(8,128)(2,1)S(1)} %bitcast.27), channel_id=1, replica_groups=mesh['zlo'=2,'y'=8,'core'=2,'zhi'=4,'x'=4] {'zhi'}, dimensions={0} | all-to-all | bytes 720896 | tf_op jit(solution)/shard_map/all_to_all | solution.py:60
  67.9 0.0 copy-done.3
  67.9 0.0 copy-done.5
  67.9 0.7 shard_map.112
  68.7 14.7 %all_to_all.33 = bf16[4,16,2816]{2,1,0:T(8,128)(2,1)S(1)} all-to-all(bf16[4,16,2816]{2,1,0:T(8,128)(2,1)S(1)} %shard_map.112), channel_id=1, replica_groups=mesh['zlo'=2,'y'=8,'core'=2,'zhi'=4,'x'=4] {'zhi'}, dimensions={0} | all-to-all | bytes 720896 | tf_op jit(solution)/shard_map/all_to_all | solution.py:223
  83.4 0.1 broadcast_in_dim.8
  83.5 17.3 %all_to_all.34 = bf16[4,64,2816]{2,1,0:T(8,128)(2,1)S(1)} all-to-all(bf16[4,64,2816]{2,1,0:T(8,128)(2,1)S(1)} %broadcast_in_dim.8), channel_id=1, replica_groups=mesh['zlo'=2,'y'=8,'core'=2,'zhi'=4,'x'=4] {'x'}, dimensions={0} | all-to-all | bytes 2883584 | tf_op jit(solution)/shard_map/all_to_all | solution.py:32
  100.8 1.7 %shard_map.113 = (f32[128,1152]{1,0:T(8,128)S(1)}, bf16[128,1152]{1,0:T(8,128)(2,1)S(1)}) custom-call(s32[2]{0:T(128)S(1)} %copy-done.5, bf16[256,2816]{1,0:T(8,128)(2,1)S(1)} %bitcast.18, bf16[512,896]{1,0:T(8,128)(2,1)S(1)} %copy-done.2, bf16[512,896]{1,0:T(8,128)(2,1)S(1)} %copy-done.1, bf16[896,512]{1,0:T(8,128)(2,1)S(1)} %copy-done, ...), custom_call_target="tpu_custom_call" | custom-call | tf_op jit(solution)/shard_map/pallas_call | solution.py:42
  102.4 7.3 %collective-permute-start = (bf16[128,1152]{1,0:T(8,128)(2,1)S(1)}, bf16[128,1152]{1,0:T(8,128)(2,1)S(1)}, u32[]{:S(2)}, u32[]{:S(2)}) collective-permute-start(bf16[128,1152]{1,0:T(8,128)(2,1)S(1)} %get-tuple-element.14), channel_id=1, source_target_pairs={{0,16},{16,0},{1,17},{17,1},{2,18},{18,2},{3,19},{19,3},{4,20},{20... | collective-permute-start | bytes 884744 | tf_op jit(solution)/shard_map/ppermute | solution.py:235
  109.8 1.0 convolution_multiply_fusion.3
  110.8 0.2 collective-permute-done.came
  111.0 0.1 shard_map.114
  111.0 18.3 %all_to_all.35.came = bf16[16,8,2048]{2,1,0:T(8,128)(2,1)S(1)} all-to-all(bf16[16,8,2048]{2,1,0:T(8,128)(2,1)S(1)} %shard_map.114), channel_id=1, replica_groups=mesh['zlo'=2,'y'=8,'core'=2,'zhi'=4,'x'=4] {'zlo','y'}, dimensions={0} | all-to-all | bytes 1048576 | tf_op jit(solution)/shard_map/all_to_all | solution.py:248
  129.3 0.1 shard_map.115
  129.4 4.3 %all-gather = bf16[128,128]{1,0:T(8,128)(2,1)S(1)} all-gather(bf16[64,128]{1,0:T(8,128)(2,1)S(1)} %get-tuple-element.17), channel_id=2, replica_groups=mesh['zlo'=2,'y'=8,'core'=2,'zhi'=4,'x'=4] {'core'}, dimensions={0}, use_global_device_ids=true | all-gather | bytes 49152 | tf_op jit(solution)/shard_map/all_gather | solution.py:258
  133.7 1.5 %shard_map.116 = (bf16[8,512]{1,0:T(8,128)(2,1)}, bf16[8,512]{1,0:T(8,128)(2,1)}, f32[128,512]{1,0:T(8,128)}) custom-call(s32[2]{0:T(128)S(1)} %copy-done.5, f32[8,1024]{1,0:T(8,128)S(1)} %get-tuple-element.16.sums, bf16[2,64,128]{2,1,0:T(8,128)(2,1)S(1)} %bitcast.24, bf16[256,1024]{1,0:T(8,128)(2,1)S(1)} %all_gather.9.both, bf16[128,512]{1,0:T(8,128)(2,1)S(1)} %bitcast.23), custom_call_target="tpu_custom_call" | custom-call | tf_op jit(solution)/shard_map/pallas_call | solution.py:42
  (2 shorter events, 0.1 us)
Async XLA Ops:
  0.6 24.1 %copy-start.4 = (bf16[2,512,64]{1,2,0:T(8,128)(2,1)S(1)}, bf16[2,512,64]{1,2,0:T(8,128)(2,1)}, u32[]{:S(2)}) copy-start(bf16[2,512,64]{1,2,0:T(8,128)(2,1)} %param.12) | copy-start | bytes 393220
  0.6 24.4 %copy-start.1 = (bf16[512,896]{1,0:T(8,128)(2,1)S(1)}, bf16[512,896]{1,0:T(8,128)(2,1)}, u32[]{:S(2)}) copy-start(bf16[512,896]{1,0:T(8,128)(2,1)} %up.1) | copy-start | bytes 2752516
  20.5 5.0 %copy-start = (bf16[896,512]{1,0:T(8,128)(2,1)S(1)}, bf16[896,512]{1,0:T(8,128)(2,1)}, u32[]{:S(2)}) copy-start(bf16[896,512]{1,0:T(8,128)(2,1)} %down.1) | copy-start | bytes 2752516
  25.0 1.2 copy-start.2
  49.6 18.3 %copy-start.3 = (bf16[2,64,896]{2,1,0:T(8,128)(2,1)S(1)}, bf16[2,64,896]{2,1,0:T(8,128)(2,1)}, u32[]{:S(2)}) copy-start(bf16[2,64,896]{2,1,0:T(8,128)(2,1)} %param.13) | copy-start | bytes 688132
  49.6 18.3 %copy-start.5 = (s32[2]{0:T(128)S(1)}, s32[2]{0:T(128)}, u32[]{:S(2)}) copy-start(s32[2]{0:T(128)} %adapter_of_block.5) | copy-start | bytes 28
  102.4 8.5 %collective-permute-start = (bf16[128,1152]{1,0:T(8,128)(2,1)S(1)}, bf16[128,1152]{1,0:T(8,128)(2,1)S(1)}, u32[]{:S(2)}, u32[]{:S(2)}) collective-permute-start(bf16[128,1152]{1,0:T(8,128)(2,1)S(1)} %get-tuple-element.14), channel_id=1, source_target_pairs={{0,16},{16,0},{1,17},{17,1},{2,18},{18,2},{3,19},{19,3},{4,20},{20... | collective-permute-start | bytes 884744 | tf_op jit(solution)/shard_map/ppermute | solution.py:235
